TPU v7x, 32 devices: a whole 2x2x4 slice. The times are simulated.
32 devices in a mesh: ctx: 8 (over y, x, core), fsdp: 4 (over z).
Axes of the slice: x: 2, y: 2, z: 4, core: 2. Of those that a mesh axis runs over, the one named last changes fastest.
Arguments:
- hidden_in: bfloat16 [4, 1024, 2048], P('fsdp', 'ctx'), may hold values from -6 to 6
- out_cotangent: bfloat16 [4, 1024, 2048], P('fsdp', 'ctx'), may hold values from -6 to 6
- seq_lengths: int32 [4], P('fsdp'), may hold values from 256 to 1024, as said below
- first_gain: bfloat16 [2048], P(('ctx', 'fsdp')), may hold values from 0.25 to 1.75
- first_shift: bfloat16 [2048], P(('ctx', 'fsdp')), may hold values from -1.75 to 1.75
- qkv_weight: bfloat16 [2048, 2304], P(('ctx', 'fsdp')), may hold values from -0.125 to 0.125
- query_bias: bfloat16 [2048], P(('ctx', 'fsdp')), may hold values from -3 to 3
- value_bias: bfloat16 [128], P(('ctx', 'fsdp')), may hold values from -0.1875 to 0.1875
- proj_weight: bfloat16 [2048, 2048], P(('ctx', 'fsdp')), may hold values from -2 to 2
- proj_bias: bfloat16 [2048], P(('ctx', 'fsdp')), may hold values from -3.5 to 3.5
- second_gain: bfloat16 [2048], P(('ctx', 'fsdp')), may hold values from 0.25 to 1.75
- second_shift: bfloat16 [2048], P(('ctx', 'fsdp')), may hold values from -1.75 to 1.75
- up_weight: bfloat16 [2048, 8192], P(('ctx', 'fsdp')), may hold values from -0.125 to 0.125
- up_bias: bfloat16 [8192], P(('ctx', 'fsdp')), may hold values from -3 to 3
- down_weight: bfloat16 [8192, 2048], P(('ctx', 'fsdp')), may hold values from -0.0625 to 0.0625
- down_bias: bfloat16 [2048], P(('ctx', 'fsdp')), may hold values from -3.5 to 3.5
Outputs:
- layer_out: bfloat16 [4, 1024, 2048], P('fsdp', 'ctx')
- input_grad: float32 [4, 1024, 2048], P('fsdp', 'ctx')
- first_gain_grad: float32 [2048], P(('ctx', 'fsdp'))
- first_shift_grad: float32 [2048], P(('ctx', 'fsdp'))
- qkv_weight_grad: float32 [2048, 2304], P(('ctx', 'fsdp'))
- query_bias_grad: float32 [2048], P(('ctx', 'fsdp'))
- value_bias_grad: float32 [128], P(('ctx', 'fsdp'))
- proj_weight_grad: float32 [2048, 2048], P(('ctx', 'fsdp'))
- proj_bias_grad: float32 [2048], P(('ctx', 'fsdp'))
- second_gain_grad: float32 [2048], P(('ctx', 'fsdp'))
- second_shift_grad: float32 [2048], P(('ctx', 'fsdp'))
- up_weight_grad: float32 [2048, 8192], P(('ctx', 'fsdp'))
- up_bias_grad: float32 [8192], P(('ctx', 'fsdp'))
- down_weight_grad: float32 [8192, 2048], P(('ctx', 'fsdp'))
- down_bias_grad: float32 [2048], P(('ctx', 'fsdp'))
Inputs may be any that keep to these rules, and one draw needn't show every extreme that they name: `seq_lengths`: live positions of a sequence come first; in every draw some sequence is full (1024).
All inputs are finite; a program needn't handle non-finite values.
Results may differ from a plain program's by a relative error of at most 0.025.
Values may be sent and summed in bfloat16 or wider, within the bound.
No kernel may reach another device: no remote copies, remote signals or barrier semaphores. Data moves between devices by JAX's collectives and lax.ppermute only.
A program may use at most 384 MiB of HBM per device.

v0:
```python
import math

import jax
import jax.numpy as jnp
from jax import lax
from jax.sharding import PartitionSpec as P

D = 2048
HEADS = 16
HD = 128


EPS = 1e-05
NEG = -1e30


def from_behind(value, axis, steps):
    count = lax.axis_size(axis)
    initial, last = (max(0, -steps), min(count, count - steps))
    return lax.ppermute(value, axis, [(source, source + steps) for source in range(initial, last)])


def shifted(shard, axis, by):
    devices = lax.axis_size(axis)
    return lax.ppermute(shard, axis, [(i, (i + by) % devices) for i in range(devices)])


def norm_forward(values, gain, shift):
    center = values - jnp.mean(values, -1, keepdims=True)
    inverse = lax.rsqrt(jnp.mean(center * center, -1, keepdims=True) + EPS)
    scaled = center * inverse
    return (scaled * gain + shift, scaled, inverse)


def norm_backward(upstream_gradient, scaled, inverse, gain):
    inner = upstream_gradient * gain
    return inverse * (
        inner
        - jnp.mean(inner, -1, keepdims=True)
        - scaled * jnp.mean(inner * scaled, -1, keepdims=True)
    )


def gelu_tanh_approx(values):
    return jax.nn.gelu(values, approximate=True)


def contract(left_operand, right_operand, left_dim, right_dim):
    return lax.dot_general(
        left_operand,
        right_operand,
        (((left_dim,), (right_dim,)), ((), ())),
        preferred_element_type=jnp.float32,
    )


def key_mask(context, key_start, count):
    key_pos = key_start + jnp.arange(count, dtype=jnp.int32)
    return (key_pos[None, :] <= context["row_pos"][:, None]) & (
        key_pos[None, :] < context["length"]
    )


def is_active(context, key_start):
    return (key_start <= context["last"]) & (key_start < context["length"])


def forward_piece(carry, pair, key_start, context):
    running_max, running_sum, running_acc = carry
    scores = contract(context["queries"], pair[:, :HD], 1, 1) * context["scale"]
    allowed = key_mask(context, key_start, pair.shape[0])
    scores = jnp.where(allowed, scores, NEG)
    new_max = jnp.maximum(running_max, jnp.max(scores, -1))
    factor = jnp.exp(running_max - new_max)
    expo = jnp.where(allowed, jnp.exp(scores - new_max[:, None]), 0.0)
    running_sum = running_sum * factor + jnp.sum(expo, -1)
    running_acc = running_acc * factor[:, None] + jnp.dot(
        expo.astype(jnp.bfloat16), pair[:, HD:], preferred_element_type=jnp.float32
    )
    return (new_max, running_sum, running_acc)


def forward_guarded(carry, pair, key_start, context):
    return lax.cond(
        is_active(context, key_start),
        lambda state: forward_piece(state, pair, key_start, context),
        lambda state: state,
        carry,
    )


def forward_keys(carry, pair, key_start, context):
    count = pair.shape[0]
    blocked = context["block"]
    return forward_guarded(carry, pair, key_start, context)


def backward_piece(grad_acc, pair, key_start, context):
    scores = contract(context["queries"], pair[:, :HD], 1, 1) * context["scale"]
    allowed = key_mask(context, key_start, pair.shape[0])
    probs = jnp.where(
        allowed, jnp.exp(jnp.where(allowed, scores, NEG) - context["lse"][:, None]), 0.0
    )
    grad_values = contract(probs.astype(jnp.bfloat16), context["grads"], 0, 0)
    grad_probs = contract(context["grads"], pair[:, HD:], 1, 1)
    grad_scores = (probs * (grad_probs - context["delta"][:, None])).astype(jnp.bfloat16)
    grad_acc = (
        grad_acc
        + jnp.dot(grad_scores, pair[:, :HD], preferred_element_type=jnp.float32) * context["scale"]
    )
    grad_keys = contract(grad_scores, context["queries"], 0, 0) * context["scale"]
    return (grad_acc, jnp.concatenate([grad_keys, grad_values], axis=1))


def backward_guarded(grad_acc, pair, key_start, context):
    empty = jnp.zeros((pair.shape[0], 2 * HD), jnp.float32)
    return lax.cond(
        is_active(context, key_start),
        lambda state: backward_piece(state, pair, key_start, context),
        lambda state: (state, empty),
        grad_acc,
    )


def body(
    hidden_in,
    out_cotangent,
    seq_lengths,
    first_gain,
    first_shift,
    qkv_weight,
    query_bias,
    value_bias,
    proj_weight,
    proj_bias,
    second_gain,
    second_shift,
    up_weight,
    up_bias,
    down_weight,
    down_bias,
):
    cycle_size = lax.axis_size("ctx")
    cycle_pos = lax.axis_index("ctx")
    span = hidden_in.shape[1]
    rows_in = hidden_in[0].astype(jnp.float32)
    live_length = seq_lengths[0]
    positions = cycle_pos * span + jnp.arange(span, dtype=jnp.int32)
    live = (positions < live_length)[:, None]
    gain_one, shift_one, qkv_full, qbias_full, vbias_full, proj_full, pbias_full = (
        lax.all_gather(first_gain, ("ctx", "fsdp"), axis=0, tiled=True),
        lax.all_gather(first_shift, ("ctx", "fsdp"), axis=0, tiled=True),
        lax.all_gather(qkv_weight, ("ctx", "fsdp"), axis=0, tiled=True),
        lax.all_gather(query_bias, ("ctx", "fsdp"), axis=0, tiled=True),
        lax.all_gather(value_bias, ("ctx", "fsdp"), axis=0, tiled=True),
        lax.all_gather(proj_weight, ("ctx", "fsdp"), axis=0, tiled=True),
        lax.all_gather(proj_bias, ("ctx", "fsdp"), axis=0, tiled=True),
    )
    normed_one, scaled_one, inverse_one = norm_forward(
        rows_in, gain_one.astype(jnp.float32), shift_one.astype(jnp.float32)
    )
    normed_one = normed_one.astype(jnp.bfloat16)
    mixed = jnp.dot(normed_one, qkv_full, preferred_element_type=jnp.float32)
    queries = (mixed[:, :D] + qbias_full.astype(jnp.float32)).astype(jnp.bfloat16)
    pair_own = jnp.concatenate(
        [mixed[:, D : D + HD], mixed[:, D + HD :] + vbias_full.astype(jnp.float32)], axis=1
    ).astype(jnp.bfloat16)
    rows_count = span * HEADS
    context = {
        "queries": queries.reshape(rows_count, HD),
        "row_pos": jnp.repeat(positions, HEADS),
        "length": live_length,
        "last": cycle_pos * span + span - 1,
        "scale": 1.0 / math.sqrt(HD),
        "block": span,
    }
    initial = (
        jnp.full((rows_count,), NEG, jnp.float32),
        jnp.zeros((rows_count,), jnp.float32),
        jnp.zeros((rows_count, HD), jnp.float32),
    )
    carry = forward_keys(initial, pair_own, cycle_pos * span, context)

    def forward_rotation(step, state):
        carry_now, pair = state
        pair = from_behind(pair, "ctx", 1)
        source = (cycle_pos - step) % cycle_size
        return (forward_keys(carry_now, pair, source * span, context), pair)

    carry, _ = lax.fori_loop(1, cycle_size, forward_rotation, (carry, pair_own))
    final_max, final_sum, final_acc = carry
    attended_rows = final_acc / final_sum[:, None]
    log_total = final_max + jnp.log(final_sum)
    attended = attended_rows.astype(jnp.bfloat16).reshape(span, D)
    middle = (
        rows_in
        + jnp.dot(attended, proj_full, preferred_element_type=jnp.float32)
        + pbias_full.astype(jnp.float32)
    )
    gain_two, shift_two, up_full, ubias_full, down_full, dbias_full = (
        lax.all_gather(second_gain, ("ctx", "fsdp"), axis=0, tiled=True),
        lax.all_gather(second_shift, ("ctx", "fsdp"), axis=0, tiled=True),
        lax.all_gather(up_weight, ("ctx", "fsdp"), axis=0, tiled=True),
        lax.all_gather(up_bias, ("ctx", "fsdp"), axis=0, tiled=True),
        lax.all_gather(down_weight, ("ctx", "fsdp"), axis=0, tiled=True),
        lax.all_gather(down_bias, ("ctx", "fsdp"), axis=0, tiled=True),
    )
    normed_two, scaled_two, inverse_two = norm_forward(
        middle, gain_two.astype(jnp.float32), shift_two.astype(jnp.float32)
    )
    normed_two = normed_two.astype(jnp.bfloat16)
    before = jnp.dot(normed_two, up_full, preferred_element_type=jnp.float32) + ubias_full.astype(
        jnp.float32
    )
    active = gelu_tanh_approx(before).astype(jnp.bfloat16)
    result = (
        middle
        + jnp.dot(active, down_full, preferred_element_type=jnp.float32)
        + dbias_full.astype(jnp.float32)
    )
    layer_out = jnp.where(live, result, 0.0).astype(jnp.bfloat16)
    upstream_gradient = jnp.where(live, out_cotangent[0].astype(jnp.float32), 0.0)
    gain_two_back, up_back, down_back, gain_one_back, qkv_back, proj_back = (
        lax.all_gather(second_gain, ("ctx", "fsdp"), axis=0, tiled=True),
        lax.all_gather(up_weight, ("ctx", "fsdp"), axis=0, tiled=True),
        lax.all_gather(down_weight, ("ctx", "fsdp"), axis=0, tiled=True),
        lax.all_gather(first_gain, ("ctx", "fsdp"), axis=0, tiled=True),
        lax.all_gather(qkv_weight, ("ctx", "fsdp"), axis=0, tiled=True),
        lax.all_gather(proj_weight, ("ctx", "fsdp"), axis=0, tiled=True),
    )
    grad_mlp = upstream_gradient.astype(jnp.bfloat16)
    down_bias_term = jnp.sum(grad_mlp.astype(jnp.float32), 0)
    down_weight_term = contract(active, grad_mlp, 0, 0)
    grad_active = contract(grad_mlp, down_back, 1, 1)
    _, gelu_pull = jax.vjp(gelu_tanh_approx, before)
    grad_before = gelu_pull(grad_active)[0].astype(jnp.bfloat16)
    up_bias_term = jnp.sum(grad_before.astype(jnp.float32), 0)
    up_weight_term = contract(normed_two, grad_before, 0, 0)
    grad_two = contract(grad_before, up_back, 1, 1)
    gain_two_term = jnp.sum(grad_two * scaled_two, 0)
    shift_two_term = jnp.sum(grad_two, 0)
    grad_middle = upstream_gradient + norm_backward(
        grad_two, scaled_two, inverse_two, gain_two_back.astype(jnp.float32)
    )
    mlp_sums = (
        lax.psum_scatter(gain_two_term, ("ctx", "fsdp"), scatter_dimension=0, tiled=True),
        lax.psum_scatter(shift_two_term, ("ctx", "fsdp"), scatter_dimension=0, tiled=True),
        lax.psum_scatter(up_weight_term, ("ctx", "fsdp"), scatter_dimension=0, tiled=True),
        lax.psum_scatter(up_bias_term, ("ctx", "fsdp"), scatter_dimension=0, tiled=True),
        lax.psum_scatter(down_weight_term, ("ctx", "fsdp"), scatter_dimension=0, tiled=True),
        lax.psum_scatter(down_bias_term, ("ctx", "fsdp"), scatter_dimension=0, tiled=True),
    )
    grad_branch = grad_middle.astype(jnp.bfloat16)
    proj_bias_term = jnp.sum(grad_branch.astype(jnp.float32), 0)
    proj_weight_term = contract(attended, grad_branch, 0, 0)
    grad_attended = (
        contract(grad_branch, proj_back, 1, 1).astype(jnp.bfloat16).reshape(rows_count, HD)
    )
    delta = jnp.sum(grad_attended.astype(jnp.float32) * attended_rows, -1)
    context_back = dict(context, lse=log_total, grads=grad_attended, delta=delta)
    grad_start = jnp.zeros((rows_count, HD), jnp.float32)
    travel_start = jnp.zeros((span, 2 * HD), jnp.float32)

    def backward_turn(step, state):
        grad_acc, pair, travel_offset = state
        source = (cycle_pos - step) % cycle_size
        grad_acc, term = backward_guarded(grad_acc, pair, source * span, context_back)
        pair = from_behind(pair, "ctx", 1)
        travel_offset = shifted(travel_offset + term, "ctx", 1)
        return (grad_acc, pair, travel_offset)

    grad_queries_acc, _, pair_grads = lax.fori_loop(
        0, cycle_size, backward_turn, (grad_start, pair_own, travel_start)
    )
    grad_queries = grad_queries_acc.astype(jnp.bfloat16).reshape(span, D)
    grad_pair = pair_grads.astype(jnp.bfloat16)
    grad_mixed = jnp.concatenate([grad_queries, grad_pair], axis=1)
    query_bias_contribution = jnp.sum(grad_queries.astype(jnp.float32), 0)
    value_bias_term = jnp.sum(grad_pair[:, HD:].astype(jnp.float32), 0)
    qkv_weight_term = contract(normed_one, grad_mixed, 0, 0)
    grad_one = contract(grad_mixed, qkv_back, 1, 1)
    gain_one_term = jnp.sum(grad_one * scaled_one, 0)
    shift_one_term = jnp.sum(grad_one, 0)
    input_grad = grad_middle + norm_backward(
        grad_one, scaled_one, inverse_one, gain_one_back.astype(jnp.float32)
    )
    attn_sums = (
        lax.psum_scatter(gain_one_term, ("ctx", "fsdp"), scatter_dimension=0, tiled=True),
        lax.psum_scatter(shift_one_term, ("ctx", "fsdp"), scatter_dimension=0, tiled=True),
        lax.psum_scatter(qkv_weight_term, ("ctx", "fsdp"), scatter_dimension=0, tiled=True),
        lax.psum_scatter(query_bias_contribution, ("ctx", "fsdp"), scatter_dimension=0, tiled=True),
        lax.psum_scatter(value_bias_term, ("ctx", "fsdp"), scatter_dimension=0, tiled=True),
        lax.psum_scatter(proj_weight_term, ("ctx", "fsdp"), scatter_dimension=0, tiled=True),
        lax.psum_scatter(proj_bias_term, ("ctx", "fsdp"), scatter_dimension=0, tiled=True),
    )
    return (
        layer_out[None],
        input_grad[None],
        attn_sums[0],
        attn_sums[1],
        attn_sums[2],
        attn_sums[3],
        attn_sums[4],
        attn_sums[5],
        attn_sums[6],
        mlp_sums[0],
        mlp_sums[1],
        mlp_sums[2],
        mlp_sums[3],
        mlp_sums[4],
        mlp_sums[5],
    )


def solution(mesh):
    placed = (
        P("fsdp", "ctx", None),
        P("fsdp", "ctx", None),
        P("fsdp"),
        P(("ctx", "fsdp")),
        P(("ctx", "fsdp")),
        P(("ctx", "fsdp"), None),
        P(("ctx", "fsdp")),
        P(("ctx", "fsdp")),
        P(("ctx", "fsdp"), None),
        P(("ctx", "fsdp")),
        P(("ctx", "fsdp")),
        P(("ctx", "fsdp")),
        P(("ctx", "fsdp"), None),
        P(("ctx", "fsdp")),
        P(("ctx", "fsdp"), None),
        P(("ctx", "fsdp")),
    )
    return jax.shard_map(
        body,
        mesh=mesh,
        in_specs=placed,
        out_specs=(
            P("fsdp", "ctx", None),
            P("fsdp", "ctx", None),
            P(("ctx", "fsdp")),
            P(("ctx", "fsdp")),
            P(("ctx", "fsdp"), None),
            P(("ctx", "fsdp")),
            P(("ctx", "fsdp")),
            P(("ctx", "fsdp"), None),
            P(("ctx", "fsdp")),
            P(("ctx", "fsdp")),
            P(("ctx", "fsdp")),
            P(("ctx", "fsdp"), None),
            P(("ctx", "fsdp")),
            P(("ctx", "fsdp"), None),
            P(("ctx", "fsdp")),
        ),
        check_vma=False,
    )
```

profile of v0, /device:TPU:0, one launch (start us, length us, event | category | flops | bytes accessed | tf_op | source)
XLA Modules:
  0.0 4265.8 jit_solution(8968699399750971658)
XLA Ops:
  16.8 43.2 %all-reduce.18 = (bf16[2048]{0:T(1024)(128)(2,1)S(1)}, bf16[2048]{0:T(1024)(128)(2,1)S(1)}, bf16[128]{0:T(256)(128)(2,1)S(1)}, bf16[2048]{0:T(1024)(128)(2,1)S(1...) all-reduce(bf16[2048]{0:T(1024)(128)(2,1)S(1)} %dynamic-update-slic, ...), channel_id=1, replica_groups=mesh['ctx'=8,'fsdp'=4] {'ctx','fsdp'}, use_global_device_ids=true, to_apply=%add.1 | all-reduce | flops 14464 | bytes 57856
  61.4 66.5 %all-gather = bf16[32,1,256]{2,1,0:T(2,128)(2,1)S(1)} all-gather(bf16[1,1,256]{2,1,0:T(2,128)(2,1)S(1)} %reshape.159), channel_id=1, replica_groups=mesh['ctx'=8,'fsdp'=4] {'ctx','fsdp'}, dimensions={0}, use_global_device_ids=true | all-gather | bytes 16896 | tf_op jit(solution)/shard_map/all_gather | solution.py:204
  131.0 5.2 fusion.88
  136.7 5.8 conditional.3
  141.0 1.4 convolution_add_fusion
  142.5 54.1 %while.45 = (s32[]{:T(128)}, f32[2048]{0:T(1024)}, f32[2048]{0:T(1024)S(1)}, f32[2048,128]{1,0:T(8,128)S(1)}, bf16[128,256]{1,0:T(8,128)(2,1)S(1)}, /*index=5*/s...) while((s32[]{:T(128)}, f32[2048]{0:T(1024)}, ...), condition=%wide.region_11.12_spmd.clone, body=%wide.region_6.11_spmd.clone.sunk | while | flops 138678672 | bytes 6410456 | solution.py:190
  144.7 7.4 collective-permute-start
  153.0 3.6 collective-permute-start
  157.5 11.1 collective-permute-start
  169.5 6.7 collective-permute-start
  177.1 10.8 collective-permute-start
  188.8 6.8 collective-permute-start
  197.4 5.0 fusion.94
  204.0 168.0 %all-gather.10.cloned.1.call-done = bf16[2048,8192]{1,0:T(8,128)(2,1)} async-done(((bf16[64,8192]{1,0:T(8,128)(2,1)}), bf16[2048,8192]{1,0:T(8,128)(2,1)}) %all-gather.10.cloned.1.call-update) | async-done | bytes 33554448 | tf_op jit(solution)/shard_map/all_gather | solution.py:203
  372.0 18.1 convolution_add_fusion.2
  390.1 177.7 %all-gather.12.cloned.1.call-done = bf16[8192,2048]{1,0:T(8,128)(2,1)} async-done(((bf16[256,2048]{1,0:T(8,128)(2,1)}), bf16[8192,2048]{1,0:T(8,128)(2,1)}) %all-gather.12.cloned.1.call-update) | async-done | bytes 33554448 | tf_op jit(solution)/shard_map/all_gather | solution.py:205
  567.8 19.6 convert_reduce_fusion
  587.4 19.9 multiply_reduce_fusion
  607.3 2.4 convert_reduce_fusion.3
  610.7 7.1 convolution_convert_fusion
  620.4 96.0 %while.46 = (s32[]{:T(128)}, f32[2048,128]{1,0:T(8,128)S(1)}, bf16[128,256]{1,0:T(8,128)(2,1)S(1)}, f32[128,256]{0,1:T(8,128)S(1)}, s32[]{:T(128)}, /*index=5*/s...) while((s32[]{:T(128)}, f32[2048,128]{1,0:T(8,128)S(1)}, ...), condition=%wide.region_20.21_spmd.clone, body=%wide.region_17.20_spmd.clone.sunk | while | flops 338772384 | bytes 12864140 | solution.py:272
  621.1 5.5 conditional.9
  622.6 1.8 fusion.34
  627.5 3.2 collective-permute-start.1
  634.1 5.0 collective-permute-start.2
  639.1 4.3 collective-permute-start.1
  646.1 9.7 collective-permute-start.1
  658.6 4.7 collective-permute-start.1
  664.2 2.0 collective-permute-done.2
  667.6 4.3 collective-permute-start.2
  672.0 4.7 collective-permute-start.1
  680.1 9.9 collective-permute-start.1
  693.1 4.7 collective-permute-start.1
  698.8 4.8 collective-permute-done.2
  704.9 2.9 collective-permute-start.1
  708.7 7.7 collective-permute-done.2
  718.1 8.5 fusion.67
  726.8 8.4 fusion.72
  736.6 8.1 fusion.78
  745.4 24.9 fusion.90
  771.3 25.7 fusion.81
  797.7 2.6 fusion.66
  800.3 17.8 fusion.52
  818.1 33.7 all-reduce.21.cloned.1.call-done
  863.1 204.5 %reduce-scatter.5.cloned.1.call-done = f32[64,2304]{1,0:T(8,128)} async-done(((f32[2048,2304]{1,0:T(8,128)}), f32[64,2304]{1,0:T(8,128)}) %reduce-scatter.5.cloned.1.call-update) | async-done | bytes 589840 | tf_op jit(solution)/shard_map/reduce_scatter | solution.py:290
  1067.6 366.2 %reduce-scatter.7.cloned.1.call-done = f32[64,2048]{1,0:T(8,128)} async-done(((f32[2048,2048]{1,0:T(8,128)}), f32[64,2048]{1,0:T(8,128)}) %reduce-scatter.7.cloned.1.call-update) | async-done | bytes 524304 | tf_op jit(solution)/shard_map/reduce_scatter | solution.py:293
  1433.7 1411.6 %reduce-scatter.9.cloned.1.call-done = f32[64,8192]{1,0:T(8,128)} async-done(((f32[2048,8192]{1,0:T(8,128)}), f32[64,8192]{1,0:T(8,128)}) %reduce-scatter.9.cloned.1.call-update) | async-done | bytes 2097168 | tf_op jit(solution)/shard_map/reduce_scatter | solution.py:248
  2845.4 1413.7 %reduce-scatter.11.cloned.1.call-done = f32[256,2048]{1,0:T(8,128)} async-done(((f32[8192,2048]{1,0:T(8,128)}), f32[256,2048]{1,0:T(8,128)}) %reduce-scatter.11.cloned.1.call-update) | async-done | bytes 2097168 | tf_op jit(solution)/shard_map/reduce_scatter | solution.py:250
  (222 shorter events, 64.3 us)
Async XLA Ops:
  7.2 123.9 %copy-start = (bf16[1,128,2048]{2,1,0:T(8,128)(2,1)S(1)}, bf16[1,128,2048]{2,1,0:T(8,128)(2,1)}, u32[]{:S(2)}) copy-start(bf16[1,128,2048]{2,1,0:T(8,128)(2,1)} %param.26) | copy-start | bytes 1572868
  7.2 123.8 %all-gather.6.cloned.1.call-start = ((), (), s32[]{:S(2)}) async-start(), calls=%async_computation.4 | async-start | bytes 9732096 | tf_op jit(solution)/shard_map/all_gather | solution.py:153
  7.9 189.4 %all-gather.8.cloned.1.call-start = ((), (), s32[]{:S(2)}) async-start(), calls=%async_computation.5 | async-start | bytes 8650752 | tf_op jit(solution)/shard_map/all_gather | solution.py:156
  8.7 363.3 %all-gather.10.cloned.1.call-start = ((), (), s32[]{:S(2)}) async-start(), calls=%async_computation.6 | async-start | bytes 34603008 | tf_op jit(solution)/shard_map/all_gather | solution.py:203
  9.4 558.4 %all-gather.12.cloned.1.call-start = ((), (), s32[]{:S(2)}) async-start(), calls=%async_computation.7 | async-start | bytes 34603008 | tf_op jit(solution)/shard_map/all_gather | solution.py:205
  10.0 841.8 %all-reduce.21.cloned.1.call-start = ((), (), s32[]{:S(2)}) async-start(), calls=%async_computation.12 | async-start | bytes 181248
  60.7 75.6 %copy-start.11 = (f32[2048]{0:T(1024)}, f32[2048]{0:T(1024)S(1)}, u32[]{:S(2)}) copy-start(f32[2048]{0:T(1024)S(1)} %convert_element_type.135) | copy-start | bytes 24580
  60.7 75.5 %copy-start.9 = (f32[2048]{0:T(1024)}, f32[2048]{0:T(1024)S(1)}, u32[]{:S(2)}) copy-start(f32[2048]{0:T(1024)S(1)} %convert_element_type.134) | copy-start | bytes 24580
  128.4 478.8 %copy-start.22 = (pred[128]{0:T(512)(128)(4,1)}, pred[128]{0:T(512)(128)(4,1)S(1)}, u32[]{:S(2)}) copy-start(pred[128]{0:T(512)(128)(4,1)S(1)} %broadcast_compare_fusion.3) | copy-start | bytes 388
  129.7 6.6 copy-start.17
  131.0 5.3 copy-start.19
  142.5 2.2 collective-permute-start
  144.7 8.3 collective-permute-start
  153.0 4.5 collective-permute-start
  157.5 12.0 collective-permute-start
  169.5 7.6 collective-permute-start
  177.1 11.7 collective-permute-start
  188.8 7.7 collective-permute-start
  197.4 5.0 copy-start.5
  202.4 404.9 %copy-start.13 = (f32[128]{0:T(128)}, f32[128]{0:T(128)S(1)}, u32[]{:S(2)}) copy-start(f32[128]{0:T(128)S(1)} %broadcast_multiply_fusion.4) | copy-start | bytes 1540
  202.7 404.6 %copy-start.15 = (f32[128]{0:T(128)}, f32[128]{0:T(128)S(1)}, u32[]{:S(2)}) copy-start(f32[128]{0:T(128)S(1)} %add_rsqrt_fusion) | copy-start | bytes 1540
  372.0 195.8 %copy-start.7 = (bf16[1,128,2048]{2,1,0:T(8,128)(2,1)S(1)}, bf16[1,128,2048]{2,1,0:T(8,128)(2,1)}, u32[]{:S(2)}) copy-start(bf16[1,128,2048]{2,1,0:T(8,128)(2,1)} %param.27) | copy-start | bytes 1572868
  622.6 3.6 copy-start.2
  627.2 5.5 collective-permute-start.2
  627.5 4.1 collective-permute-start.1
  634.1 10.1 collective-permute-start.2
  639.1 5.2 collective-permute-start.1
  645.6 11.0 collective-permute-start.2
  646.1 10.6 collective-permute-start.1
  658.1 8.2 collective-permute-start.2
  658.6 5.6 collective-permute-start.1
  667.6 11.0 collective-permute-start.2
  672.0 5.6 collective-permute-start.1
  680.1 11.0 collective-permute-start.2
  680.1 10.8 collective-permute-start.1
  692.5 11.0 collective-permute-start.2
  693.1 5.6 collective-permute-start.1
  704.9 11.5 collective-permute-start.2
  704.9 3.8 collective-permute-start.1
  718.1 8.6 copy-start.10
  718.1 8.6 copy-start.12
  718.1 8.6 copy-start.18
  718.1 8.6 copy-start.20
  726.7 340.9 %reduce-scatter.5.cloned.1.call-start = ((), (), s32[]{:S(2)}) async-start(), calls=%async_computation.8 | async-start | bytes 19464192 | tf_op jit(solution)/shard_map/reduce_scatter | solution.py:290
  735.2 1.4 copy-start.6
  735.2 698.5 %reduce-scatter.7.cloned.1.call-start = ((), (), s32[]{:S(2)}) async-start(), calls=%async_computation.9 | async-start | bytes 17301504 | tf_op jit(solution)/shard_map/reduce_scatter | solution.py:293
  744.7 2100.7 %reduce-scatter.9.cloned.1.call-start = ((), (), s32[]{:S(2)}) async-start(), calls=%async_computation.10 | async-start | bytes 69206016 | tf_op jit(solution)/shard_map/reduce_scatter | solution.py:248
  770.3 3488.8 %reduce-scatter.11.cloned.1.call-start = ((), (), s32[]{:S(2)}) async-start(), calls=%async_computation.11 | async-start | bytes 69206016 | tf_op jit(solution)/shard_map/reduce_scatter | solution.py:250
  (8 other events, 7.1 us)
Sparse Core Ops, SparseCore 0:
  10.8 84.6 all-gather.5
  98.5 77.0 all-gather.7
  178.4 193.5 all-gather.9
  374.8 192.9 all-gather.11
  726.8 124.9 all-reduce.20
  859.7 207.8 reduce-scatter.4
  1070.5 363.1 reduce-scatter.6
  1436.8 1408.5 reduce-scatter.8
  2848.4 1410.5 reduce-scatter.10
where the time goes:
time: 4270 us
  waiting for transfers between devices  3800 us (89%)
  matrix products  174 us (4%)
  blocking collectives  110 us (3%)
  starting transfers between devices  103 us (2%)
    reduce_scatter x1, waiting for transfers between devices, body(): lax.psum_scatter(down_weight_term, ('ctx', 'fsdp'), scatter_dimension=0,...  1410 us
    reduce_scatter x1, waiting for transfers between devices, body(): lax.psum_scatter(up_weight_term, ('ctx', 'fsdp'), scatter_dimension=0, ti...  1410 us
    reduce_scatter x1, waiting for transfers between devices, body(): lax.psum_scatter(proj_weight_term, ('ctx', 'fsdp'), scatter_dimension=0,...  366 us
    reduce_scatter x1, waiting for transfers between devices, body(): lax.psum_scatter(qkv_weight_term, ('ctx', 'fsdp'), scatter_dimension=0, t...  204 us
    all_gather x1, waiting for transfers between devices, body(): lax.all_gather(down_weight, ('ctx', 'fsdp'), axis=0, tiled=True)  178 us
    all_gather x1, waiting for transfers between devices, body(): lax.all_gather(up_weight, ('ctx', 'fsdp'), axis=0, tiled=True)  168 us
    dot_general x13, matrix products, contract(): lax.dot_general(left_operand, right_operand, (((left_dim,), (right_dim,))...  126 us
    ppermute x15, starting transfers between devices, from_behind(): lax.ppermute(value, axis, [(source, source + steps) for source in range(i...  91.9 us
  transfers between devices with their start and end apart: 32, of which 28 were waited for; matrix products, arithmetic and copies ran while one was open for 3% of the time, Pallas kernels for 0%

commit v1 on v0

v1 whole, which is shorter than its diff:
```python
import math

import jax
import jax.numpy as jnp
from jax import lax
from jax.sharding import PartitionSpec as P

HEADS = 16
HD = 128
EPS = 1e-05
NEG = -1e30
BOTH = ("ctx", "fsdp")
BF = jnp.bfloat16
F32 = jnp.float32


def dot(a, b, da, db):
    return lax.dot_general(
        a, b, (((da,), (db,)), ((), ())), preferred_element_type=F32
    )


def normalize(values):
    center = values - jnp.mean(values, -1, keepdims=True)
    inverse = lax.rsqrt(jnp.mean(center * center, -1, keepdims=True) + EPS)
    return center * inverse, inverse


def norm_backward(grad, scaled, inverse, gain):
    inner = grad * gain
    return inverse * (
        inner
        - jnp.mean(inner, -1, keepdims=True)
        - scaled * jnp.mean(inner * scaled, -1, keepdims=True)
    )


def gelu(values):
    return jax.nn.gelu(values, approximate=True)


def after(value, *first):
    return lax.optimization_barrier((value,) + first)[0]


def exchange(value, mask):
    count = lax.axis_size("ctx")
    return lax.ppermute(value, "ctx", [(i, i ^ mask) for i in range(count)])


def chip_groups():
    count = lax.axis_size("ctx")
    return [list(range(core, count, 2)) for core in range(2)]


def chip_devices():
    width = 2 * lax.axis_size("fsdp")
    total = lax.axis_size("ctx") * lax.axis_size("fsdp")
    return [list(range(at, at + width)) for at in range(0, total, width)]


def plane_pieces(value):
    chips = lax.axis_size("ctx") // 2
    return [value] + [exchange(value, 2 * k) for k in range(1, chips)]


def both_cores(pieces):
    return jnp.concatenate(pieces + [exchange(piece, 1) for piece in pieces], 0)


def plane_scatter(left, weight, dim):
    chips = lax.axis_size("ctx") // 2
    rows = left.shape[0] // (2 * chips)
    half = rows * chips
    other = exchange(dot(left[half:], weight, 1, dim).astype(BF), 1)

    def block(k):
        return dot(left[k * rows : (k + 1) * rows], weight, 1, dim) + other[
            k * rows : (k + 1) * rows
        ].astype(F32)

    arrived = [exchange(block(k).astype(BF), 2 * k) for k in range(1, chips)]
    total = block(0)
    for piece in arrived:
        total = total + piece.astype(F32)
    return total


def column_chain(value):
    depth = lax.axis_size("fsdp")
    at = lax.axis_index("fsdp")
    upward, downward = [value], [value]
    for s in range(1, depth):
        upward.append(
            lax.ppermute(upward[-1], "fsdp", [(i, i + 1) for i in range(s - 1, depth - 1)])
        )
        downward.append(
            lax.ppermute(downward[-1], "fsdp", [(i, i - 1) for i in range(1, depth - s + 1)])
        )
    return [value] + [
        jnp.where(at >= s, upward[s], downward[depth - s]) for s in range(1, depth)
    ]


def turned(value, by):
    depth = lax.axis_size("fsdp")
    return lax.ppermute(value, "fsdp", [(i, (i + by) % depth) for i in range(depth)])


def column_direct(value):
    depth = lax.axis_size("fsdp")
    return [value] + [turned(value, s) for s in range(1, depth)]


def column_scatter(left, weight, dim, chain):
    depth = lax.axis_size("fsdp")
    rows = left.shape[0] // (2 * depth)
    half = rows * depth
    other = exchange(dot(left[half:], weight, 1, dim).astype(BF), 1)

    def block(s):
        return dot(left[s * rows : (s + 1) * rows], weight, 1, dim) + other[
            s * rows : (s + 1) * rows
        ].astype(F32)

    if not chain:
        total = block(0)
        for s in range(1, depth):
            total = total + turned(block(s).astype(BF), -s).astype(F32)
        return total
    upward = downward = None
    for s in range(1, depth):
        rising, falling = block(s), block(depth - s)
        if upward is not None:
            rising = rising + upward.astype(F32)
            falling = falling + downward.astype(F32)
        upward = lax.ppermute(
            rising.astype(BF), "fsdp", [(i, i + 1) for i in range(min(s, depth - 1))]
        )
        downward = lax.ppermute(
            falling.astype(BF), "fsdp", [(i, i - 1) for i in range(max(depth - s, 1), depth)]
        )
    return block(0) + upward.astype(F32) + downward.astype(F32)


def pad_rows(flat, width):
    rows = -(-flat.shape[0] // width)
    rows = -(-rows // 8) * 8
    return jnp.pad(flat, (0, rows * width - flat.shape[0])).reshape(rows, width)


def body(
    hidden_in,
    out_cotangent,
    seq_lengths,
    first_gain,
    first_shift,
    qkv_weight,
    query_bias,
    value_bias,
    proj_weight,
    proj_bias,
    second_gain,
    second_shift,
    up_weight,
    up_bias,
    down_weight,
    down_bias,
):
    count, depth = lax.axis_size("ctx"), lax.axis_size("fsdp")
    chips = count // 2
    at, level = lax.axis_index("ctx"), lax.axis_index("fsdp")
    core = at % 2
    span, width = hidden_in.shape[1:]
    wrows = qkv_weight.shape[0]
    hidden = up_weight.shape[1]
    frows = down_weight.shape[0]
    share = HEADS // count
    qcols = share * HD
    wide_cols = qcols + HD
    scale = 1.0 / math.sqrt(HD)
    length = seq_lengths[0]
    own_rows = hidden_in[0].astype(F32)
    positions = at * span + jnp.arange(span, dtype=jnp.int32)
    live = (positions < length)[:, None]
    upstream = jnp.where(live, out_cotangent[0].astype(F32), 0.0)
    grad_mlp_own = upstream.astype(BF)

    small = [
        first_gain,
        first_shift,
        query_bias,
        value_bias,
        proj_bias,
        second_gain,
        second_shift,
        up_bias,
        down_bias,
    ]
    packed = pad_rows(jnp.concatenate(small), wide_cols)
    qpart = qkv_weight[:, :width].reshape(wrows, count, qcols).transpose(1, 0, 2)
    kvpart = qkv_weight[:, width:].reshape(wrows, 2, HD).transpose(1, 0, 2)
    kvpart = jnp.broadcast_to(kvpart[None], (chips, 2, wrows, HD)).reshape(count, wrows, HD)
    outgoing = jnp.concatenate(
        [
            jnp.concatenate([qpart, kvpart], 2),
            jnp.broadcast_to(packed[None], (count,) + packed.shape),
        ],
        1,
    )
    incoming = lax.all_to_all(outgoing, "ctx", 0, 0, tiled=True)
    attn_all = lax.all_gather(incoming, "fsdp", axis=0)
    hidden_own, proj_own = lax.optimization_barrier((hidden_in[0], proj_weight, incoming))[:2]
    row_pieces = plane_pieces(hidden_own)
    rows = both_cores(row_pieces).astype(F32)
    proj_local = lax.all_gather(proj_own, "fsdp", axis=0, tiled=True)
    down_own = after(down_weight, *row_pieces)
    down_pieces = plane_pieces(down_own)
    scaled_all, _ = normalize(rows)
    scaled_all, attn_all = lax.optimization_barrier((scaled_all, attn_all))
    attn_rows = attn_all.transpose(1, 0, 2, 3)
    qkv_local = attn_rows[:, :, :wrows].reshape(width, wide_cols)
    table = attn_rows[:, :, wrows:].reshape(count * depth, -1)
    vectors, offset = [], 0
    for piece in small:
        n = piece.shape[0]
        vectors.append(table[:, offset : offset + n].reshape(-1).astype(F32))
        offset += n
    gain_one, shift_one, qbias, vbias, pbias, gain_two, shift_two, ubias, dbias = vectors
    qbias = lax.dynamic_slice(qbias, (at * qcols,), (qcols,))
    ubias = lax.dynamic_slice(
        ubias.reshape(chips, 2 * depth, frows), (0, core * depth + level, 0), (chips, 1, frows)
    ).reshape(-1)

    up_parts = (
        after(up_weight, attn_all)
        .reshape(wrows, chips, 2 * depth, frows)
        .transpose(2, 0, 1, 3)
        .reshape(2 * depth, wrows, chips * frows)
    )
    up_parts = lax.all_to_all(
        up_parts, BOTH, 0, 0, tiled=True, axis_index_groups=chip_devices()
    ).reshape(2 * depth * wrows, chips * frows)
    mlp_pieces = column_direct(after(grad_mlp_own, up_parts))

    normed_one = (scaled_all * gain_one + shift_one).astype(BF)
    mixed = dot(normed_one, qkv_local, 1, 0)
    total = span * count
    queries = (mixed[:, :qcols] + qbias).astype(BF)
    mine = (mixed[:, qcols:] + jnp.where(core == 1, vbias, 0.0)).astype(BF)
    theirs = jnp.roll(exchange(mine, 1), total // 2, 0)
    keys = jnp.where(core == 0, mine, theirs)
    values = jnp.where(core == 0, theirs, mine)
    base = jnp.stack([at ^ (2 * k + j) for j in range(2) for k in range(chips)]) * span
    pos = (base[:, None] + jnp.arange(span, dtype=jnp.int32)[None]).reshape(total)
    allowed = (pos[None, :] <= pos[:, None]) & (pos[None, :] < length)
    heads = []
    attended_f = []
    for h in range(share):
        q = queries[:, h * HD : (h + 1) * HD]
        scores = jnp.where(allowed, dot(q, keys, 1, 1) * scale, NEG)
        top = jnp.max(scores, -1, keepdims=True)
        expo = jnp.where(allowed, jnp.exp(scores - top), 0.0)
        probs = expo / jnp.sum(expo, -1, keepdims=True)
        attended_f.append(dot(probs.astype(BF), values, 1, 0))
        heads.append((q, probs))
    attended = jnp.concatenate(attended_f, 1).astype(BF)
    branch = plane_scatter(attended, proj_local, 0)
    middle = own_rows + branch + pbias
    scaled_two, inverse_two = normalize(middle)
    normed_two_own = (scaled_two * gain_two + shift_two).astype(BF)

    up_local = lax.all_gather(
        after(up_parts, normed_two_own), "ctx", axis=0, tiled=True, axis_index_groups=chip_groups()
    )
    chip = at // 2
    down_local = jnp.zeros((chips, frows, width), BF)
    for k, piece in enumerate(down_pieces):
        down_local = lax.dynamic_update_slice(down_local, piece[None], (chip ^ k, 0, 0))
    down_local = down_local.reshape(chips * frows, width)
    grad_mlp = both_cores(mlp_pieces)
    grad_active = dot(grad_mlp, down_local, 1, 1)
    normed_two = both_cores(column_chain(normed_two_own))
    normed_two, grad_active = lax.optimization_barrier((normed_two, grad_active))
    before = dot(normed_two, up_local, 1, 0) + ubias
    active_f, gelu_pull = jax.vjp(gelu, before)
    active = active_f.astype(BF)
    grad_before = gelu_pull(grad_active)[0].astype(BF)
    ubias_term = jnp.sum(grad_before.astype(F32), 0)
    grad_two = column_scatter(grad_before, up_local, 1, True)

    def chip_sum(term):
        return lax.psum_scatter(
            term, "ctx", scatter_dimension=0, tiled=True, axis_index_groups=chip_groups()
        )

    down_term = dot(active, grad_mlp, 0, 0).astype(BF)
    up_term = dot(normed_two, grad_before, 0, 0).astype(BF)
    grad_two, down_term, up_term = lax.optimization_barrier((grad_two, down_term, up_term))
    down_grad = chip_sum(down_term)
    up_grad = chip_sum(up_term)
    gain_two_term = jnp.sum(grad_two * scaled_two, 0)
    shift_two_term = jnp.sum(grad_two, 0)
    grad_middle = upstream + norm_backward(grad_two, scaled_two, inverse_two, gain_two)
    grad_branch_own = grad_middle.astype(BF)
    pbias_term = jnp.sum(grad_branch_own.astype(F32), 0)
    dbias_term = jnp.sum(grad_mlp_own.astype(F32), 0)
    active_late = after(active, grad_branch_own)
    result = middle + column_scatter(active_late, down_local, 0, False) + dbias
    layer_out = jnp.where(live, result, 0.0).astype(BF)

    grad_branch = both_cores(plane_pieces(grad_branch_own))
    grad_attended = dot(grad_branch, proj_local, 1, 1).astype(BF)
    proj_grad = lax.psum_scatter(
        dot(attended, grad_branch, 0, 0).astype(BF), "fsdp", scatter_dimension=0, tiled=True
    ).astype(F32)
    grad_queries, grad_keys, grad_values = [], 0.0, 0.0
    for h in range(share):
        q, probs = heads[h]
        ga = grad_attended[:, h * HD : (h + 1) * HD]
        delta = jnp.sum(ga.astype(F32) * attended_f[h], -1, keepdims=True)
        grad_scores = (probs * (dot(ga, values, 1, 1) - delta)).astype(BF)
        grad_queries.append((dot(grad_scores, keys, 1, 0) * scale).astype(BF))
        grad_keys = grad_keys + dot(grad_scores, q, 0, 0)
        grad_values = grad_values + dot(probs.astype(BF), ga, 0, 0)
    grad_keys = grad_keys * scale
    given = jnp.where(core == 0, grad_values, grad_keys).astype(BF)
    given = jnp.roll(exchange(given, 1), total // 2, 0).astype(F32)
    grad_kind = (jnp.where(core == 0, grad_keys, grad_values) + given).astype(BF)
    grad_mixed = jnp.concatenate(grad_queries + [grad_kind], 1)
    grad_one = plane_scatter(grad_mixed, qkv_local, 1)
    qkv_term = dot(normed_one, grad_mixed, 0, 0).astype(BF)
    qkv_term = qkv_term.reshape(count, depth, wrows, wide_cols).transpose(1, 0, 2, 3)
    qkv_grad = lax.psum_scatter(
        qkv_term.reshape(depth * count * wrows, wide_cols),
        "fsdp",
        scatter_dimension=0,
        tiled=True,
    ).reshape(count, wrows, wide_cols)
    qkv_grad = lax.all_to_all(qkv_grad, "ctx", 0, 0, tiled=True).transpose(1, 0, 2).astype(F32)
    kinds = jnp.sum(qkv_grad[:, :, qcols:].reshape(wrows, chips, 2 * HD), 1)
    qkv_grad = jnp.concatenate([qkv_grad[:, :, :qcols].reshape(wrows, width), kinds], 1)
    scaled_one, inverse_one = normalize(own_rows)
    gain_one_term = jnp.sum(grad_one * scaled_one, 0)
    shift_one_term = jnp.sum(grad_one, 0)
    input_grad = grad_middle + norm_backward(grad_one, scaled_one, inverse_one, gain_one)

    up_grad = lax.all_to_all(
        up_grad.reshape(2 * depth, wrows, chips * frows),
        BOTH,
        0,
        0,
        tiled=True,
        axis_index_groups=chip_devices(),
    )
    up_grad = (
        up_grad.reshape(2 * depth, wrows, chips, frows)
        .transpose(1, 2, 0, 3)
        .reshape(wrows, hidden)
        .astype(F32)
    )
    down_grad = down_grad.astype(F32)

    mixed_term = jnp.sum(grad_mixed.astype(F32), 0)
    qbias_term = mixed_term[:qcols]
    vbias_term = jnp.where(core == 1, mixed_term[qcols:], 0.0)
    wide = [gain_one_term, shift_one_term, pbias_term, gain_two_term, shift_two_term, dbias_term]
    spread = jnp.concatenate(
        [v.reshape(count, depth, -1) for v in wide + [vbias_term]], 2
    ).reshape(count, -1)
    ub = ubias_term.reshape(chips, 1, frows) * (jnp.arange(2) == core).astype(F32)[None, :, None]
    spread = jnp.concatenate([spread, ub.reshape(count, frows)], 1)
    held = spread.shape[1]
    spread = jnp.pad(spread, ((0, 0), (0, -held % 1024))).reshape(count, -1, 128)
    first = jnp.sum(lax.all_to_all(spread, "ctx", 0, 0, tiled=True), 0).reshape(-1)
    ubias_grad = first[held - frows : held]
    second = jnp.concatenate(
        [first[: held - frows].reshape(depth, -1), qbias_term.reshape(depth, -1)], 1
    )
    kept = second.shape[1]
    second = jnp.pad(second, ((0, 0), (0, -kept % 1024))).reshape(depth, -1, 128)
    second = jnp.sum(lax.all_to_all(second, "fsdp", 0, 0, tiled=True), 0).reshape(-1)
    wide_grads = [second[i * wrows : (i + 1) * wrows] for i in range(6)]
    edge = 6 * wrows
    vn = value_bias.shape[0]
    vbias_grad = second[edge : edge + vn]
    qbias_grad = second[edge + vn : edge + vn + wrows]
    return (
        layer_out[None],
        input_grad[None],
        wide_grads[0],
        wide_grads[1],
        qkv_grad,
        qbias_grad,
        vbias_grad,
        proj_grad,
        wide_grads[2],
        wide_grads[3],
        wide_grads[4],
        up_grad,
        ubias_grad,
        down_grad,
        wide_grads[5],
    )


def solution(mesh):
    rows = P("fsdp", "ctx", None)
    vector = P(BOTH)
    matrix = P(BOTH, None)
    return jax.shard_map(
        body,
        mesh=mesh,
        in_specs=(
            rows, rows, P("fsdp"), vector, vector, matrix, vector, vector, matrix,
            vector, vector, vector, matrix, vector, matrix, vector,
        ),
        out_specs=(
            rows, rows, vector, vector, matrix, vector, vector, matrix, vector,
            vector, vector, matrix, vector, matrix, vector,
        ),
        check_vma=False,
    )
```

time: 4270 us -> 662 us (0.16)
  waiting for transfers between devices: 3800 us -> 335 us
  blocking collectives: 110 us -> 13.9 us
  matrix products: 174 us -> 118 us
    reduce_scatter x4, waiting for transfers between devices: 3400 us -> 83.7 us  [the longest x2 83.7 us: chip_sum(): lax.psum_scatter(term, 'ctx', scatter_dimension=0, tiled=True, axis_index...]
    all_gather x4 -> x3, waiting for transfers between devices: 346 us -> 9.73 us  [the longest x1 4.91 us: body(): attn_all = lax.all_gather(incoming, 'fsdp', axis=0)]
    ppermute x23 -> x55, waiting for transfers between devices: 25.4 us -> 205 us  [the longest x37 105 us: exchange(): return lax.ppermute(value, 'ctx', [(i, i ^ mask) for i in range(count)])]
    all_gather x1 -> x0, blocking collectives: 66.5 us -> none  [body(): lax.all_gather(up_bias, ('ctx', 'fsdp'), axis=0, tiled=True)]
    dot_general x19 -> x40, matrix products: 174 us -> 118 us  [dot(): lax.dot_general(a, b, (((da,), (db,)), ((), ())), preferred_element_type=...]
    ppermute x23 -> x55, starting transfers between devices: 103 us -> 58.4 us  [the longest x37 22.1 us: exchange(): return lax.ppermute(value, 'ctx', [(i, i ^ mask) for i in range(count)])]
    unnamed x1 -> x0, blocking collectives: 43.2 us -> none
  transfers between devices with their start and end apart: 32 -> 67, of which waited for: 28 -> 30; matrix products, arithmetic and copies ran while one was open for 3% -> 23% of each run, Pallas kernels for 0% -> 0%
where the time goes in v1:
time: 662 us; the launch traced here: 653 us
  waiting for transfers between devices  335 us (51%)
  matrix products  118 us (18%)
  starting transfers between devices  78.4 us (12%)
  local copies, waits for them, and re-layouts  47 us (7%)
  other arithmetic  45.4 us (7%)
  between operations  16.3 us (2%)
  blocking collectives  13.9 us (2%)
    dot_general x40, matrix products, dot(): lax.dot_general(a, b, (((da,), (db,)), ((), ())), preferred_element_type=...  118 us
    ppermute x37, waiting for transfers between devices, exchange(): return lax.ppermute(value, 'ctx', [(i, i ^ mask) for i in range(count)])  105 us
    reduce_scatter x2, waiting for transfers between devices, chip_sum(): lax.psum_scatter(term, 'ctx', scatter_dimension=0, tiled=True, axis_index...  83.7 us
    ppermute x6, waiting for transfers between devices, turned(): lax.ppermute(value, 'fsdp', [(i, (i + by) % depth) for i in range(depth)])  43.3 us
    all_to_all x1, waiting for transfers between devices, body(): lax.all_to_all(second, 'fsdp', 0, 0, tiled=True)  26 us
    ppermute x3, waiting for transfers between devices, column_chain(): lax.ppermute(downward[-1], 'fsdp', [(i, i - 1) for i in range(1, depth -...  24.7 us
    ppermute x37, starting transfers between devices, exchange(): return lax.ppermute(value, 'ctx', [(i, i ^ mask) for i in range(count)])  22.1 us
    ppermute x3, waiting for transfers between devices, column_scatter(): lax.ppermute(rising.astype(BF), 'fsdp', [(i, i + 1) for i in range(min(s,...  19.5 us
  transfers between devices with their start and end apart: 67, of which 30 were waited for; matrix products, arithmetic and copies ran while one was open for 23% of the time, Pallas kernels for 0%

profile of v1, /device:TPU:0, one launch (start us, length us, event | category | flops | bytes accessed | tf_op | source)
XLA Modules:
  0.0 653.3 jit_solution(16685757654205836297)
XLA Ops:
  9.0 6.1 concatenate.52
  15.4 13.9 %all_to_all.30 = bf16[8,72,384]{2,1,0:T(8,128)(2,1)} all-to-all(bf16[8,72,384]{2,1,0:T(8,128)(2,1)S(1)} %copy.143), channel_id=1, replica_groups=mesh['ctx'=8,'fsdp'=4] {'ctx'}, dimensions={0} | all-to-all | bytes 884736 | tf_op jit(solution)/shard_map/all_to_all | solution.py:211
  34.0 12.0 %collective-permute-done.2 = bf16[128,2048]{1,0:T(8,128)(2,1)S(1)} collective-permute-done((bf16[128,2048]{1,0:T(8,128)(2,1)S(1)}, bf16[128,2048]{1,0:T(8,128)(2,1)S(1)}, u32[]{:S(2)}, u32[]{:S(2)}) %collective-permute-start.2) | collective-permute-done | bytes 524320 | tf_op jit(solution)/shard_map/ppermute | solution.py:48
  46.0 9.4 %collective-permute-done.1 = bf16[128,2048]{1,0:T(8,128)(2,1)S(1)} collective-permute-done((bf16[128,2048]{1,0:T(8,128)(2,1)S(1)}, bf16[128,2048]{1,0:T(8,128)(2,1)S(1)}, u32[]{:S(2)}, u32[]{:S(2)}) %collective-permute-start.1) | collective-permute-done | bytes 524320 | tf_op jit(solution)/shard_map/ppermute | solution.py:48
  60.1 4.2 fusion
  64.3 4.9 all-gather.9.cloned.1.call-done
  72.5 5.7 fusion.33
  85.6 3.3 fusion.24
  92.8 4.8 all-gather.5.cloned.1.call-done
  113.5 4.3 all-to-all-start.1
  127.3 24.5 %collective-permute-done.29 = bf16[256,2048]{1,0:T(8,128)(2,1)} collective-permute-done((bf16[256,2048]{1,0:T(8,128)(2,1)}, bf16[256,2048]{1,0:T(8,128)(2,1)}, u32[]{:S(2)}, u32[]{:S(2)}) %collective-permute-start.29) | collective-permute-done | bytes 1048608 | tf_op jit(solution)/shard_map/ppermute | solution.py:48
  156.9 6.2 collective-permute-done.9
  163.1 10.8 %collective-permute-done.11 = bf16[128,2048]{1,0:T(8,128)(2,1)} collective-permute-done((bf16[128,2048]{1,0:T(8,128)(2,1)}, bf16[128,2048]{1,0:T(8,128)(2,1)}, u32[]{:S(2)}, u32[]{:S(2)}) %collective-permute-start.11) | collective-permute-done | bytes 524320 | tf_op jit(solution)/shard_map/ppermute | solution.py:48
  187.4 9.4 %collective-permute-done.24 = bf16[128,2048]{1,0:T(8,128)(2,1)S(1)} collective-permute-done((bf16[128,2048]{1,0:T(8,128)(2,1)S(1)}, bf16[128,2048]{1,0:T(8,128)(2,1)S(1)}, u32[]{:S(2)}, u32[]{:S(2)}) %collective-permute-start.24) | collective-permute-done | bytes 524320 | tf_op jit(solution)/shard_map/ppermute | solution.py:107
  196.8 33.8 %collective-permute-done.23 = bf16[128,2048]{1,0:T(8,128)(2,1)S(1)} collective-permute-done((bf16[128,2048]{1,0:T(8,128)(2,1)S(1)}, bf16[128,2048]{1,0:T(8,128)(2,1)S(1)}, u32[]{:S(2)}, u32[]{:S(2)}) %collective-permute-start.23) | collective-permute-done | bytes 524320 | tf_op jit(solution)/shard_map/ppermute | solution.py:107
  233.3 4.0 collective-permute-start.12
  237.3 9.6 %collective-permute-done.13 = bf16[128,2048]{1,0:T(8,128)(2,1)S(1)} collective-permute-done((bf16[128,2048]{1,0:T(8,128)(2,1)S(1)}, bf16[128,2048]{1,0:T(8,128)(2,1)S(1)}, u32[]{:S(2)}, u32[]{:S(2)}) %collective-permute-start.13) | collective-permute-done | bytes 524320 | tf_op jit(solution)/shard_map/ppermute | solution.py:98
  249.8 12.0 %collective-permute-done.14 = bf16[128,2048]{1,0:T(8,128)(2,1)S(1)} collective-permute-done((bf16[128,2048]{1,0:T(8,128)(2,1)S(1)}, bf16[128,2048]{1,0:T(8,128)(2,1)S(1)}, u32[]{:S(2)}, u32[]{:S(2)}) %collective-permute-start.14) | collective-permute-done | bytes 524320 | tf_op jit(solution)/shard_map/ppermute | solution.py:98
  263.0 8.8 %fusion.130 = f32[1024,1024]{1,0:T(8,128)} fusion(bf16[1024,2048]{1,0:T(8,128)(2,1)S(1)} %constant_dynamic-update-slice_fusion.16, bf16[1024,2048]{1,0:T(8,128)(2,1)} %bitcast.24), kind=kOutput, calls=%fused_computation.268 | convolution fusion | flops 4294967296 | bytes 12582912 | tf_op jit(solution)/shard_map/dot_general | solution.py:18
  282.7 7.6 %fusion.131 = f32[1024,1024]{1,0:T(8,128)S(1)} fusion(bf16[1024,2048]{1,0:T(8,128)(2,1)} %constant_dynamic-update-slice_fusion.8, bf16[2048,1024]{1,0:T(8,128)(2,1)} %all-gather.7.cloned.1.call-done), kind=kOutput, calls=%fused_computation.269 | convolution fusion | flops 4294967296 | bytes 12582912 | tf_op jit(solution)/shard_map/dot_general | solution.py:18
  290.4 4.3 convert_reduce_fusion.1
  297.6 3.8 collective-permute-done.32
  306.9 10.2 %collective-permute-done.33 = bf16[128,2048]{1,0:T(8,128)(2,1)S(1)} collective-permute-done((bf16[128,2048]{1,0:T(8,128)(2,1)S(1)}, bf16[128,2048]{1,0:T(8,128)(2,1)S(1)}, u32[]{:S(2)}, u32[]{:S(2)}) %collective-permute-start.33) | collective-permute-done | bytes 524320 | tf_op jit(solution)/shard_map/ppermute | solution.py:137
  317.4 4.6 collective-permute-start.34
  323.5 9.3 %collective-permute-done.34 = bf16[128,2048]{1,0:T(8,128)(2,1)S(1)} collective-permute-done((bf16[128,2048]{1,0:T(8,128)(2,1)S(1)}, bf16[128,2048]{1,0:T(8,128)(2,1)S(1)}, u32[]{:S(2)}, u32[]{:S(2)}) %collective-permute-start.34) | collective-permute-done | bytes 524320 | tf_op jit(solution)/shard_map/ppermute | solution.py:137
  337.0 8.4 %convolution_convert_fusion = bf16[2048,1024]{1,0:T(8,128)(2,1)} fusion(bf16[1024,2048]{1,0:T(8,128)(2,1)} %constant_dynamic-update-slice_fusion.8, bf16[1024,1024]{1,0:T(8,128)(2,1)S(1)} %get-tuple-element.63), kind=kOutput, calls=%fused_computation.24 | convolution fusion | flops 4297064448 | bytes 10485760 | tf_op jit(solution)/shard_map/dot_general | solution.py:18
  345.3 5.0 collective-permute-start.35
  354.2 9.4 %convolution_convert_fusion.1 = bf16[1024,2048]{1,0:T(8,128)(2,1)} fusion(bf16[1024,1024]{1,0:T(8,128)(2,1)} %get-tuple-element.40, bf16[1024,2048]{1,0:T(8,128)(2,1)} %copy-done.35), kind=kOutput, calls=%fused_computation.25 | convolution fusion | flops 4297064448 | bytes 10485760 | tf_op jit(solution)/shard_map/dot_general | solution.py:18
  363.6 3.8 fusion.59
  367.4 12.0 %collective-permute-done.38 = bf16[128,2048]{1,0:T(8,128)(2,1)} collective-permute-done((bf16[128,2048]{1,0:T(8,128)(2,1)}, bf16[128,2048]{1,0:T(8,128)(2,1)}, u32[]{:S(2)}, u32[]{:S(2)}) %collective-permute-start.38) | collective-permute-done | bytes 524320 | tf_op jit(solution)/shard_map/ppermute | solution.py:140
  386.5 12.2 %collective-permute-done.45 = bf16[128,2048]{1,0:T(8,128)(2,1)S(1)} collective-permute-done((bf16[128,2048]{1,0:T(8,128)(2,1)S(1)}, bf16[128,2048]{1,0:T(8,128)(2,1)S(1)}, u32[]{:S(2)}, u32[]{:S(2)}) %collective-permute-start.45) | collective-permute-done | bytes 524320 | tf_op jit(solution)/shard_map/ppermute | solution.py:48
  398.8 7.2 %collective-permute-done.44 = bf16[128,2048]{1,0:T(8,128)(2,1)S(1)} collective-permute-done((bf16[128,2048]{1,0:T(8,128)(2,1)S(1)}, bf16[128,2048]{1,0:T(8,128)(2,1)S(1)}, u32[]{:S(2)}, u32[]{:S(2)}) %collective-permute-start.44) | collective-permute-done | bytes 524320 | tf_op jit(solution)/shard_map/ppermute | solution.py:48
  428.6 4.5 convolution_convert_fusion.7
  434.5 6.2 convolution_convert_fusion.2
  446.0 3.9 fusion.19
  450.0 8.0 %collective-permute-start.40 = (bf16[128,2048]{1,0:T(8,128)(2,1)}, bf16[128,2048]{1,0:T(8,128)(2,1)}, u32[]{:S(2)}, u32[]{:S(2)}) collective-permute-start(bf16[128,2048]{1,0:T(8,128)(2,1)} %fusion.19), channel_id=1, source_target_pairs={{0,3},{1,0},{2,1},{3,2},{4,7},{5,4},{6,5},{7,6},{8,11},{9,8},{10,9... | collective-permute-start | bytes 1572872 | tf_op jit(solution)/shard_map/ppermute | solution.py:107
  466.8 3.9 fusion.20
  470.8 3.9 fusion.21
  475.2 12.4 %collective-permute-done.53 = bf16[128,2048]{1,0:T(8,128)(2,1)S(1)} collective-permute-done((bf16[128,2048]{1,0:T(8,128)(2,1)S(1)}, bf16[128,2048]{1,0:T(8,128)(2,1)S(1)}, u32[]{:S(2)}, u32[]{:S(2)}) %collective-permute-start.53) | collective-permute-done | bytes 524320 | tf_op jit(solution)/shard_map/ppermute | solution.py:48
  491.5 3.3 all-to-all-start.2
  494.9 4.9 all-to-all-done.2
  503.9 26.0 %all-to-all-done.3 = f32[4,8,128]{2,1,0:T(8,128)S(1)} async-done(((f32[4,8,128]{2,1,0:T(8,128)}), f32[4,8,128]{2,1,0:T(8,128)S(1)}, u32[]{:S(2)}, u32[]{:S(2)}) %all-to-all-start.3) | async-done | bytes 16416 | tf_op jit(solution)/shard_map/all_to_all | solution.py:382
  529.8 3.6 all-to-all-start.4
  533.5 4.9 fusion.22
  540.2 4.1 all-to-all-done.4
  544.3 38.7 %reduce-scatter.9.cloned.1.call-done = bf16[512,1024]{1,0:T(8,128)(2,1)} async-done(((bf16[2048,1024]{1,0:T(8,128)(2,1)}), bf16[512,1024]{1,0:T(8,128)(2,1)}) %reduce-scatter.9.cloned.1.call-update) | async-done | bytes 1048592 | tf_op jit(solution)/shard_map/reduce_scatter | solution.py:293
  583.0 4.8 all-to-all-start.5
  593.8 45.0 %reduce-scatter.11.cloned.1.call-done = bf16[256,2048]{1,0:T(8,128)(2,1)} async-done(((bf16[1024,2048]{1,0:T(8,128)(2,1)}), bf16[256,2048]{1,0:T(8,128)(2,1)}) %reduce-scatter.11.cloned.1.call-update) | async-done | bytes 1048592 | tf_op jit(solution)/shard_map/reduce_scatter | solution.py:293
  (366 shorter events, 172.9 us)
Async XLA Ops:
  7.2 62.1 %all-gather.9.cloned.1.call-start = ((), (), s32[]{:S(2)}) async-start(), calls=%async_computation.16 | async-start | bytes 2211840 | tf_op jit(solution)/shard_map/all_gather | solution.py:212
  29.4 68.3 %all-gather.5.cloned.1.call-start = ((), (), s32[]{:S(2)}) async-start(), calls=%async_computation.10 | async-start | bytes 1310720 | tf_op jit(solution)/shard_map/all_gather | solution.py:216
  30.2 15.8 %collective-permute-start.2 = (bf16[128,2048]{1,0:T(8,128)(2,1)S(1)}, bf16[128,2048]{1,0:T(8,128)(2,1)S(1)}, u32[]{:S(2)}, u32[]{:S(2)}) collective-permute-start(bf16[128,2048]{1,0:T(8,128)(2,1)S(1)} %bitcast.148), channel_id=1, source_target_pairs={{0,24},{4,28},{8,16},{12,20},{16,8},{20,12},{24,0},{28,4},{1,25},{... | collective-permute-start | bytes 1572872 | tf_op jit(solution)/shard_map/ppermute | solution.py:48
  30.8 24.6 %collective-permute-start.1 = (bf16[128,2048]{1,0:T(8,128)(2,1)S(1)}, bf16[128,2048]{1,0:T(8,128)(2,1)S(1)}, u32[]{:S(2)}, u32[]{:S(2)}) collective-permute-start(bf16[128,2048]{1,0:T(8,128)(2,1)S(1)} %bitcast.149), channel_id=1, source_target_pairs={{0,16},{4,20},{8,24},{12,28},{16,0},{20,4},{24,8},{28,12},{1,17},{... | collective-permute-start | bytes 1572872 | tf_op jit(solution)/shard_map/ppermute | solution.py:48
  32.3 23.1 %collective-permute-start = (bf16[128,2048]{1,0:T(8,128)(2,1)S(1)}, bf16[128,2048]{1,0:T(8,128)(2,1)S(1)}, u32[]{:S(2)}, u32[]{:S(2)}) collective-permute-start(bf16[128,2048]{1,0:T(8,128)(2,1)S(1)} %bitcast.150), channel_id=1, source_target_pairs={{0,8},{4,12},{8,0},{12,4},{16,24},{20,28},{24,16},{28,20},{1,9},{5... | collective-permute-start | bytes 1572872 | tf_op jit(solution)/shard_map/ppermute | solution.py:48
  33.9 22.2 %collective-permute-start.3 = (bf16[128,2048]{1,0:T(8,128)(2,1)S(1)}, bf16[128,2048]{1,0:T(8,128)(2,1)S(1)}, u32[]{:S(2)}, u32[]{:S(2)}) collective-permute-start(bf16[128,2048]{1,0:T(8,128)(2,1)S(1)} %bitcast.151), channel_id=1, source_target_pairs={{0,4},{4,0},{8,12},{12,8},{16,20},{20,16},{24,28},{28,24},{1,5},{5... | collective-permute-start | bytes 1572872 | tf_op jit(solution)/shard_map/ppermute | solution.py:48
  100.9 16.9 %collective-permute-start.8 = (bf16[512,2048]{1,0:T(8,128)(2,1)}, bf16[512,2048]{1,0:T(8,128)(2,1)}, u32[]{:S(2)}, u32[]{:S(2)}) collective-permute-start(bf16[512,2048]{1,0:T(8,128)(2,1)} %convolution_convert_fusion.4), channel_id=1, source_target_pairs={{0,4},{4,0},{8,12},{12,8},{16,20},{20,16},{24,28},{28,24},{1,5},{5... | collective-permute-start | bytes 6291464 | tf_op jit(solution)/shard_map/ppermute | solution.py:48
  102.1 78.0 %collective-permute-start.31 = (bf16[256,2048]{1,0:T(8,128)(2,1)}, bf16[256,2048]{1,0:T(8,128)(2,1)}, u32[]{:S(2)}, u32[]{:S(2)}) collective-permute-start(bf16[256,2048]{1,0:T(8,128)(2,1)} %param.30), channel_id=1, source_target_pairs={{0,24},{4,28},{8,16},{12,20},{16,8},{20,12},{24,0},{28,4},{1,25},{... | collective-permute-start | bytes 3145736 | tf_op jit(solution)/shard_map/ppermute | solution.py:48
  104.5 73.2 %collective-permute-start.30 = (bf16[256,2048]{1,0:T(8,128)(2,1)}, bf16[256,2048]{1,0:T(8,128)(2,1)}, u32[]{:S(2)}, u32[]{:S(2)}) collective-permute-start(bf16[256,2048]{1,0:T(8,128)(2,1)} %param.30), channel_id=1, source_target_pairs={{0,16},{4,20},{8,24},{12,28},{16,0},{20,4},{24,8},{28,12},{1,17},{... | collective-permute-start | bytes 3145736 | tf_op jit(solution)/shard_map/ppermute | solution.py:48
  105.0 46.8 %collective-permute-start.29 = (bf16[256,2048]{1,0:T(8,128)(2,1)}, bf16[256,2048]{1,0:T(8,128)(2,1)}, u32[]{:S(2)}, u32[]{:S(2)}) collective-permute-start(bf16[256,2048]{1,0:T(8,128)(2,1)} %param.30), channel_id=1, source_target_pairs={{0,8},{4,12},{8,0},{12,4},{16,24},{20,28},{24,16},{28,20},{1,9},{5... | collective-permute-start | bytes 3145736 | tf_op jit(solution)/shard_map/ppermute | solution.py:48
  113.5 64.1 %all-to-all-start.1 = ((bf16[8,64,1024]{2,1,0:T(8,128)(2,1)}), bf16[8,64,1024]{2,1,0:T(8,128)(2,1)}, u32[]{:S(2)}, u32[]{:S(2)}) async-start(bf16[8,64,1024]{2,1,0:T(8,128)(2,1)} %reshape.395), calls=%async_computation.1 | async-start | bytes 2097152 | tf_op jit(solution)/shard_map/all_to_all | solution.py:241
  117.8 164.9 %all-gather.7.cloned.1.call-start = ((), (), s32[]{:S(2)}) async-start(), calls=%async_computation.11 | async-start | bytes 5242880 | tf_op jit(solution)/shard_map/all_gather | solution.py:273
  120.1 43.0 %collective-permute-start.9 = (bf16[128,2048]{1,0:T(8,128)(2,1)}, bf16[128,2048]{1,0:T(8,128)(2,1)}, u32[]{:S(2)}, u32[]{:S(2)}) collective-permute-start(bf16[128,2048]{1,0:T(8,128)(2,1)} %add_convert_fusion.13), channel_id=1, source_target_pairs={{0,8},{4,12},{8,0},{12,4},{16,24},{20,28},{24,16},{28,20},{1,9},{5... | collective-permute-start | bytes 1572872 | tf_op jit(solution)/shard_map/ppermute | solution.py:48
  123.7 39.4 %collective-permute-start.10 = (bf16[128,2048]{1,0:T(8,128)(2,1)}, bf16[128,2048]{1,0:T(8,128)(2,1)}, u32[]{:S(2)}, u32[]{:S(2)}) collective-permute-start(bf16[128,2048]{1,0:T(8,128)(2,1)} %add_convert_fusion.12), channel_id=1, source_target_pairs={{0,16},{4,20},{8,24},{12,28},{16,0},{20,4},{24,8},{28,12},{1,17},{... | collective-permute-start | bytes 1572872 | tf_op jit(solution)/shard_map/ppermute | solution.py:48
  151.8 22.1 %collective-permute-start.11 = (bf16[128,2048]{1,0:T(8,128)(2,1)}, bf16[128,2048]{1,0:T(8,128)(2,1)}, u32[]{:S(2)}, u32[]{:S(2)}) collective-permute-start(bf16[128,2048]{1,0:T(8,128)(2,1)} %add_convert_fusion.11), channel_id=1, source_target_pairs={{0,24},{4,28},{8,16},{12,20},{16,8},{20,12},{24,0},{28,4},{1,25},{... | collective-permute-start | bytes 1572872 | tf_op jit(solution)/shard_map/ppermute | solution.py:48
  177.6 352.2 %reduce-scatter.5.cloned.1.call-start = ((), (), s32[]{:S(2)}) async-start(), calls=%async_computation.12 | async-start | bytes 1966080 | tf_op jit(solution)/shard_map/reduce_scatter | solution.py:334
  182.5 14.3 %collective-permute-start.24 = (bf16[128,2048]{1,0:T(8,128)(2,1)S(1)}, bf16[128,2048]{1,0:T(8,128)(2,1)S(1)}, u32[]{:S(2)}, u32[]{:S(2)}) collective-permute-start(bf16[128,2048]{1,0:T(8,128)(2,1)S(1)} %copy-done.26), channel_id=1, source_target_pairs={{0,3},{1,0},{2,1},{3,2},{4,7},{5,4},{6,5},{7,6},{8,11},{9,8},{10,9... | collective-permute-start | bytes 1572872 | tf_op jit(solution)/shard_map/ppermute | solution.py:107
  184.4 46.2 %collective-permute-start.23 = (bf16[128,2048]{1,0:T(8,128)(2,1)S(1)}, bf16[128,2048]{1,0:T(8,128)(2,1)S(1)}, u32[]{:S(2)}, u32[]{:S(2)}) collective-permute-start(bf16[128,2048]{1,0:T(8,128)(2,1)S(1)} %copy-done.26), channel_id=1, source_target_pairs={{0,2},{1,3},{2,0},{3,1},{4,6},{5,7},{6,4},{7,5},{8,10},{9,11},{10,... | collective-permute-start | bytes 1572872 | tf_op jit(solution)/shard_map/ppermute | solution.py:107
  185.4 45.2 %collective-permute-start.22 = (bf16[128,2048]{1,0:T(8,128)(2,1)S(1)}, bf16[128,2048]{1,0:T(8,128)(2,1)S(1)}, u32[]{:S(2)}, u32[]{:S(2)}) collective-permute-start(bf16[128,2048]{1,0:T(8,128)(2,1)S(1)} %copy-done.26), channel_id=1, source_target_pairs={{0,1},{1,2},{2,3},{3,0},{4,5},{5,6},{6,7},{7,4},{8,9},{9,10},{10,1... | collective-permute-start | bytes 1572872 | tf_op jit(solution)/shard_map/ppermute | solution.py:107
  187.2 45.3 %collective-permute-start.25 = (bf16[128,2048]{1,0:T(8,128)(2,1)S(1)}, bf16[128,2048]{1,0:T(8,128)(2,1)S(1)}, u32[]{:S(2)}, u32[]{:S(2)}) collective-permute-start(bf16[128,2048]{1,0:T(8,128)(2,1)S(1)} %copy-done.26), channel_id=1, source_target_pairs={{0,4},{4,0},{8,12},{12,8},{16,20},{20,16},{24,28},{28,24},{1,5},{5... | collective-permute-start | bytes 1572872 | tf_op jit(solution)/shard_map/ppermute | solution.py:48
  196.8 51.5 %collective-permute-start.28 = (bf16[128,2048]{1,0:T(8,128)(2,1)S(1)}, bf16[128,2048]{1,0:T(8,128)(2,1)S(1)}, u32[]{:S(2)}, u32[]{:S(2)}) collective-permute-start(bf16[128,2048]{1,0:T(8,128)(2,1)S(1)} %collective-permute-done.24), channel_id=1, source_target_pairs={{0,4},{4,0},{8,12},{12,8},{16,20},{20,16},{24,28},{28,24},{1,5},{5... | collective-permute-start | bytes 1572872 | tf_op jit(solution)/shard_map/ppermute | solution.py:48
  230.6 17.6 %collective-permute-start.27 = (bf16[128,2048]{1,0:T(8,128)(2,1)S(1)}, bf16[128,2048]{1,0:T(8,128)(2,1)S(1)}, u32[]{:S(2)}, u32[]{:S(2)}) collective-permute-start(bf16[128,2048]{1,0:T(8,128)(2,1)S(1)} %collective-permute-done.23), channel_id=1, source_target_pairs={{0,4},{4,0},{8,12},{12,8},{16,20},{20,16},{24,28},{28,24},{1,5},{5... | collective-permute-start | bytes 1572872 | tf_op jit(solution)/shard_map/ppermute | solution.py:48
  231.2 15.7 %collective-permute-start.13 = (bf16[128,2048]{1,0:T(8,128)(2,1)S(1)}, bf16[128,2048]{1,0:T(8,128)(2,1)S(1)}, u32[]{:S(2)}, u32[]{:S(2)}) collective-permute-start(bf16[128,2048]{1,0:T(8,128)(2,1)S(1)} %copy-done.33), channel_id=1, source_target_pairs={{1,0},{2,1},{3,2},{5,4},{6,5},{7,6},{9,8},{10,9},{11,10},{13,12},{... | collective-permute-start | bytes 1572872 | tf_op jit(solution)/shard_map/ppermute | solution.py:98
  232.6 46.5 %collective-permute-start.18 = (bf16[128,2048]{1,0:T(8,128)(2,1)S(1)}, bf16[128,2048]{1,0:T(8,128)(2,1)S(1)}, u32[]{:S(2)}, u32[]{:S(2)}) collective-permute-start(bf16[128,2048]{1,0:T(8,128)(2,1)S(1)} %copy-done.33), channel_id=1, source_target_pairs={{0,4},{4,0},{8,12},{12,8},{16,20},{20,16},{24,28},{28,24},{1,5},{5... | collective-permute-start | bytes 1572872 | tf_op jit(solution)/shard_map/ppermute | solution.py:48
  233.3 15.8 %collective-permute-start.12 = (bf16[128,2048]{1,0:T(8,128)(2,1)S(1)}, bf16[128,2048]{1,0:T(8,128)(2,1)S(1)}, u32[]{:S(2)}, u32[]{:S(2)}) collective-permute-start(bf16[128,2048]{1,0:T(8,128)(2,1)S(1)} %copy-done.33), channel_id=1, source_target_pairs={{0,1},{1,2},{2,3},{4,5},{5,6},{6,7},{8,9},{9,10},{10,11},{12,13},{... | collective-permute-start | bytes 1572872 | tf_op jit(solution)/shard_map/ppermute | solution.py:95
  246.9 14.9 %collective-permute-start.14 = (bf16[128,2048]{1,0:T(8,128)(2,1)S(1)}, bf16[128,2048]{1,0:T(8,128)(2,1)S(1)}, u32[]{:S(2)}, u32[]{:S(2)}) collective-permute-start(bf16[128,2048]{1,0:T(8,128)(2,1)S(1)} %collective-permute-done.13), channel_id=1, source_target_pairs={{1,0},{2,1},{5,4},{6,5},{9,8},{10,9},{13,12},{14,13},{17,16},{18,1... | collective-permute-start | bytes 1572872 | tf_op jit(solution)/shard_map/ppermute | solution.py:98
  249.1 22.8 %collective-permute-start.16 = (bf16[128,2048]{1,0:T(8,128)(2,1)S(1)}, bf16[128,2048]{1,0:T(8,128)(2,1)S(1)}, u32[]{:S(2)}, u32[]{:S(2)}) collective-permute-start(bf16[128,2048]{1,0:T(8,128)(2,1)S(1)} %collective-permute-done.12), channel_id=1, source_target_pairs={{1,2},{2,3},{5,6},{6,7},{9,10},{10,11},{13,14},{14,15},{17,18},{18... | collective-permute-start | bytes 1572872 | tf_op jit(solution)/shard_map/ppermute | solution.py:95
  317.4 15.4 %collective-permute-start.34 = (bf16[128,2048]{1,0:T(8,128)(2,1)S(1)}, bf16[128,2048]{1,0:T(8,128)(2,1)S(1)}, u32[]{:S(2)}, u32[]{:S(2)}) collective-permute-start(bf16[128,2048]{1,0:T(8,128)(2,1)S(1)} %add_convert_fusion.9), channel_id=1, source_target_pairs={{0,1},{1,2},{4,5},{5,6},{8,9},{9,10},{12,13},{13,14},{16,17},{17,1... | collective-permute-start | bytes 1572872 | tf_op jit(solution)/shard_map/ppermute | solution.py:137
  335.5 14.9 %collective-permute-start.37 = (bf16[128,2048]{1,0:T(8,128)(2,1)}, bf16[128,2048]{1,0:T(8,128)(2,1)}, u32[]{:S(2)}, u32[]{:S(2)}) collective-permute-start(bf16[128,2048]{1,0:T(8,128)(2,1)} %add_convert_fusion.7), channel_id=1, source_target_pairs={{2,1},{3,2},{6,5},{7,6},{10,9},{11,10},{14,13},{15,14},{18,17},{19... | collective-permute-start | bytes 1572872 | tf_op jit(solution)/shard_map/ppermute | solution.py:140
  345.3 22.0 %collective-permute-start.35 = (bf16[128,2048]{1,0:T(8,128)(2,1)}, bf16[128,2048]{1,0:T(8,128)(2,1)}, u32[]{:S(2)}, u32[]{:S(2)}) collective-permute-start(bf16[128,2048]{1,0:T(8,128)(2,1)} %get-tuple-element.78), channel_id=1, source_target_pairs={{0,1},{1,2},{2,3},{4,5},{5,6},{6,7},{8,9},{9,10},{10,11},{12,13},{... | collective-permute-start | bytes 1572872 | tf_op jit(solution)/shard_map/ppermute | solution.py:137
  352.9 26.5 %collective-permute-start.38 = (bf16[128,2048]{1,0:T(8,128)(2,1)}, bf16[128,2048]{1,0:T(8,128)(2,1)}, u32[]{:S(2)}, u32[]{:S(2)}) collective-permute-start(bf16[128,2048]{1,0:T(8,128)(2,1)} %add_convert_fusion.6), channel_id=1, source_target_pairs={{1,0},{2,1},{3,2},{5,4},{6,5},{7,6},{9,8},{10,9},{11,10},{13,12},{... | collective-permute-start | bytes 1572872 | tf_op jit(solution)/shard_map/ppermute | solution.py:140
  383.0 15.8 %collective-permute-start.45 = (bf16[128,2048]{1,0:T(8,128)(2,1)S(1)}, bf16[128,2048]{1,0:T(8,128)(2,1)S(1)}, u32[]{:S(2)}, u32[]{:S(2)}) collective-permute-start(bf16[128,2048]{1,0:T(8,128)(2,1)S(1)} %get-tuple-element.60), channel_id=1, source_target_pairs={{0,24},{4,28},{8,16},{12,20},{16,8},{20,12},{24,0},{28,4},{1,25},{... | collective-permute-start | bytes 1572872 | tf_op jit(solution)/shard_map/ppermute | solution.py:48
  385.3 20.7 %collective-permute-start.44 = (bf16[128,2048]{1,0:T(8,128)(2,1)S(1)}, bf16[128,2048]{1,0:T(8,128)(2,1)S(1)}, u32[]{:S(2)}, u32[]{:S(2)}) collective-permute-start(bf16[128,2048]{1,0:T(8,128)(2,1)S(1)} %get-tuple-element.60), channel_id=1, source_target_pairs={{0,16},{4,20},{8,24},{12,28},{16,0},{20,4},{24,8},{28,12},{1,17},{... | collective-permute-start | bytes 1572872 | tf_op jit(solution)/shard_map/ppermute | solution.py:48
  385.9 20.2 %collective-permute-start.43 = (bf16[128,2048]{1,0:T(8,128)(2,1)S(1)}, bf16[128,2048]{1,0:T(8,128)(2,1)S(1)}, u32[]{:S(2)}, u32[]{:S(2)}) collective-permute-start(bf16[128,2048]{1,0:T(8,128)(2,1)S(1)} %get-tuple-element.60), channel_id=1, source_target_pairs={{0,8},{4,12},{8,0},{12,4},{16,24},{20,28},{24,16},{28,20},{1,9},{5... | collective-permute-start | bytes 1572872 | tf_op jit(solution)/shard_map/ppermute | solution.py:48
  386.5 20.2 %collective-permute-start.46 = (bf16[128,2048]{1,0:T(8,128)(2,1)S(1)}, bf16[128,2048]{1,0:T(8,128)(2,1)S(1)}, u32[]{:S(2)}, u32[]{:S(2)}) collective-permute-start(bf16[128,2048]{1,0:T(8,128)(2,1)S(1)} %get-tuple-element.60), channel_id=1, source_target_pairs={{0,4},{4,0},{8,12},{12,8},{16,20},{20,16},{24,28},{28,24},{1,5},{5... | collective-permute-start | bytes 1572872 | tf_op jit(solution)/shard_map/ppermute | solution.py:48
  428.6 109.9 %reduce-scatter.7.cloned.1.call-start = ((), (), s32[]{:S(2)}) async-start(), calls=%async_computation.13 | async-start | bytes 1310720 | tf_op jit(solution)/shard_map/reduce_scatter | solution.py:314
  433.2 149.9 %reduce-scatter.9.cloned.1.call-start = ((), (), s32[]{:S(2)}) async-start(), calls=%async_computation.14 | async-start | bytes 5242880 | tf_op jit(solution)/shard_map/reduce_scatter | solution.py:293
  433.7 205.0 %reduce-scatter.11.cloned.1.call-start = ((), (), s32[]{:S(2)}) async-start(), calls=%async_computation.15 | async-start | bytes 5242880 | tf_op jit(solution)/shard_map/reduce_scatter | solution.py:293
  443.5 14.5 %collective-permute-start.51 = (bf16[512,2048]{1,0:T(8,128)(2,1)}, bf16[512,2048]{1,0:T(8,128)(2,1)}, u32[]{:S(2)}, u32[]{:S(2)}) collective-permute-start(bf16[512,2048]{1,0:T(8,128)(2,1)} %convolution_convert_fusion.5), channel_id=1, source_target_pairs={{0,4},{4,0},{8,12},{12,8},{16,20},{20,16},{24,28},{28,24},{1,5},{5... | collective-permute-start | bytes 6291464 | tf_op jit(solution)/shard_map/ppermute | solution.py:48
  450.0 83.5 %collective-permute-start.40 = (bf16[128,2048]{1,0:T(8,128)(2,1)}, bf16[128,2048]{1,0:T(8,128)(2,1)}, u32[]{:S(2)}, u32[]{:S(2)}) collective-permute-start(bf16[128,2048]{1,0:T(8,128)(2,1)} %fusion.19), channel_id=1, source_target_pairs={{0,3},{1,0},{2,1},{3,2},{4,7},{5,4},{6,5},{7,6},{8,11},{9,8},{10,9... | collective-permute-start | bytes 1572872 | tf_op jit(solution)/shard_map/ppermute | solution.py:107
  459.7 15.0 %collective-permute-start.52 = (bf16[128,2048]{1,0:T(8,128)(2,1)S(1)}, bf16[128,2048]{1,0:T(8,128)(2,1)S(1)}, u32[]{:S(2)}, u32[]{:S(2)}) collective-permute-start(bf16[128,2048]{1,0:T(8,128)(2,1)S(1)} %add_convert_fusion.5), channel_id=1, source_target_pairs={{0,8},{4,12},{8,0},{12,4},{16,24},{20,28},{24,16},{28,20},{1,9},{5... | collective-permute-start | bytes 1572872 | tf_op jit(solution)/shard_map/ppermute | solution.py:48
  462.9 24.7 %collective-permute-start.53 = (bf16[128,2048]{1,0:T(8,128)(2,1)S(1)}, bf16[128,2048]{1,0:T(8,128)(2,1)S(1)}, u32[]{:S(2)}, u32[]{:S(2)}) collective-permute-start(bf16[128,2048]{1,0:T(8,128)(2,1)S(1)} %add_convert_fusion.4), channel_id=1, source_target_pairs={{0,16},{4,20},{8,24},{12,28},{16,0},{20,4},{24,8},{28,12},{1,17},{... | collective-permute-start | bytes 1572872 | tf_op jit(solution)/shard_map/ppermute | solution.py:48
  465.7 22.0 %collective-permute-start.54 = (bf16[128,2048]{1,0:T(8,128)(2,1)S(1)}, bf16[128,2048]{1,0:T(8,128)(2,1)S(1)}, u32[]{:S(2)}, u32[]{:S(2)}) collective-permute-start(bf16[128,2048]{1,0:T(8,128)(2,1)S(1)} %add_convert_fusion.3), channel_id=1, source_target_pairs={{0,24},{4,28},{8,16},{12,20},{16,8},{20,12},{24,0},{28,4},{1,25},{... | collective-permute-start | bytes 1572872 | tf_op jit(solution)/shard_map/ppermute | solution.py:48
  470.8 62.7 %collective-permute-start.41 = (bf16[128,2048]{1,0:T(8,128)(2,1)}, bf16[128,2048]{1,0:T(8,128)(2,1)}, u32[]{:S(2)}, u32[]{:S(2)}) collective-permute-start(bf16[128,2048]{1,0:T(8,128)(2,1)} %fusion.20), channel_id=1, source_target_pairs={{0,2},{1,3},{2,0},{3,1},{4,6},{5,7},{6,4},{7,5},{8,10},{9,11},{10,... | collective-permute-start | bytes 1572872 | tf_op jit(solution)/shard_map/ppermute | solution.py:107
  474.7 58.8 %collective-permute-start.42 = (bf16[128,2048]{1,0:T(8,128)(2,1)}, bf16[128,2048]{1,0:T(8,128)(2,1)}, u32[]{:S(2)}, u32[]{:S(2)}) collective-permute-start(bf16[128,2048]{1,0:T(8,128)(2,1)} %fusion.21), channel_id=1, source_target_pairs={{0,1},{1,2},{2,3},{3,0},{4,5},{5,6},{6,7},{7,4},{8,9},{9,10},{10,1... | collective-permute-start | bytes 1572872 | tf_op jit(solution)/shard_map/ppermute | solution.py:107
  500.5 29.3 %all-to-all-start.3 = ((f32[4,8,128]{2,1,0:T(8,128)}), f32[4,8,128]{2,1,0:T(8,128)S(1)}, u32[]{:S(2)}, u32[]{:S(2)}) async-start(f32[4,8,128]{2,1,0:T(8,128)} %bitcast.138), calls=%async_computation.3 | async-start | bytes 32768 | tf_op jit(solution)/shard_map/all_to_all | solution.py:382
  529.8 14.5 %all-to-all-start.4 = ((bf16[8,64,384]{2,1,0:T(8,128)(2,1)}), bf16[8,64,384]{2,1,0:T(8,128)(2,1)S(1)}, u32[]{:S(2)}, u32[]{:S(2)}) async-start(bf16[8,64,384]{2,1,0:T(8,128)(2,1)} %bitcast.173), calls=%async_computation.5 | async-start | bytes 786432 | tf_op jit(solution)/shard_map/all_to_all | solution.py:340
  583.0 58.5 %all-to-all-start.5 = ((bf16[8,64,1024]{2,1,0:T(8,128)(2,1)}), bf16[8,64,1024]{2,1,0:T(8,128)(2,1)S(1)}, u32[]{:S(2)}, u32[]{:S(2)}) async-start(bf16[8,64,1024]{2,1,0:T(8,128)(2,1)} %bitcast.166), calls=%async_computation.8 | async-start | bytes 2097152 | tf_op jit(solution)/shard_map/all_to_all | solution.py:348
  (58 other events, 517.8 us)
Sparse Core Ops, SparseCore 0:
  29.5 39.6 all-gather.8
  70.8 26.8 all-gather.4
  177.8 52.1 all-gather.6
  428.7 48.2 reduce-scatter.4
  479.1 49.6 reduce-scatter.6
  531.9 51.0 reduce-scatter.8
  586.0 52.7 reduce-scatter.10

commit v2 on v1

v2 whole, which is shorter than its diff:
```python
import math

import jax
import jax.numpy as jnp
from jax import lax
from jax.experimental import pallas as pl
from jax.experimental.pallas import tpu as pltpu
from jax.sharding import PartitionSpec as P

HEADS = 16
HD = 128
EPS = 1e-05
NEG = -1e30
TILE = 256
BOTH = ("ctx", "fsdp")
BF = jnp.bfloat16
F32 = jnp.float32


def dot(a, b, da, db):
    return lax.dot_general(
        a, b, (((da,), (db,)), ((), ())), preferred_element_type=F32
    )


def normalize(values):
    center = values - jnp.mean(values, -1, keepdims=True)
    inverse = lax.rsqrt(jnp.mean(center * center, -1, keepdims=True) + EPS)
    return center * inverse, inverse


def norm_backward(grad, scaled, inverse, gain):
    inner = grad * gain
    return inverse * (
        inner
        - jnp.mean(inner, -1, keepdims=True)
        - scaled * jnp.mean(inner * scaled, -1, keepdims=True)
    )


def gelu(values):
    return jax.nn.gelu(values, approximate=True)


def attend_kernel(q_ref, k_ref, v_ref, row_limit_ref, key_pos_ref, out_ref):
    scale = 1.0 / math.sqrt(HD)
    allowed = key_pos_ref[...] <= row_limit_ref[...]
    scores = jnp.where(allowed, dot(q_ref[...], k_ref[...], 1, 1) * scale, NEG)
    top = jnp.max(scores, -1, keepdims=True)
    expo = jnp.exp(scores - top)
    probs = expo * (1.0 / jnp.sum(expo, -1, keepdims=True))
    out_ref[...] = dot(probs.astype(BF), v_ref[...], 1, 0).astype(BF)


def attend(queries, keys, values, limit, pos):
    rows = min(TILE, queries.shape[0])
    count = queries.shape[1] // HD
    tile = pl.BlockSpec((rows, HD), lambda h, i: (i, h))
    whole = pl.BlockSpec(keys.shape, lambda h, i: (0, 0))
    return pl.pallas_call(
        attend_kernel,
        grid=(count, queries.shape[0] // rows),
        in_specs=[
            tile,
            whole,
            whole,
            pl.BlockSpec((rows, 1), lambda h, i: (i, 0)),
            pl.BlockSpec((1, keys.shape[0]), lambda h, i: (0, 0)),
        ],
        out_specs=tile,
        out_shape=jax.ShapeDtypeStruct(queries.shape, BF),
        cost_estimate=pl.CostEstimate(flops=0, bytes_accessed=0, transcendentals=0),
        name="attend",
    )(queries, keys, values, limit[:, None], pos[None, :])


def attend_back_kernel(
    q_ref, k_ref, v_ref, grad_ref, row_limit_ref, key_pos_ref, gq_ref, gk_ref, gv_ref
):
    scale = 1.0 / math.sqrt(HD)

    @pl.when((pl.program_id(0) == 0) & (pl.program_id(1) == 0))
    def _():
        gk_ref[...] = jnp.zeros_like(gk_ref)
        gv_ref[...] = jnp.zeros_like(gv_ref)

    q, k, v, grad = q_ref[...], k_ref[...], v_ref[...], grad_ref[...]
    allowed = key_pos_ref[...] <= row_limit_ref[...]
    scores = jnp.where(allowed, dot(k, q, 1, 1) * scale, NEG)
    top = jnp.max(scores, 0, keepdims=True)
    expo = jnp.exp(scores - top)
    probs = expo * (1.0 / jnp.sum(expo, 0, keepdims=True))
    gv_ref[...] += dot(probs.astype(BF), grad, 1, 0)
    grad_probs = dot(v, grad, 1, 1)
    delta = jnp.sum(probs * grad_probs, 0, keepdims=True)
    grad_scores = (probs * (grad_probs - delta)).astype(BF)
    gk_ref[...] += dot(grad_scores, q, 1, 0) * scale
    gq_ref[...] = (dot(grad_scores, k, 0, 0) * scale).astype(BF)


def attend_back(queries, keys, values, grads, limit, pos):
    rows = min(TILE, queries.shape[0])
    count = queries.shape[1] // HD
    tile = pl.BlockSpec((rows, HD), lambda h, i: (i, h))
    whole = pl.BlockSpec(keys.shape, lambda h, i: (0, 0))
    return pl.pallas_call(
        attend_back_kernel,
        grid=(count, queries.shape[0] // rows),
        in_specs=[
            tile,
            whole,
            whole,
            tile,
            pl.BlockSpec((1, rows), lambda h, i: (0, i)),
            pl.BlockSpec((keys.shape[0], 1), lambda h, i: (0, 0)),
        ],
        out_specs=[tile, whole, whole],
        out_shape=[
            jax.ShapeDtypeStruct(queries.shape, BF),
            jax.ShapeDtypeStruct(keys.shape, F32),
            jax.ShapeDtypeStruct(keys.shape, F32),
        ],
        cost_estimate=pl.CostEstimate(flops=0, bytes_accessed=0, transcendentals=0),
        name="attend_back",
    )(queries, keys, values, grads, limit[None, :], pos[:, None])


def stage(*values):
    return lax.optimization_barrier(values)


def dot_over_rows(lefts, rights):
    return dot(lefts[0], rights[0], 0, 0) + dot(lefts[1], rights[1], 0, 0)


def exchange(value, mask):
    count = lax.axis_size("ctx")
    return lax.ppermute(value, "ctx", [(i, i ^ mask) for i in range(count)])


def chip_groups():
    count = lax.axis_size("ctx")
    return [list(range(core, count, 2)) for core in range(2)]


def chip_devices():
    width = 2 * lax.axis_size("fsdp")
    total = lax.axis_size("ctx") * lax.axis_size("fsdp")
    return [list(range(at, at + width)) for at in range(0, total, width)]


def plane_direct(value):
    chips = lax.axis_size("ctx") // 2
    return [value] + [exchange(value, 2 * k) for k in range(1, chips)]


def both_cores(own):
    return own, exchange(own, 1)


def core_sum(lefts, weight, dim):
    other, early = stage(dot(lefts[1], weight, 1, dim).astype(BF), lefts[0])
    return stage(dot(early, weight, 1, dim), exchange(other, 1))


def plane_parts(halves):
    own, other = halves
    chips = lax.axis_size("ctx") // 2
    rows = own.shape[0] // chips
    parts = [
        own[k * rows : (k + 1) * rows] + other[k * rows : (k + 1) * rows].astype(F32)
        for k in range(chips)
    ]
    return [parts[0]] + [piece.astype(BF) for piece in parts[1:]]


def plane_sum(parts, fill=None):
    chips = lax.axis_size("ctx") // 2
    arrived = [exchange(parts[k], 2 * k) for k in range(1, chips - 1)]
    filled = fill(*parts) if fill else ()
    last = stage(parts[chips - 1], filled)[0]
    total = parts[0]
    for piece in arrived + [exchange(last, 2 * chips - 2)]:
        total = total + piece.astype(F32)
    return total, filled


def turned(value, by):
    depth = lax.axis_size("fsdp")
    return lax.ppermute(value, "fsdp", [(i, (i + by) % depth) for i in range(depth)])


def slot(s):
    depth = lax.axis_size("fsdp")
    return (lax.axis_index("fsdp") - s) % depth


def near_rows(value):
    depth = lax.axis_size("fsdp")
    return {s: turned(value, s) for s in range(1, depth) if s != depth // 2}


def far_rows(value, near):
    depth = lax.axis_size("fsdp")
    pieces = {0: value, **near, depth // 2: turned(value, depth // 2)}
    rows = jnp.zeros((depth,) + value.shape, value.dtype)
    for s, piece in pieces.items():
        rows = lax.dynamic_update_slice(rows, piece[None], (slot(s), 0, 0))
    return rows.reshape(depth * value.shape[0], value.shape[1])


def column_parts(own, other=None):
    depth = lax.axis_size("fsdp")
    rows = own.shape[0] // depth
    parts = []
    for s in range(depth):
        part = lax.dynamic_slice_in_dim(own, slot(s) * rows, rows, 0)
        if other is not None:
            theirs = lax.dynamic_slice_in_dim(other, slot(s) * rows, rows, 0)
            part = part + theirs.astype(F32)
        parts.append(part.astype(BF) if s else part.astype(F32))
    return parts


def column_near(parts):
    depth = len(parts)
    return [parts[0]] + [turned(parts[s], -s) for s in range(1, depth) if s != depth // 2]


def column_far(parts, near):
    middle = len(parts) // 2
    total = turned(parts[middle], -middle).astype(F32)
    for piece in near:
        total = total + piece.astype(F32)
    return total


def lay_out(vectors, width):
    row, column, laid, places = 0, 0, 0, []
    for v in vectors:
        n = v.shape[0]
        if column + n > width:
            row, column = row + 1, 0
        places.append((row, column, n))
        laid = laid + jnp.pad(v[None], ((row, 7 - row), (column, width - column - n)))
        column += -(-n // 128) * 128
    return laid, places


def body(
    hidden_in,
    out_cotangent,
    seq_lengths,
    first_gain,
    first_shift,
    qkv_weight,
    query_bias,
    value_bias,
    proj_weight,
    proj_bias,
    second_gain,
    second_shift,
    up_weight,
    up_bias,
    down_weight,
    down_bias,
):
    count, depth = lax.axis_size("ctx"), lax.axis_size("fsdp")
    chips = count // 2
    at, level = lax.axis_index("ctx"), lax.axis_index("fsdp")
    core, chip = at % 2, at // 2
    span, width = hidden_in.shape[1:]
    wrows = qkv_weight.shape[0]
    hidden = up_weight.shape[1]
    frows = down_weight.shape[0]
    share = HEADS // count
    qcols = share * HD
    wide_cols = qcols + HD
    total = span * count
    length = seq_lengths[0]
    positions = at * span + jnp.arange(span, dtype=jnp.int32)
    live = (positions < length)[:, None]

    small = [
        first_gain,
        first_shift,
        query_bias,
        value_bias,
        proj_bias,
        second_gain,
        second_shift,
        up_bias,
        down_bias,
    ]
    packed, places = lay_out(small, wide_cols)
    qpart = qkv_weight[:, :width].reshape(wrows, count, qcols).transpose(1, 0, 2)
    kvpart = qkv_weight[:, width:].reshape(wrows, 2, HD).transpose(1, 0, 2)
    kvpart = jnp.broadcast_to(kvpart[None], (chips, 2, wrows, HD)).reshape(count, wrows, HD)
    outgoing = jnp.concatenate(
        [
            jnp.concatenate([qpart, kvpart], 2),
            jnp.broadcast_to(packed[None], (count,) + packed.shape),
        ],
        1,
    )
    incoming = lax.all_to_all(outgoing, "ctx", 0, 0, tiled=True)
    incoming, hidden_own, upstream = stage(incoming, hidden_in[0], out_cotangent[0])

    attn_all = lax.all_gather(incoming, "fsdp", axis=0)
    row_pieces = plane_direct(hidden_own)
    row_halves = both_cores(jnp.concatenate(row_pieces, 0))
    down_pieces = plane_direct(stage(down_weight, row_pieces)[0])
    own_rows = hidden_own.astype(F32)
    upstream = jnp.where(live, upstream.astype(F32), 0.0)
    grad_mlp_own = upstream.astype(BF)
    attn_all, row_halves, grad_mlp_own, proj_own, up_own = stage(
        attn_all, row_halves, grad_mlp_own, proj_weight, up_weight
    )

    proj_local = lax.all_gather(proj_own, "fsdp", axis=0, tiled=True)
    mlp_rows = lax.all_gather(grad_mlp_own, "fsdp", axis=0, tiled=True)
    up_parts = (
        up_own.reshape(wrows, chips, 2 * depth, frows)
        .transpose(2, 0, 1, 3)
        .reshape(2 * depth, wrows, chips * frows)
    )
    up_parts = lax.all_to_all(
        up_parts, BOTH, 0, 0, tiled=True, axis_index_groups=chip_devices()
    ).reshape(2 * depth * wrows, chips * frows)
    attn_rows = attn_all.transpose(1, 0, 2, 3)
    qkv_local = attn_rows[:, :, :wrows].reshape(width, wide_cols)
    table = attn_rows[:, :, wrows:].reshape(count * depth, 8, wide_cols)
    vectors = [table[:, r, c : c + n].reshape(-1).astype(F32) for r, c, n in places]
    gain_one, shift_one, qbias, vbias, pbias, gain_two, shift_two, ubias, dbias = vectors
    qbias = lax.dynamic_slice(qbias, (at * qcols,), (qcols,))
    ubias = lax.dynamic_slice(
        ubias.reshape(chips, 2 * depth, frows), (0, core * depth + level, 0), (chips, 1, frows)
    ).reshape(-1)
    normed_one = [
        (normalize(half.astype(F32))[0] * gain_one + shift_one).astype(BF) for half in row_halves
    ]
    mixed = jnp.concatenate([dot(half, qkv_local, 1, 0) for half in normed_one], 0)
    queries = (mixed[:, :qcols] + qbias).astype(BF)
    mine = (mixed[:, qcols:] + jnp.where(core == 1, vbias, 0.0)).astype(BF)
    theirs = jnp.roll(exchange(mine, 1), total // 2, 0)
    keys = jnp.where(core == 0, mine, theirs)
    values = jnp.where(core == 0, theirs, mine)
    base = jnp.stack([at ^ (2 * k + j) for j in range(2) for k in range(chips)]) * span
    pos = (base[:, None] + jnp.arange(span, dtype=jnp.int32)[None]).reshape(total)
    limit = jnp.minimum(pos, length - 1)
    attended = attend(queries, keys, values, limit, pos)
    held = (pbias, gain_two, shift_two, ubias, dbias)
    attended, up_parts, held, proj_local, down_pieces = stage(
        attended, up_parts, held, proj_local, down_pieces
    )
    pbias, gain_two, shift_two, ubias, dbias = held

    attended_halves = attended[: total // 2], attended[total // 2 :]
    down_local = jnp.zeros((chips, frows, width), BF)
    for k, piece in enumerate(down_pieces):
        down_local = lax.dynamic_update_slice(down_local, piece[None], (chip ^ k, 0, 0))
    down_local = down_local.reshape(chips * frows, width)
    branch, _ = plane_sum(plane_parts(core_sum(attended_halves, proj_local, 0)))
    middle = own_rows + branch + pbias
    scaled_two, inverse_two = normalize(middle)
    normed_two_own = (scaled_two * gain_two + shift_two).astype(BF)
    normed_two_own, down_local = stage(normed_two_own, down_local)

    up_local = lax.all_gather(
        stage(up_parts, mlp_rows)[0], "ctx", axis=0, tiled=True, axis_index_groups=chip_groups()
    )

    near = near_rows(normed_two_own)
    near, normed_value = stage(near, normed_two_own)
    mlp_halves = both_cores(stage(mlp_rows, near)[0])
    grad_active = [dot(half, down_local, 1, 1) for half in mlp_halves]
    normed_rows = far_rows(normed_value, near)
    normed_rows, mlp_halves, grad_active = stage(normed_rows, mlp_halves, grad_active)

    normed_halves = both_cores(normed_rows)
    active, grad_before = [], []
    befores = stage(*[dot(half, up_local, 1, 0) for half in normed_halves])
    for before, grad_half in zip(befores, grad_active):
        before = before + ubias
        active_f, gelu_pull = jax.vjp(gelu, before)
        active.append(active_f.astype(BF))
        grad_before.append(gelu_pull(grad_half)[0].astype(BF))

    def chip_sum(term):
        return lax.psum_scatter(
            term, "ctx", scatter_dimension=0, tiled=True, axis_index_groups=chip_groups()
        )

    two_parts = column_parts(*core_sum(grad_before, up_local, 1))

    held = stage(normed_halves, grad_before, active, mlp_halves, two_parts)
    normed, grads, acts, mlps = held[:4]
    up_term = dot_over_rows(normed, grads).astype(BF)
    down_term = dot_over_rows(acts, mlps).astype(BF)
    ubias_term = jnp.sum(grads[0].astype(F32), 0) + jnp.sum(grads[1].astype(F32), 0)
    near, two_parts, up_term, down_term, ubias_term = stage(
        column_near(two_parts), two_parts, up_term, down_term, ubias_term
    )
    up_grad = chip_sum(up_term)
    out_own, out_other = core_sum(stage(acts, near)[0], down_local, 0)
    out_term = (out_own + out_other.astype(F32)).astype(BF)
    grad_two = column_far(two_parts, near)
    gain_two_term = jnp.sum(grad_two * scaled_two, 0)
    shift_two_term = jnp.sum(grad_two, 0)
    grad_middle = upstream + norm_backward(grad_two, scaled_two, inverse_two, gain_two)
    grad_branch_own = grad_middle.astype(BF)
    grad_branch_own, out_term, down_term = stage(grad_branch_own, out_term, down_term)

    branch_halves = both_cores(jnp.concatenate(plane_direct(grad_branch_own), 0))
    pbias_term = jnp.sum(grad_branch_own.astype(F32), 0)
    dbias_term = jnp.sum(grad_mlp_own.astype(F32), 0)
    out_sum = lax.psum_scatter(out_term, "fsdp", scatter_dimension=0, tiled=True)
    branch_halves, pbias_term, dbias_term, down_term, up_grad = stage(
        branch_halves, pbias_term, dbias_term, down_term, up_grad
    )

    grad_attended = jnp.concatenate(
        [dot(half, proj_local, 1, 1) for half in branch_halves], 0
    ).astype(BF)
    grad_queries, grad_keys, grad_values = attend_back(
        queries, keys, values, grad_attended, limit, pos
    )
    given = jnp.where(core == 0, grad_values, grad_keys).astype(BF)
    given = jnp.roll(exchange(given, 1), total // 2, 0).astype(F32)
    grad_kind = (jnp.where(core == 0, grad_keys, grad_values) + given).astype(BF)
    grad_mixed = jnp.concatenate([grad_queries, grad_kind], 1)
    up_grad = lax.all_to_all(
        up_grad.reshape(2 * depth, wrows, chips * frows),
        BOTH,
        0,
        0,
        tiled=True,
        axis_index_groups=chip_devices(),
    )
    grad_mixed, up_grad = stage(grad_mixed, up_grad)

    mixed_halves = grad_mixed[: total // 2], grad_mixed[total // 2 :]
    proj_term = dot_over_rows(attended_halves, branch_halves).astype(BF)
    one_sums = core_sum(mixed_halves, qkv_local, 1)
    one_sums, proj_term, out_sum = stage(one_sums, proj_term, out_sum)
    proj_grad = lax.psum_scatter(proj_term, "fsdp", scatter_dimension=0, tiled=True)
    down_grad = chip_sum(stage(down_term, proj_term)[0])
    one_parts = plane_parts(one_sums)

    def qkv_parts(*gate):
        halves = stage(mixed_halves, gate)[0]
        term = dot_over_rows(normed_one, halves).astype(BF)
        term = term.reshape(count, depth, wrows, wide_cols).transpose(1, 0, 2, 3)
        return column_parts(term.reshape(depth * count * wrows, wide_cols))

    grad_one, qkv_term = plane_sum(one_parts, qkv_parts)
    qkv_near = column_near(qkv_term)
    scaled_one, inverse_one = normalize(own_rows)
    gain_one_term = jnp.sum(grad_one * scaled_one, 0)
    shift_one_term = jnp.sum(grad_one, 0)
    held = (grad_one, qkv_term, qkv_near, up_grad)
    gain_one_term, shift_one_term, held = stage(gain_one_term, shift_one_term, held)
    grad_one, qkv_term, qkv_near, up_grad = held

    result = middle + out_sum.astype(F32) + dbias
    layer_out = jnp.where(live, result, 0.0).astype(BF)
    qkv_grad = column_far(qkv_term, qkv_near).astype(BF)
    qkv_grad = qkv_grad.reshape(count, wrows, wide_cols)
    input_grad = grad_middle + norm_backward(grad_one, scaled_one, inverse_one, gain_one)
    up_grad = (
        up_grad.reshape(2 * depth, wrows, chips, frows)
        .transpose(1, 2, 0, 3)
        .reshape(wrows, hidden)
        .astype(F32)
    )
    qkv_grad = lax.all_to_all(qkv_grad, "ctx", 0, 0, tiled=True).transpose(1, 0, 2).astype(F32)
    kinds = jnp.sum(qkv_grad[:, :, qcols:].reshape(wrows, chips, 2 * HD), 1)
    qkv_grad = jnp.concatenate([qkv_grad[:, :, :qcols].reshape(wrows, width), kinds], 1)
    down_grad = down_grad.astype(F32)
    proj_grad = proj_grad.astype(F32)

    mixed_term = jnp.sum(grad_mixed.astype(F32), 0)
    vbias_term = jnp.where(core == 1, mixed_term[qcols:], 0.0).reshape(count * depth, -1)
    vbias_term = jnp.pad(vbias_term, ((0, 0), (0, wrows - vbias_term.shape[1]))).reshape(-1)
    ubias_term = ubias_term.reshape(chips, 1, frows)
    ubias_term = jnp.where(jnp.arange(2)[None, :, None] == core, ubias_term, 0.0)
    terms = [pbias_term, gain_two_term, shift_two_term, dbias_term, vbias_term]
    early = jnp.stack(terms + [jnp.zeros_like(vbias_term)] * 3)
    early = early.reshape(8, count, -1)
    ub = jnp.pad(ubias_term.reshape(1, count, frows), ((0, 7), (0, 0), (0, 0)))
    early, ub = early.transpose(1, 0, 2), ub.transpose(1, 0, 2)
    late = jnp.stack([gain_one_term, shift_one_term]).reshape(2, count, -1).transpose(1, 0, 2)
    late = jnp.pad(late, ((0, 0), (5, 1), (0, 0)))
    block = late.shape[2]
    first = lax.all_to_all(
        jnp.concatenate([early + late, ub], 2), "ctx", 0, 0, tiled=True
    )
    first = jnp.sum(first, 0)
    ubias_grad = first[0, block:]
    second = first[:, :block] + jnp.pad(mixed_term[None, :qcols], ((7, 0), (0, 0)))
    second = second.reshape(8, depth, wrows).transpose(1, 0, 2)
    second = jnp.sum(lax.all_to_all(second, "fsdp", 0, 0, tiled=True), 0)
    wide_grads = [second[i] for i in (5, 6, 0, 1, 2, 3)]
    vbias_grad = second[4, : value_bias.shape[0]]
    qbias_grad = second[7]
    return (
        layer_out[None],
        input_grad[None],
        wide_grads[0],
        wide_grads[1],
        qkv_grad,
        qbias_grad,
        vbias_grad,
        proj_grad,
        wide_grads[2],
        wide_grads[3],
        wide_grads[4],
        up_grad,
        ubias_grad,
        down_grad,
        wide_grads[5],
    )


def solution(mesh):
    rows = P("fsdp", "ctx", None)
    vector = P(BOTH)
    matrix = P(BOTH, None)
    return jax.shard_map(
        body,
        mesh=mesh,
        in_specs=(
            rows, rows, P("fsdp"), vector, vector, matrix, vector, vector, matrix,
            vector, vector, vector, matrix, vector, matrix, vector,
        ),
        out_specs=(
            rows, rows, vector, vector, matrix, vector, vector, matrix, vector,
            vector, vector, matrix, vector, matrix, vector,
        ),
        check_vma=False,
    )
```

time: 662 us -> 547 us (0.83)
  waiting for transfers between devices: 335 us -> 214 us
  Pallas kernels: 0 us -> 24.1 us
  matrix products: 118 us -> 94.4 us
  starting transfers between devices: 78.4 us -> 55 us
  other arithmetic: 45.4 us -> 62.9 us
  local copies, waits for them, and re-layouts: 47 us -> 55.6 us
    reduce_scatter x2, waiting for transfers between devices: 83.7 us -> 0.01 us  [chip_sum(): lax.psum_scatter(term, 'ctx', scatter_dimension=0, tiled=True, axis_index...]
    ppermute x12 -> x0, waiting for transfers between devices: 57 us -> none  [the longest x3 24.7 us: column_chain(): lax.ppermute(downward[-1], 'fsdp', [(i, i - 1) for i in range(1, depth -...]
    ppermute x37 -> x25, waiting for transfers between devices: 105 us -> 61.1 us  [exchange(): return lax.ppermute(value, 'ctx', [(i, i ^ mask) for i in range(count)])]
    all_to_all x1, waiting for transfers between devices: 0.01 us -> 27.5 us  [body(): lax.all_to_all(up_grad.reshape(2 * depth, wrows, chips * frows), BOTH, 0,...]
    all_to_all x2, waiting for transfers between devices: 30.8 us -> 5.36 us  [the longest x1 4.49 us: body(): lax.all_to_all(jnp.concatenate([early + late, ub], 2), 'ctx', 0, 0, tiled...]
    pallas_call x0 -> x2, Pallas kernels: none -> 24.1 us  [the longest x1 15.3 us: attend_back(): pl.pallas_call(attend_back_kernel, grid=(count, queries.shape[0] // rows)...]
    ppermute x12 -> x0, starting transfers between devices: 23.8 us -> none  [the longest x3 11.1 us: column_scatter(): lax.ppermute(rising.astype(BF), 'fsdp', [(i, i + 1) for i in range(min(s,...]
    all_gather x1 -> x2, waiting for transfers between devices: 0.01 us -> 23.4 us  [the longest x1 23.4 us: body(): mlp_rows = lax.all_gather(grad_mlp_own, 'fsdp', axis=0, tiled=True)]
  transfers between devices with their start and end apart: 67 -> 47, of which waited for: 30 -> 20; matrix products, arithmetic and copies ran while one was open for 23% -> 34% of each run, Pallas kernels for 0% -> 4%
where the time goes in v2:
time: 547 us; the launch traced here: 537 us
  waiting for transfers between devices  214 us (39%)
  matrix products  94.4 us (17%)
  other arithmetic  62.9 us (11%)
  local copies, waits for them, and re-layouts  55.6 us (10%)
  starting transfers between devices  55 us (10%)
  Pallas kernels  24.1 us (4%)
  between operations  16.5 us (3%)
  blocking collectives  13.9 us (3%)
    dot_general x24, matrix products, dot(): lax.dot_general(a, b, (((da,), (db,)), ((), ())), preferred_element_type=...  94.4 us
    ppermute x25, waiting for transfers between devices, exchange(): return lax.ppermute(value, 'ctx', [(i, i ^ mask) for i in range(count)])  61.1 us
    ppermute x9, waiting for transfers between devices, turned(): lax.ppermute(value, 'fsdp', [(i, (i + by) % depth) for i in range(depth)])  59.2 us
    all_to_all x1, waiting for transfers between devices, body(): lax.all_to_all(up_grad.reshape(2 * depth, wrows, chips * frows), BOTH, 0,...  27.5 us
    all_gather x1, waiting for transfers between devices, body(): mlp_rows = lax.all_gather(grad_mlp_own, 'fsdp', axis=0, tiled=True)  23.4 us
    ppermute x25, starting transfers between devices, exchange(): return lax.ppermute(value, 'ctx', [(i, i ^ mask) for i in range(count)])  19.2 us
    ppermute x9, starting transfers between devices, turned(): lax.ppermute(value, 'fsdp', [(i, (i + by) % depth) for i in range(depth)])  15.8 us
    pallas_call x1, Pallas kernels, attend_back(): pl.pallas_call(attend_back_kernel, grid=(count, queries.shape[0] // rows)...  15.3 us
  transfers between devices with their start and end apart: 47, of which 20 were waited for; matrix products, arithmetic and copies ran while one was open for 34% of the time, Pallas kernels for 4%

profile of v2, /device:TPU:0, one launch (start us, length us, event | category | flops | bytes accessed | tf_op | source)
XLA Modules:
  0.0 536.9 jit_solution(2347003960294732183)
XLA Ops:
  10.8 13.9 %all_to_all.30 = bf16[8,72,384]{2,1,0:T(8,128)(2,1)} all-to-all(bf16[8,72,384]{2,1,0:T(8,128)(2,1)S(1)} %copy.93), channel_id=1, replica_groups=mesh['ctx'=8,'fsdp'=4] {'ctx'}, dimensions={0} | all-to-all | bytes 884736 | tf_op jit(solution)/shard_map/all_to_all | solution.py:306
  29.1 10.4 %collective-permute-done = bf16[128,2048]{1,0:T(8,128)(2,1)S(1)} collective-permute-done((bf16[128,2048]{1,0:T(8,128)(2,1)S(1)}, bf16[128,2048]{1,0:T(8,128)(2,1)S(1)}, u32[]{:S(2)}, u32[]{:S(2)}) %collective-permute-start) | collective-permute-done | bytes 524320 | tf_op jit(solution)/shard_map/ppermute | solution.py:138
  40.4 9.6 %collective-permute-done.1 = bf16[128,2048]{1,0:T(8,128)(2,1)S(1)} collective-permute-done((bf16[128,2048]{1,0:T(8,128)(2,1)S(1)}, bf16[128,2048]{1,0:T(8,128)(2,1)S(1)}, u32[]{:S(2)}, u32[]{:S(2)}) %collective-permute-start.1) | collective-permute-done | bytes 524320 | tf_op jit(solution)/shard_map/ppermute | solution.py:138
  58.2 10.7 %all-gather.12.cloned.1.call-done = bf16[32,72,384]{2,1,0:T(8,128)(2,1)} async-done(((bf16[8,72,384]{2,1,0:T(8,128)(2,1)}), bf16[32,72,384]{2,1,0:T(8,128)(2,1)}) %all-gather.12.cloned.1.call-update) | async-done | bytes 1769488 | tf_op jit(solution)/shard_map/all_gather | solution.py:309
  82.5 3.6 all-to-all-start.1
  86.2 3.8 fusion.65
  99.3 8.8 %attend.1 = bf16[1024,256]{1,0:T(8,128)(2,1)} custom-call(bf16[1024,256]{1,0:T(8,128)(2,1)} %fusion.42.q_ref, bf16[1024,128]{1,0:T(8,128)(2,1)} %get-tuple-element.257.k_ref, bf16[1024,128]{1,0:T(8,128)(2,1)} %get-tuple-element.256.v_ref, s32[1024,1]{1,0:T(8,128)} %broadcast_minimum_fusion.row_limit_ref, s32[1,1024]{1,0:T(1,128)} %bitcast.187), custom_call_target="tpu_custom_call" | custom-call | tf_op jit(solution)/shard_map/attend/pallas_call | solution.py:60
  108.1 14.5 %all-to-all-done.1 = bf16[8,64,1024]{2,1,0:T(8,128)(2,1)S(1)} async-done(((bf16[8,64,1024]{2,1,0:T(8,128)(2,1)}), bf16[8,64,1024]{2,1,0:T(8,128)(2,1)S(1)}, u32[]{:S(2)}, u32[]{:S(2)}) %all-to-all-start.1) | async-done | bytes 1048608 | tf_op jit(solution)/shard_map/all_to_all | solution.py:327
  122.6 3.7 convolution_convert_fusion.2
  147.3 23.4 %all-gather.8.cloned.1.call-done = bf16[512,2048]{1,0:T(8,128)(2,1)} async-done(((bf16[128,2048]{1,0:T(8,128)(2,1)}), bf16[512,2048]{1,0:T(8,128)(2,1)}) %all-gather.8.cloned.1.call-update) | async-done | bytes 2097168 | tf_op jit(solution)/shard_map/all_gather | solution.py:321
  170.8 3.0 fusion.69
  177.2 12.6 %collective-permute-done.13 = bf16[128,2048]{1,0:T(8,128)(2,1)} collective-permute-done((bf16[128,2048]{1,0:T(8,128)(2,1)}, bf16[128,2048]{1,0:T(8,128)(2,1)}, u32[]{:S(2)}, u32[]{:S(2)}) %collective-permute-start.13) | collective-permute-done | bytes 524320 | tf_op jit(solution)/shard_map/ppermute | solution.py:190
  189.8 11.1 %collective-permute-done.12 = bf16[128,2048]{1,0:T(8,128)(2,1)} collective-permute-done((bf16[128,2048]{1,0:T(8,128)(2,1)}, bf16[128,2048]{1,0:T(8,128)(2,1)}, u32[]{:S(2)}, u32[]{:S(2)}) %collective-permute-start.12) | collective-permute-done | bytes 524320 | tf_op jit(solution)/shard_map/ppermute | solution.py:190
  205.3 5.9 %fusion.75 = f32[512,1024]{1,0:T(8,128)} fusion(bf16[512,2048]{1,0:T(8,128)(2,1)S(1)} %copy-done.57, bf16[1024,2048]{1,0:T(8,128)(2,1)} %bitcast.35), kind=kOutput, calls=%fused_computation.204 | convolution fusion | flops 2147483648 | bytes 8388608 | tf_op jit(solution)/shard_map/dot_general | solution.py:21
  215.0 11.0 %collective-permute-done.14 = bf16[128,2048]{1,0:T(8,128)(2,1)S(1)} collective-permute-done((bf16[128,2048]{1,0:T(8,128)(2,1)}, bf16[128,2048]{1,0:T(8,128)(2,1)S(1)}, u32[]{:S(2)}, u32[]{:S(2)}) %collective-permute-start.14) | collective-permute-done | bytes 524320 | tf_op jit(solution)/shard_map/ppermute | solution.py:190
  226.8 6.7 %fusion.76 = f32[512,1024]{1,0:T(8,128)} fusion(bf16[512,2048]{1,0:T(8,128)(2,1)S(1)} %collective-permute-done.15, bf16[1024,2048]{1,0:T(8,128)(2,1)} %bitcast.35), kind=kOutput, calls=%fused_computation.205 | convolution fusion | flops 2147483648 | bytes 8388608 | tf_op jit(solution)/shard_map/dot_general | solution.py:21
  233.5 5.3 fusion.77
  238.9 4.1 fusion.78
  243.0 4.6 multiply_convert_fusion
  247.6 3.7 convolution_convert_fusion.1
  251.9 4.9 fusion.79
  256.8 3.6 add_convert_fusion.7
  260.4 4.0 collective-permute-start.18
  264.7 4.0 fusion.80
  269.3 6.2 %add_convert_fusion.1 = bf16[2048,1024]{1,0:T(8,128)(2,1)} fusion(f32[2048,1024]{1,0:T(8,128)S(1)} %fusion.80, bf16[512,2048]{1,0:T(8,128)(2,1)} %bitcast.40, bf16[512,1024]{1,0:T(8,128)(2,1)S(1)} %copy-done.9), kind=kOutput, calls=%fused_computation.1 | convolution fusion | flops 2151677952 | bytes 15728640 | tf_op jit(solution)/shard_map/dot_general | solution.py:21
  275.5 4.5 fusion.81
  280.0 4.7 add_convert_fusion
  286.2 5.0 convolution_convert_fusion
  293.6 4.5 fusion.82
  298.2 19.6 %collective-permute-done.20 = bf16[128,2048]{1,0:T(8,128)(2,1)S(1)} collective-permute-done((bf16[128,2048]{1,0:T(8,128)(2,1)S(1)}, bf16[128,2048]{1,0:T(8,128)(2,1)S(1)}, u32[]{:S(2)}, u32[]{:S(2)}) %collective-permute-start.20) | collective-permute-done | bytes 524320 | tf_op jit(solution)/shard_map/ppermute | solution.py:190
  329.4 19.4 %collective-permute-done.22 = bf16[128,2048]{1,0:T(8,128)(2,1)S(1)} collective-permute-done((bf16[128,2048]{1,0:T(8,128)(2,1)}, bf16[128,2048]{1,0:T(8,128)(2,1)S(1)}, u32[]{:S(2)}, u32[]{:S(2)}) %collective-permute-start.22) | collective-permute-done | bytes 524320 | tf_op jit(solution)/shard_map/ppermute | solution.py:138
  350.5 10.0 %collective-permute-done.24 = bf16[128,2048]{1,0:T(8,128)(2,1)S(1)} collective-permute-done((bf16[128,2048]{1,0:T(8,128)(2,1)}, bf16[128,2048]{1,0:T(8,128)(2,1)S(1)}, u32[]{:S(2)}, u32[]{:S(2)}) %collective-permute-start.24) | collective-permute-done | bytes 524320 | tf_op jit(solution)/shard_map/ppermute | solution.py:138
  365.8 4.3 all-to-all-start.2
  376.4 15.3 %attend_back.1 = (bf16[1024,256]{1,0:T(8,128)(2,1)}, f32[1024,128]{1,0:T(8,128)}, f32[1024,128]{1,0:T(8,128)}) custom-call(bf16[1024,256]{1,0:T(8,128)(2,1)} %fusion.42.q_ref, bf16[1024,128]{1,0:T(8,128)(2,1)} %get-tuple-element.257.k_ref, bf16[1024,128]{1,0:T(8,128)(2,1)} %get-tuple-element.256.v_ref, bf16[1024,256]{1,0:T(8,128)(2,1)} %pad_maximum_fusion.3.grad_ref, ...), custom_call_target="tpu_custom_call" | custom-call | tf_op jit(solution)/shard_map/attend_back/pallas_call | solution.py:106
  395.7 27.5 %all-to-all-done.2 = bf16[8,64,1024]{2,1,0:T(8,128)(2,1)} async-done(((bf16[8,64,1024]{2,1,0:T(8,128)(2,1)}), bf16[8,64,1024]{2,1,0:T(8,128)(2,1)}, u32[]{:S(2)}, u32[]{:S(2)}) %all-to-all-start.2) | async-done | bytes 1048608 | tf_op jit(solution)/shard_map/all_to_all | solution.py:432
  425.2 3.7 convolution_convert_fusion.3
  431.4 3.3 fusion.12
  434.7 3.2 fusion.83
  440.4 5.0 add_convert_fusion.5
  447.3 3.2 fusion.63
  457.0 4.1 collective-permute-start.31
  463.1 9.0 %collective-permute-done.30 = bf16[128,2048]{1,0:T(8,128)(2,1)S(1)} collective-permute-done((bf16[128,2048]{1,0:T(8,128)(2,1)}, bf16[128,2048]{1,0:T(8,128)(2,1)S(1)}, u32[]{:S(2)}, u32[]{:S(2)}) %collective-permute-start.30) | collective-permute-done | bytes 524320 | tf_op jit(solution)/shard_map/ppermute | solution.py:138
  474.2 3.6 collective-permute-done.31
  478.6 3.7 all-to-all-start.3
  485.0 4.5 all-to-all-done.3
  490.3 3.7 all-to-all-start.4
  506.8 3.8 all-to-all-start.5
  511.7 11.8 %all-to-all-done.5 = bf16[8,64,384]{2,1,0:T(8,128)(2,1)S(1)} async-done(((bf16[8,64,384]{2,1,0:T(8,128)(2,1)}), bf16[8,64,384]{2,1,0:T(8,128)(2,1)S(1)}, u32[]{:S(2)}, u32[]{:S(2)}) %all-to-all-start.5) | async-done | bytes 393248 | tf_op jit(solution)/shard_map/all_to_all | solution.py:476
  (354 shorter events, 149.9 us)
Async XLA Ops:
  7.2 61.7 %all-gather.12.cloned.1.call-start = ((), (), s32[]{:S(2)}) async-start(), calls=%async_computation.17 | async-start | bytes 2211840 | tf_op jit(solution)/shard_map/all_gather | solution.py:309
  24.7 14.8 %collective-permute-start = (bf16[128,2048]{1,0:T(8,128)(2,1)S(1)}, bf16[128,2048]{1,0:T(8,128)(2,1)S(1)}, u32[]{:S(2)}, u32[]{:S(2)}) collective-permute-start(bf16[128,2048]{1,0:T(8,128)(2,1)S(1)} %bitcast.152), channel_id=1, source_target_pairs={{0,8},{4,12},{8,0},{12,4},{16,24},{20,28},{24,16},{28,20},{1,9},{5... | collective-permute-start | bytes 1572872 | tf_op jit(solution)/shard_map/ppermute | solution.py:138
  25.3 24.7 %collective-permute-start.1 = (bf16[128,2048]{1,0:T(8,128)(2,1)S(1)}, bf16[128,2048]{1,0:T(8,128)(2,1)S(1)}, u32[]{:S(2)}, u32[]{:S(2)}) collective-permute-start(bf16[128,2048]{1,0:T(8,128)(2,1)S(1)} %bitcast.153), channel_id=1, source_target_pairs={{0,16},{4,20},{8,24},{12,28},{16,0},{20,4},{24,8},{28,12},{1,17},{... | collective-permute-start | bytes 1572872 | tf_op jit(solution)/shard_map/ppermute | solution.py:138
  25.8 25.0 %collective-permute-start.2 = (bf16[128,2048]{1,0:T(8,128)(2,1)S(1)}, bf16[128,2048]{1,0:T(8,128)(2,1)S(1)}, u32[]{:S(2)}, u32[]{:S(2)}) collective-permute-start(bf16[128,2048]{1,0:T(8,128)(2,1)S(1)} %bitcast.154), channel_id=1, source_target_pairs={{0,24},{4,28},{8,16},{12,20},{16,8},{20,12},{24,0},{28,4},{1,25},{... | collective-permute-start | bytes 1572872 | tf_op jit(solution)/shard_map/ppermute | solution.py:138
  29.1 79.0 %all-gather.6.cloned.1.call-start = ((), (), s32[]{:S(2)}) async-start(), calls=%async_computation.10 | async-start | bytes 1310720 | tf_op jit(solution)/shard_map/all_gather | solution.py:320
  51.7 6.5 %collective-permute-start.3 = (bf16[512,2048]{1,0:T(8,128)(2,1)}, bf16[512,2048]{1,0:T(8,128)(2,1)}, u32[]{:S(2)}, u32[]{:S(2)}) collective-permute-start(bf16[512,2048]{1,0:T(8,128)(2,1)} %constant_dynamic-update-slice_fusion), channel_id=1, source_target_pairs={{0,4},{4,0},{8,12},{12,8},{16,20},{20,16},{24,28},{28,24},{1,5},{5... | collective-permute-start | bytes 6291464 | tf_op jit(solution)/shard_map/ppermute | solution.py:138
  54.7 53.4 %collective-permute-start.7 = (bf16[256,2048]{1,0:T(8,128)(2,1)}, bf16[256,2048]{1,0:T(8,128)(2,1)}, u32[]{:S(2)}, u32[]{:S(2)}) collective-permute-start(bf16[256,2048]{1,0:T(8,128)(2,1)} %param.30), channel_id=1, source_target_pairs={{0,24},{4,28},{8,16},{12,20},{16,8},{20,12},{24,0},{28,4},{1,25},{... | collective-permute-start | bytes 3145736 | tf_op jit(solution)/shard_map/ppermute | solution.py:138
  55.0 53.1 %collective-permute-start.6 = (bf16[256,2048]{1,0:T(8,128)(2,1)}, bf16[256,2048]{1,0:T(8,128)(2,1)}, u32[]{:S(2)}, u32[]{:S(2)}) collective-permute-start(bf16[256,2048]{1,0:T(8,128)(2,1)} %param.30), channel_id=1, source_target_pairs={{0,16},{4,20},{8,24},{12,28},{16,0},{20,4},{24,8},{28,12},{1,17},{... | collective-permute-start | bytes 3145736 | tf_op jit(solution)/shard_map/ppermute | solution.py:138
  57.3 50.8 %collective-permute-start.5 = (bf16[256,2048]{1,0:T(8,128)(2,1)}, bf16[256,2048]{1,0:T(8,128)(2,1)}, u32[]{:S(2)}, u32[]{:S(2)}) collective-permute-start(bf16[256,2048]{1,0:T(8,128)(2,1)} %param.30), channel_id=1, source_target_pairs={{0,8},{4,12},{8,0},{12,4},{16,24},{20,28},{24,16},{28,20},{1,9},{5... | collective-permute-start | bytes 3145736 | tf_op jit(solution)/shard_map/ppermute | solution.py:138
  82.5 40.0 %all-to-all-start.1 = ((bf16[8,64,1024]{2,1,0:T(8,128)(2,1)}), bf16[8,64,1024]{2,1,0:T(8,128)(2,1)S(1)}, u32[]{:S(2)}, u32[]{:S(2)}) async-start(bf16[8,64,1024]{2,1,0:T(8,128)(2,1)} %reshape.417), calls=%async_computation.1 | async-start | bytes 2097152 | tf_op jit(solution)/shard_map/all_to_all | solution.py:327
  86.1 84.6 %all-gather.8.cloned.1.call-start = ((), (), s32[]{:S(2)}) async-start(), calls=%async_computation.11 | async-start | bytes 2621440 | tf_op jit(solution)/shard_map/all_gather | solution.py:321
  94.4 2.9 collective-permute-start.4
  126.3 10.2 %collective-permute-start.8 = (bf16[512,2048]{1,0:T(8,128)(2,1)}, bf16[512,2048]{1,0:T(8,128)(2,1)}, u32[]{:S(2)}, u32[]{:S(2)}) collective-permute-start(bf16[512,2048]{1,0:T(8,128)(2,1)} %convolution_convert_fusion.2), channel_id=1, source_target_pairs={{0,4},{4,0},{8,12},{12,8},{16,20},{20,16},{24,28},{28,24},{1,5},{5... | collective-permute-start | bytes 6291464 | tf_op jit(solution)/shard_map/ppermute | solution.py:138
  126.4 107.1 %all-gather.10.cloned.1.call-start = ((), (), s32[]{:S(2)}) async-start(), calls=%async_computation.12 | async-start | bytes 5242880 | tf_op jit(solution)/shard_map/all_gather | solution.py:369
  126.9 43.9 %copy-start.37 = (f32[128]{0:T(128)}, f32[128]{0:T(128)S(1)}, u32[]{:S(2)}) copy-start(f32[128]{0:T(128)S(1)} %broadcast_multiply_fusion.4) | copy-start | bytes 1540
  139.1 31.7 %collective-permute-start.11 = (bf16[128,2048]{1,0:T(8,128)(2,1)}, bf16[128,2048]{1,0:T(8,128)(2,1)}, u32[]{:S(2)}, u32[]{:S(2)}) collective-permute-start(bf16[128,2048]{1,0:T(8,128)(2,1)} %get-tuple-element.243), channel_id=1, source_target_pairs={{0,24},{4,28},{8,16},{12,20},{16,8},{20,12},{24,0},{28,4},{1,25},{... | collective-permute-start | bytes 1572872 | tf_op jit(solution)/shard_map/ppermute | solution.py:138
  141.6 29.2 %collective-permute-start.9 = (bf16[128,2048]{1,0:T(8,128)(2,1)S(1)}, bf16[128,2048]{1,0:T(8,128)(2,1)}, u32[]{:S(2)}, u32[]{:S(2)}) collective-permute-start(bf16[128,2048]{1,0:T(8,128)(2,1)S(1)} %get-tuple-element.242), channel_id=1, source_target_pairs={{0,8},{4,12},{8,0},{12,4},{16,24},{20,28},{24,16},{28,20},{1,9},{5... | collective-permute-start | bytes 1572872 | tf_op jit(solution)/shard_map/ppermute | solution.py:138
  142.2 28.6 %collective-permute-start.10 = (bf16[128,2048]{1,0:T(8,128)(2,1)S(1)}, bf16[128,2048]{1,0:T(8,128)(2,1)}, u32[]{:S(2)}, u32[]{:S(2)}) collective-permute-start(bf16[128,2048]{1,0:T(8,128)(2,1)S(1)} %get-tuple-element.244), channel_id=1, source_target_pairs={{0,16},{4,20},{8,24},{12,28},{16,0},{20,4},{24,8},{28,12},{1,17},{... | collective-permute-start | bytes 1572872 | tf_op jit(solution)/shard_map/ppermute | solution.py:138
  170.7 195.1 %reduce-scatter.5.cloned.1.call-start = ((), (), s32[]{:S(2)}) async-start(), calls=%async_computation.13 | async-start | bytes 5242880 | tf_op jit(solution)/shard_map/reduce_scatter | solution.py:390
  175.2 14.6 %collective-permute-start.13 = (bf16[128,2048]{1,0:T(8,128)(2,1)}, bf16[128,2048]{1,0:T(8,128)(2,1)}, u32[]{:S(2)}, u32[]{:S(2)}) collective-permute-start(bf16[128,2048]{1,0:T(8,128)(2,1)} %add_convert_fusion.10), channel_id=1, source_target_pairs={{0,3},{1,0},{2,1},{3,2},{4,7},{5,4},{6,5},{7,6},{8,11},{9,8},{10,9... | collective-permute-start | bytes 1572872 | tf_op jit(solution)/shard_map/ppermute | solution.py:190
  176.3 24.6 %collective-permute-start.12 = (bf16[128,2048]{1,0:T(8,128)(2,1)}, bf16[128,2048]{1,0:T(8,128)(2,1)}, u32[]{:S(2)}, u32[]{:S(2)}) collective-permute-start(bf16[128,2048]{1,0:T(8,128)(2,1)} %add_convert_fusion.10), channel_id=1, source_target_pairs={{0,1},{1,2},{2,3},{3,0},{4,5},{5,6},{6,7},{7,4},{8,9},{9,10},{10,1... | collective-permute-start | bytes 1572872 | tf_op jit(solution)/shard_map/ppermute | solution.py:190
  200.9 25.1 %collective-permute-start.14 = (bf16[128,2048]{1,0:T(8,128)(2,1)}, bf16[128,2048]{1,0:T(8,128)(2,1)S(1)}, u32[]{:S(2)}, u32[]{:S(2)}) collective-permute-start(bf16[128,2048]{1,0:T(8,128)(2,1)} %add_convert_fusion.10), channel_id=1, source_target_pairs={{0,2},{1,3},{2,0},{3,1},{4,6},{5,7},{6,4},{7,5},{8,10},{9,11},{10,... | collective-permute-start | bytes 1572872 | tf_op jit(solution)/shard_map/ppermute | solution.py:190
  201.9 25.0 %collective-permute-start.15 = (bf16[512,2048]{1,0:T(8,128)(2,1)}, bf16[512,2048]{1,0:T(8,128)(2,1)S(1)}, u32[]{:S(2)}, u32[]{:S(2)}) collective-permute-start(bf16[512,2048]{1,0:T(8,128)(2,1)} %all-gather.8.cloned.1.call-done), channel_id=1, source_target_pairs={{0,4},{4,0},{8,12},{12,8},{16,20},{20,16},{24,28},{28,24},{1,5},{5... | collective-permute-start | bytes 6291464 | tf_op jit(solution)/shard_map/ppermute | solution.py:138
  233.5 5.3 collective-permute-start.16
  251.4 5.4 %collective-permute-start.17 = (bf16[512,2048]{1,0:T(8,128)(2,1)}, bf16[512,2048]{1,0:T(8,128)(2,1)}, u32[]{:S(2)}, u32[]{:S(2)}) collective-permute-start(bf16[512,2048]{1,0:T(8,128)(2,1)} %convolution_convert_fusion.1), channel_id=1, source_target_pairs={{0,4},{4,0},{8,12},{12,8},{16,20},{20,16},{24,28},{28,24},{1,5},{5... | collective-permute-start | bytes 6291464 | tf_op jit(solution)/shard_map/ppermute | solution.py:138
  260.4 24.3 %collective-permute-start.19 = (bf16[128,2048]{1,0:T(8,128)(2,1)}, bf16[128,2048]{1,0:T(8,128)(2,1)}, u32[]{:S(2)}, u32[]{:S(2)}) collective-permute-start(bf16[128,2048]{1,0:T(8,128)(2,1)} %get-tuple-element.239), channel_id=1, source_target_pairs={{0,1},{1,2},{2,3},{3,0},{4,5},{5,6},{6,7},{7,4},{8,9},{9,10},{10,1... | collective-permute-start | bytes 1572872 | tf_op jit(solution)/shard_map/ppermute | solution.py:190
  260.4 25.6 %collective-permute-start.18 = (bf16[128,2048]{1,0:T(8,128)(2,1)}, bf16[128,2048]{1,0:T(8,128)(2,1)}, u32[]{:S(2)}, u32[]{:S(2)}) collective-permute-start(bf16[128,2048]{1,0:T(8,128)(2,1)} %get-tuple-element.240), channel_id=1, source_target_pairs={{0,3},{1,0},{2,1},{3,2},{4,7},{5,4},{6,5},{7,6},{8,11},{9,8},{10,9... | collective-permute-start | bytes 1572872 | tf_op jit(solution)/shard_map/ppermute | solution.py:190
  286.0 152.0 %reduce-scatter.7.cloned.1.call-start = ((), (), s32[]{:S(2)}) async-start(), calls=%async_computation.14 | async-start | bytes 2621440 | tf_op jit(solution)/shard_map/reduce_scatter | solution.py:417
  291.2 30.7 %collective-permute-start.21 = (bf16[512,2048]{1,0:T(8,128)(2,1)S(1)}, bf16[512,2048]{1,0:T(8,128)(2,1)S(1)}, u32[]{:S(2)}, u32[]{:S(2)}) collective-permute-start(bf16[512,2048]{1,0:T(8,128)(2,1)S(1)} %convolution_convert_fusion), channel_id=1, source_target_pairs={{0,4},{4,0},{8,12},{12,8},{16,20},{20,16},{24,28},{28,24},{1,5},{5... | collective-permute-start | bytes 6291464 | tf_op jit(solution)/shard_map/ppermute | solution.py:138
  291.3 26.5 %collective-permute-start.20 = (bf16[128,2048]{1,0:T(8,128)(2,1)S(1)}, bf16[128,2048]{1,0:T(8,128)(2,1)S(1)}, u32[]{:S(2)}, u32[]{:S(2)}) collective-permute-start(bf16[128,2048]{1,0:T(8,128)(2,1)S(1)} %copy-done.28), channel_id=1, source_target_pairs={{0,2},{1,3},{2,0},{3,1},{4,6},{5,7},{6,4},{7,5},{8,10},{9,11},{10,... | collective-permute-start | bytes 1572872 | tf_op jit(solution)/shard_map/ppermute | solution.py:190
  324.0 24.8 %collective-permute-start.22 = (bf16[128,2048]{1,0:T(8,128)(2,1)}, bf16[128,2048]{1,0:T(8,128)(2,1)S(1)}, u32[]{:S(2)}, u32[]{:S(2)}) collective-permute-start(bf16[128,2048]{1,0:T(8,128)(2,1)} %get-tuple-element.176), channel_id=1, source_target_pairs={{0,8},{4,12},{8,0},{12,4},{16,24},{20,28},{24,16},{28,20},{1,9},{5... | collective-permute-start | bytes 1572872 | tf_op jit(solution)/shard_map/ppermute | solution.py:138
  325.5 24.2 %collective-permute-start.23 = (bf16[128,2048]{1,0:T(8,128)(2,1)}, bf16[128,2048]{1,0:T(8,128)(2,1)S(1)}, u32[]{:S(2)}, u32[]{:S(2)}) collective-permute-start(bf16[128,2048]{1,0:T(8,128)(2,1)} %get-tuple-element.176), channel_id=1, source_target_pairs={{0,16},{4,20},{8,24},{12,28},{16,0},{20,4},{24,8},{28,12},{1,17},{... | collective-permute-start | bytes 1572872 | tf_op jit(solution)/shard_map/ppermute | solution.py:138
  326.9 33.5 %collective-permute-start.24 = (bf16[128,2048]{1,0:T(8,128)(2,1)}, bf16[128,2048]{1,0:T(8,128)(2,1)S(1)}, u32[]{:S(2)}, u32[]{:S(2)}) collective-permute-start(bf16[128,2048]{1,0:T(8,128)(2,1)} %get-tuple-element.176), channel_id=1, source_target_pairs={{0,24},{4,28},{8,16},{12,20},{16,8},{20,12},{24,0},{28,4},{1,25},{... | collective-permute-start | bytes 1572872 | tf_op jit(solution)/shard_map/ppermute | solution.py:138
  361.3 4.5 collective-permute-start.25
  365.8 57.4 %all-to-all-start.2 = ((bf16[8,64,1024]{2,1,0:T(8,128)(2,1)}), bf16[8,64,1024]{2,1,0:T(8,128)(2,1)}, u32[]{:S(2)}, u32[]{:S(2)}) async-start(bf16[8,64,1024]{2,1,0:T(8,128)(2,1)} %bitcast.179), calls=%async_computation.3 | async-start | bytes 2097152 | tf_op jit(solution)/shard_map/all_to_all | solution.py:432
  370.1 154.9 %reduce-scatter.9.cloned.1.call-start = ((), (), s32[]{:S(2)}) async-start(), calls=%async_computation.15 | async-start | bytes 1310720 | tf_op jit(solution)/shard_map/reduce_scatter | solution.py:446
  392.9 1.6 collective-permute-start.26
  428.8 9.1 %collective-permute-start.27 = (bf16[512,2048]{1,0:T(8,128)(2,1)}, bf16[512,2048]{1,0:T(8,128)(2,1)}, u32[]{:S(2)}, u32[]{:S(2)}) collective-permute-start(bf16[512,2048]{1,0:T(8,128)(2,1)} %convolution_convert_fusion.3), channel_id=1, source_target_pairs={{0,4},{4,0},{8,12},{12,8},{16,20},{20,16},{24,28},{28,24},{1,5},{5... | collective-permute-start | bytes 6291464 | tf_op jit(solution)/shard_map/ppermute | solution.py:138
  438.0 88.7 %reduce-scatter.11.cloned.1.call-start = ((), (), s32[]{:S(2)}) async-start(), calls=%async_computation.16 | async-start | bytes 5242880 | tf_op jit(solution)/shard_map/reduce_scatter | solution.py:390
  445.4 17.7 %collective-permute-start.29 = (bf16[128,2048]{1,0:T(8,128)(2,1)}, bf16[128,2048]{1,0:T(8,128)(2,1)}, u32[]{:S(2)}, u32[]{:S(2)}) collective-permute-start(bf16[128,2048]{1,0:T(8,128)(2,1)} %get-tuple-element.234), channel_id=1, source_target_pairs={{0,16},{4,20},{8,24},{12,28},{16,0},{20,4},{24,8},{28,12},{1,17},{... | collective-permute-start | bytes 1572872 | tf_op jit(solution)/shard_map/ppermute | solution.py:138
  445.9 17.2 %collective-permute-start.28 = (bf16[128,2048]{1,0:T(8,128)(2,1)}, bf16[128,2048]{1,0:T(8,128)(2,1)}, u32[]{:S(2)}, u32[]{:S(2)}) collective-permute-start(bf16[128,2048]{1,0:T(8,128)(2,1)} %get-tuple-element.236), channel_id=1, source_target_pairs={{0,8},{4,12},{8,0},{12,4},{16,24},{20,28},{24,16},{28,20},{1,9},{5... | collective-permute-start | bytes 1572872 | tf_op jit(solution)/shard_map/ppermute | solution.py:138
  453.7 18.4 %collective-permute-start.30 = (bf16[128,2048]{1,0:T(8,128)(2,1)}, bf16[128,2048]{1,0:T(8,128)(2,1)S(1)}, u32[]{:S(2)}, u32[]{:S(2)}) collective-permute-start(bf16[128,2048]{1,0:T(8,128)(2,1)} %get-tuple-element.197), channel_id=1, source_target_pairs={{0,24},{4,28},{8,16},{12,20},{16,8},{20,12},{24,0},{28,4},{1,25},{... | collective-permute-start | bytes 1572872 | tf_op jit(solution)/shard_map/ppermute | solution.py:138
  457.0 17.2 %collective-permute-start.32 = (bf16[512,384]{1,0:T(8,128)(2,1)}, bf16[512,384]{1,0:T(8,128)(2,1)}, u32[]{:S(2)}, u32[]{:S(2)}) collective-permute-start(bf16[512,384]{1,0:T(8,128)(2,1)} %get-tuple-element.249), channel_id=1, source_target_pairs={{0,1},{1,2},{2,3},{3,0},{4,5},{5,6},{6,7},{7,4},{8,9},{9,10},{10,1... | collective-permute-start | bytes 1179656 | tf_op jit(solution)/shard_map/ppermute | solution.py:190
  457.0 20.9 %collective-permute-start.31 = (bf16[512,384]{1,0:T(8,128)(2,1)}, bf16[512,384]{1,0:T(8,128)(2,1)}, u32[]{:S(2)}, u32[]{:S(2)}) collective-permute-start(bf16[512,384]{1,0:T(8,128)(2,1)} %get-tuple-element.251), channel_id=1, source_target_pairs={{0,3},{1,0},{2,1},{3,2},{4,7},{5,4},{6,5},{7,6},{8,11},{9,8},{10,9... | collective-permute-start | bytes 1179656 | tf_op jit(solution)/shard_map/ppermute | solution.py:190
  478.6 10.9 %all-to-all-start.3 = ((f32[8,8,512]{2,1,0:T(8,128)}), f32[8,8,512]{2,1,0:T(8,128)S(1)}, u32[]{:S(2)}, u32[]{:S(2)}) async-start(f32[8,8,512]{2,1,0:T(8,128)} %pad_maximum_fusion.6), calls=%async_computation.5 | async-start | bytes 262144 | tf_op jit(solution)/shard_map/all_to_all | solution.py:495
  482.2 22.4 %collective-permute-start.33 = (bf16[512,384]{1,0:T(8,128)(2,1)S(1)}, bf16[512,384]{1,0:T(8,128)(2,1)}, u32[]{:S(2)}, u32[]{:S(2)}) collective-permute-start(bf16[512,384]{1,0:T(8,128)(2,1)S(1)} %get-tuple-element.205), channel_id=1, source_target_pairs={{0,2},{1,3},{2,0},{3,1},{4,6},{5,7},{6,4},{7,5},{8,10},{9,11},{10,... | collective-permute-start | bytes 1179656 | tf_op jit(solution)/shard_map/ppermute | solution.py:190
  490.3 13.0 %all-to-all-start.4 = ((f32[4,1,512]{2,1,0:T(1,128)}), f32[4,1,512]{2,1,0:T(1,128)S(1)}, u32[]{:S(2)}, u32[]{:S(2)}) async-start(f32[4,1,512]{2,1,0:T(1,128)} %reshape.482), calls=%async_computation.6 | async-start | bytes 16384 | tf_op jit(solution)/shard_map/all_to_all | solution.py:502
  506.8 16.7 %all-to-all-start.5 = ((bf16[8,64,384]{2,1,0:T(8,128)(2,1)}), bf16[8,64,384]{2,1,0:T(8,128)(2,1)S(1)}, u32[]{:S(2)}, u32[]{:S(2)}) async-start(bf16[8,64,384]{2,1,0:T(8,128)(2,1)} %bitcast.61), calls=%async_computation.7 | async-start | bytes 786432 | tf_op jit(solution)/shard_map/all_to_all | solution.py:476
  (61 other events, 625.7 us)
Sparse Core Ops, SparseCore 0:
  29.2 39.6 all-gather.11
  73.1 33.7 all-gather.5
  126.6 44.1 all-gather.7
  173.0 51.4 all-gather.9
  286.1 63.0 reduce-scatter.4
  362.8 62.5 reduce-scatter.6
  438.1 25.5 reduce-scatter.8
  467.0 59.0 reduce-scatter.10

commit v3 on v2

--- a/solution.py
+++ b/solution.py
@@ -1,3 +1,4 @@
+import functools
 import math
 
 import jax
@@ -54,7 +55,7 @@
 
 def attend(queries, keys, values, limit, pos):
     rows = min(TILE, queries.shape[0])
-    count = queries.shape[1] // HD
+    count = queries.shape[1] // HD - 1
     tile = pl.BlockSpec((rows, HD), lambda h, i: (i, h))
     whole = pl.BlockSpec(keys.shape, lambda h, i: (0, 0))
     return pl.pallas_call(
@@ -68,7 +69,7 @@
             pl.BlockSpec((1, keys.shape[0]), lambda h, i: (0, 0)),
         ],
         out_specs=tile,
-        out_shape=jax.ShapeDtypeStruct(queries.shape, BF),
+        out_shape=jax.ShapeDtypeStruct((queries.shape[0], count * HD), BF),
         cost_estimate=pl.CostEstimate(flops=0, bytes_accessed=0, transcendentals=0),
         name="attend",
     )(queries, keys, values, limit[:, None], pos[None, :])
@@ -100,7 +101,7 @@
 
 def attend_back(queries, keys, values, grads, limit, pos):
     rows = min(TILE, queries.shape[0])
-    count = queries.shape[1] // HD
+    count = queries.shape[1] // HD - 1
     tile = pl.BlockSpec((rows, HD), lambda h, i: (i, h))
     whole = pl.BlockSpec(keys.shape, lambda h, i: (0, 0))
     return pl.pallas_call(
@@ -116,7 +117,7 @@
         ],
         out_specs=[tile, whole, whole],
         out_shape=[
-            jax.ShapeDtypeStruct(queries.shape, BF),
+            jax.ShapeDtypeStruct((queries.shape[0], count * HD), BF),
             jax.ShapeDtypeStruct(keys.shape, F32),
             jax.ShapeDtypeStruct(keys.shape, F32),
         ],
@@ -129,8 +130,99 @@
     return lax.optimization_barrier(values)
 
 
+def call(kernel, grid, in_specs, out_specs, out_shape, name):
+    return pl.pallas_call(
+        kernel,
+        grid=grid,
+        in_specs=in_specs,
+        out_specs=out_specs,
+        out_shape=out_shape,
+        cost_estimate=pl.CostEstimate(flops=0, bytes_accessed=0, transcendentals=0),
+        name=name,
+    )
+
+
+def multiply_kernel(dim, a_ref, b_ref, out_ref):
+    out_ref[...] = dot(a_ref[...], b_ref[...], 1, dim).astype(out_ref.dtype)
+
+
+def multiply(a, b, dim, dtype=F32):
+    rows, depth = a.shape
+    columns = b.shape[1 - dim]
+    tile = min(512, columns)
+    if dim:
+        b_spec = pl.BlockSpec((tile, depth), lambda j: (j, 0))
+    else:
+        b_spec = pl.BlockSpec((depth, tile), lambda j: (0, j))
+    return call(
+        functools.partial(multiply_kernel, dim),
+        (columns // tile,),
+        [pl.BlockSpec((rows, depth), lambda j: (0, 0)), b_spec],
+        pl.BlockSpec((rows, tile), lambda j: (0, j)),
+        jax.ShapeDtypeStruct((rows, columns), dtype),
+        "multiply",
+    )(a, b)
+
+
+def over_rows_kernel(a0_ref, a1_ref, b0_ref, b1_ref, out_ref):
+    total = dot(a0_ref[...], b0_ref[...], 0, 0) + dot(a1_ref[...], b1_ref[...], 0, 0)
+    out_ref[...] = total.astype(BF)
+
+
 def dot_over_rows(lefts, rights):
-    return dot(lefts[0], rights[0], 0, 0) + dot(lefts[1], rights[1], 0, 0)
+    rows, height = lefts[0].shape
+    width = rights[0].shape[1]
+    tile = min(256, height)
+    left = pl.BlockSpec((rows, tile), lambda i: (0, i))
+    right = pl.BlockSpec((rows, width), lambda i: (0, 0))
+    return call(
+        over_rows_kernel,
+        (height // tile,),
+        [left, left, right, right],
+        pl.BlockSpec((tile, width), lambda i: (i, 0)),
+        jax.ShapeDtypeStruct((height, width), BF),
+        "over_rows",
+    )(*lefts, *rights)
+
+
+def plain_over_rows(lefts, rights):
+    return (dot(lefts[0], rights[0], 0, 0) + dot(lefts[1], rights[1], 0, 0)).astype(BF)
+
+
+def hidden_kernel(x0_ref, x1_ref, w_ref, bias_ref, g0_ref, g1_ref, a0_ref, a1_ref, o0_ref, o1_ref):
+    root, cubic = math.sqrt(2.0 / math.pi), 0.044715
+    halves = (x0_ref, g0_ref, a0_ref, o0_ref), (x1_ref, g1_ref, a1_ref, o1_ref)
+    for x_ref, grad_ref, active_ref, out_ref in halves:
+        u = dot(x_ref[...], w_ref[...], 1, 0) + bias_ref[...]
+        square = u * u
+        t = jnp.tanh(root * u * (1.0 + cubic * square))
+        active_ref[...] = (0.5 * u * (1.0 + t)).astype(BF)
+        slope = 0.5 * (1.0 + t) + 0.5 * u * (1.0 - t * t) * (root * (1.0 + 3.0 * cubic * square))
+        out_ref[...] = (grad_ref[...] * slope).astype(BF)
+
+
+def hidden_layer(halves, weight, bias, grads):
+    count, width = halves[0].shape
+    columns = weight.shape[1]
+    tile = min(256, columns)
+    whole = pl.BlockSpec((count, width), lambda j: (0, 0))
+    piece = pl.BlockSpec((count, tile), lambda j: (0, j))
+    a0, a1, o0, o1 = call(
+        hidden_kernel,
+        (columns // tile,),
+        [
+            whole,
+            whole,
+            pl.BlockSpec((width, tile), lambda j: (0, j)),
+            pl.BlockSpec((1, tile), lambda j: (0, j)),
+            piece,
+            piece,
+        ],
+        [piece] * 4,
+        [jax.ShapeDtypeStruct((count, columns), BF)] * 4,
+        "hidden_layer",
+    )(*halves, weight, bias[None], *grads)
+    return (a0, a1), (o0, o1)
 
 
 def exchange(value, mask):
@@ -332,16 +424,21 @@
     table = attn_rows[:, :, wrows:].reshape(count * depth, 8, wide_cols)
     vectors = [table[:, r, c : c + n].reshape(-1).astype(F32) for r, c, n in places]
     gain_one, shift_one, qbias, vbias, pbias, gain_two, shift_two, ubias, dbias = vectors
-    qbias = lax.dynamic_slice(qbias, (at * qcols,), (qcols,))
     ubias = lax.dynamic_slice(
         ubias.reshape(chips, 2 * depth, frows), (0, core * depth + level, 0), (chips, 1, frows)
     ).reshape(-1)
+    bias_one = jnp.concatenate(
+        [
+            lax.dynamic_slice(qbias, (at * qcols,), (qcols,)),
+            jnp.where(core == 1, vbias, 0.0),
+        ]
+    )
     normed_one = [
         (normalize(half.astype(F32))[0] * gain_one + shift_one).astype(BF) for half in row_halves
     ]
     mixed = jnp.concatenate([dot(half, qkv_local, 1, 0) for half in normed_one], 0)
-    queries = (mixed[:, :qcols] + qbias).astype(BF)
-    mine = (mixed[:, qcols:] + jnp.where(core == 1, vbias, 0.0)).astype(BF)
+    queries = (mixed + bias_one).astype(BF)
+    mine = queries[:, qcols:]
     theirs = jnp.roll(exchange(mine, 1), total // 2, 0)
     keys = jnp.where(core == 0, mine, theirs)
     values = jnp.where(core == 0, theirs, mine)
@@ -364,27 +461,25 @@
     middle = own_rows + branch + pbias
     scaled_two, inverse_two = normalize(middle)
     normed_two_own = (scaled_two * gain_two + shift_two).astype(BF)
-    normed_two_own, down_local = stage(normed_two_own, down_local)
+    normed_two_own, down_local, up_parts, mlp_rows = stage(
+        normed_two_own, down_local, up_parts, mlp_rows
+    )
 
     up_local = lax.all_gather(
-        stage(up_parts, mlp_rows)[0], "ctx", axis=0, tiled=True, axis_index_groups=chip_groups()
+        up_parts, "ctx", axis=0, tiled=True, axis_index_groups=chip_groups()
     )
 
     near = near_rows(normed_two_own)
-    near, normed_value = stage(near, normed_two_own)
-    mlp_halves = both_cores(stage(mlp_rows, near)[0])
-    grad_active = [dot(half, down_local, 1, 1) for half in mlp_halves]
+    mlp_halves = both_cores(mlp_rows)
+    grad_active = [multiply(half, down_local, 1) for half in mlp_halves]
+    near, normed_value, mlp_halves, grad_active = stage(
+        near, normed_two_own, mlp_halves, grad_active
+    )
     normed_rows = far_rows(normed_value, near)
-    normed_rows, mlp_halves, grad_active = stage(normed_rows, mlp_halves, grad_active)
+    normed_rows = stage(normed_rows)[0]
 
     normed_halves = both_cores(normed_rows)
-    active, grad_before = [], []
-    befores = stage(*[dot(half, up_local, 1, 0) for half in normed_halves])
-    for before, grad_half in zip(befores, grad_active):
-        before = before + ubias
-        active_f, gelu_pull = jax.vjp(gelu, before)
-        active.append(active_f.astype(BF))
-        grad_before.append(gelu_pull(grad_half)[0].astype(BF))
+    active, grad_before = hidden_layer(normed_halves, up_local, ubias, grad_active)
 
     def chip_sum(term):
         return lax.psum_scatter(
@@ -395,28 +490,32 @@
 
     held = stage(normed_halves, grad_before, active, mlp_halves, two_parts)
     normed, grads, acts, mlps = held[:4]
-    up_term = dot_over_rows(normed, grads).astype(BF)
-    down_term = dot_over_rows(acts, mlps).astype(BF)
+    out_other = exchange(multiply(acts[1], down_local, 0, BF), 1)
+    out_own = multiply(acts[0], down_local, 0)
+    up_term = dot_over_rows(normed, grads)
+    near, two_parts, up_term, out_own, out_other = stage(
+        column_near(two_parts), two_parts, up_term, out_own, out_other
+    )
+    out_term = (out_own + out_other.astype(F32)).astype(BF)
+    up_grad = chip_sum(up_term)
+    acts, mlps, grads = stage(acts, mlps, grads, near)[:3]
+    down_term = dot_over_rows(acts, mlps)
     ubias_term = jnp.sum(grads[0].astype(F32), 0) + jnp.sum(grads[1].astype(F32), 0)
-    near, two_parts, up_term, down_term, ubias_term = stage(
-        column_near(two_parts), two_parts, up_term, down_term, ubias_term
-    )
-    up_grad = chip_sum(up_term)
-    out_own, out_other = core_sum(stage(acts, near)[0], down_local, 0)
-    out_term = (out_own + out_other.astype(F32)).astype(BF)
     grad_two = column_far(two_parts, near)
     gain_two_term = jnp.sum(grad_two * scaled_two, 0)
     shift_two_term = jnp.sum(grad_two, 0)
     grad_middle = upstream + norm_backward(grad_two, scaled_two, inverse_two, gain_two)
     grad_branch_own = grad_middle.astype(BF)
-    grad_branch_own, out_term, down_term = stage(grad_branch_own, out_term, down_term)
+    grad_branch_own, out_term, down_term, ubias_term = stage(
+        grad_branch_own, out_term, down_term, ubias_term
+    )
+    out_sum = lax.psum_scatter(out_term, "fsdp", scatter_dimension=0, tiled=True)
 
     branch_halves = both_cores(jnp.concatenate(plane_direct(grad_branch_own), 0))
     pbias_term = jnp.sum(grad_branch_own.astype(F32), 0)
     dbias_term = jnp.sum(grad_mlp_own.astype(F32), 0)
-    out_sum = lax.psum_scatter(out_term, "fsdp", scatter_dimension=0, tiled=True)
-    branch_halves, pbias_term, dbias_term, down_term, up_grad = stage(
-        branch_halves, pbias_term, dbias_term, down_term, up_grad
+    branch_halves, pbias_term, dbias_term, up_grad = stage(
+        branch_halves, pbias_term, dbias_term, up_grad
     )
 
     grad_attended = jnp.concatenate(
@@ -429,6 +528,16 @@
     given = jnp.roll(exchange(given, 1), total // 2, 0).astype(F32)
     grad_kind = (jnp.where(core == 0, grad_keys, grad_values) + given).astype(BF)
     grad_mixed = jnp.concatenate([grad_queries, grad_kind], 1)
+
+    grad_mixed, down_term = stage(grad_mixed, down_term)
+    down_grad = chip_sum(down_term)
+
+    mixed_halves = grad_mixed[: total // 2], grad_mixed[total // 2 :]
+    proj_term = plain_over_rows(attended_halves, branch_halves)
+    one_sums = core_sum(mixed_halves, qkv_local, 1)
+    one_sums, proj_term, out_sum = stage(one_sums, proj_term, out_sum)
+    one_parts = plane_parts(one_sums)
+    up_grad = stage(up_grad, one_parts)[0]
     up_grad = lax.all_to_all(
         up_grad.reshape(2 * depth, wrows, chips * frows),
         BOTH,
@@ -437,19 +546,10 @@
         tiled=True,
         axis_index_groups=chip_devices(),
     )
-    grad_mixed, up_grad = stage(grad_mixed, up_grad)
-
-    mixed_halves = grad_mixed[: total // 2], grad_mixed[total // 2 :]
-    proj_term = dot_over_rows(attended_halves, branch_halves).astype(BF)
-    one_sums = core_sum(mixed_halves, qkv_local, 1)
-    one_sums, proj_term, out_sum = stage(one_sums, proj_term, out_sum)
-    proj_grad = lax.psum_scatter(proj_term, "fsdp", scatter_dimension=0, tiled=True)
-    down_grad = chip_sum(stage(down_term, proj_term)[0])
-    one_parts = plane_parts(one_sums)
 
     def qkv_parts(*gate):
         halves = stage(mixed_halves, gate)[0]
-        term = dot_over_rows(normed_one, halves).astype(BF)
+        term = plain_over_rows(normed_one, halves)
         term = term.reshape(count, depth, wrows, wide_cols).transpose(1, 0, 2, 3)
         return column_parts(term.reshape(depth * count * wrows, wide_cols))
 
@@ -458,9 +558,9 @@
     scaled_one, inverse_one = normalize(own_rows)
     gain_one_term = jnp.sum(grad_one * scaled_one, 0)
     shift_one_term = jnp.sum(grad_one, 0)
-    held = (grad_one, qkv_term, qkv_near, up_grad)
+    held = (grad_one, qkv_term, qkv_near, up_grad, proj_term)
     gain_one_term, shift_one_term, held = stage(gain_one_term, shift_one_term, held)
-    grad_one, qkv_term, qkv_near, up_grad = held
+    grad_one, qkv_term, qkv_near, up_grad, proj_term = held
 
     result = middle + out_sum.astype(F32) + dbias
     layer_out = jnp.where(live, result, 0.0).astype(BF)
@@ -476,8 +576,6 @@
     qkv_grad = lax.all_to_all(qkv_grad, "ctx", 0, 0, tiled=True).transpose(1, 0, 2).astype(F32)
     kinds = jnp.sum(qkv_grad[:, :, qcols:].reshape(wrows, chips, 2 * HD), 1)
     qkv_grad = jnp.concatenate([qkv_grad[:, :, :qcols].reshape(wrows, width), kinds], 1)
-    down_grad = down_grad.astype(F32)
-    proj_grad = proj_grad.astype(F32)
 
     mixed_term = jnp.sum(grad_mixed.astype(F32), 0)
     vbias_term = jnp.where(core == 1, mixed_term[qcols:], 0.0).reshape(count * depth, -1)
@@ -499,7 +597,11 @@
     ubias_grad = first[0, block:]
     second = first[:, :block] + jnp.pad(mixed_term[None, :qcols], ((7, 0), (0, 0)))
     second = second.reshape(8, depth, wrows).transpose(1, 0, 2)
-    second = jnp.sum(lax.all_to_all(second, "fsdp", 0, 0, tiled=True), 0)
+    second = lax.all_to_all(second, "fsdp", 0, 0, tiled=True)
+    second, down_grad, proj_term = stage(second, down_grad, proj_term)
+    proj_grad = lax.psum_scatter(proj_term, "fsdp", scatter_dimension=0, tiled=True)
+    proj_grad, down_grad = proj_grad.astype(F32), down_grad.astype(F32)
+    second = jnp.sum(second, 0)
     wide_grads = [second[i] for i in (5, 6, 0, 1, 2, 3)]
     vbias_grad = second[4, : value_bias.shape[0]]
     qbias_grad = second[7]

time: 547 us -> 526 us (0.962)
  matrix products: 94.4 us -> 40.1 us
  Pallas kernels: 24.1 us -> 78.4 us
  local copies, waits for them, and re-layouts: 55.6 us -> 46.8 us
  other arithmetic: 62.9 us -> 55.7 us
    pallas_call x0 -> x7, Pallas kernels: none -> 54.3 us  [the longest x4 24.2 us: multiply(): call(functools.partial(multiply_kernel, dim), (columns // tile,), [pl.Blo...]
    dot_general x24 -> x14, matrix products: 94.4 us -> 40.1 us  [dot(): lax.dot_general(a, b, (((da,), (db,)), ((), ())), preferred_element_type=...]
    ppermute x25, waiting for transfers between devices: 61.1 us -> 103 us  [exchange(): return lax.ppermute(value, 'ctx', [(i, i ^ mask) for i in range(count)])]
    all_to_all x1, waiting for transfers between devices: 27.5 us -> 0.01 us  [body(): lax.all_to_all(up_grad.reshape(2 * depth, wrows, chips * frows), BOTH, 0,...]
    all_gather x1, waiting for transfers between devices: 23.4 us -> 8.22 us  [body(): mlp_rows = lax.all_gather(grad_mlp_own, 'fsdp', axis=0, tiled=True)]
    ppermute x9, waiting for transfers between devices: 59.2 us -> 47.4 us  [turned(): lax.ppermute(value, 'fsdp', [(i, (i + by) % depth) for i in range(depth)])]
    convert_element_type x5 -> x3, other arithmetic: 11.3 us -> 3.48 us  [the longest x2 3.34 us: body(): proj_grad, down_grad = (proj_grad.astype(F32), down_grad.astype(F32))]
    reduce_scatter x1, waiting for transfers between devices: 0.01 us -> 7.24 us  [body(): lax.psum_scatter(proj_term, 'fsdp', scatter_dimension=0, tiled=True)]
  transfers between devices with their start and end apart: 47 -> 47, of which waited for: 20 -> 27; matrix products, arithmetic and copies ran while one was open for 34% -> 24% of each run, Pallas kernels for 4% -> 12%
where the time goes in v3:
time: 526 us; the launch traced here: 516 us
  waiting for transfers between devices  210 us (40%)
  Pallas kernels  78.4 us (15%)
  other arithmetic  55.7 us (11%)
  starting transfers between devices  54.9 us (10%)
  local copies, waits for them, and re-layouts  46.8 us (9%)
  matrix products  40.1 us (8%)
  between operations  16.2 us (3%)
  blocking collectives  13.9 us (3%)
    ppermute x25, waiting for transfers between devices, exchange(): return lax.ppermute(value, 'ctx', [(i, i ^ mask) for i in range(count)])  103 us
    ppermute x9, waiting for transfers between devices, turned(): lax.ppermute(value, 'fsdp', [(i, (i + by) % depth) for i in range(depth)])  47.4 us
    dot_general x14, matrix products, dot(): lax.dot_general(a, b, (((da,), (db,)), ((), ())), preferred_element_type=...  40.1 us
    pallas_call x4, Pallas kernels, multiply(): call(functools.partial(multiply_kernel, dim), (columns // tile,), [pl.Blo...  24.2 us
    ppermute x25, starting transfers between devices, exchange(): return lax.ppermute(value, 'ctx', [(i, i ^ mask) for i in range(count)])  19.1 us
    pallas_call x2, Pallas kernels, dot_over_rows(): call(over_rows_kernel, (height // tile,), [left, left, right, right], pl....  18.8 us
    all_to_all x1, waiting for transfers between devices, body(): lax.all_to_all(up_parts, BOTH, 0, 0, tiled=True, axis_index_groups=chip_d...  17.5 us
    pallas_call x1, Pallas kernels, attend_back(): pl.pallas_call(attend_back_kernel, grid=(count, queries.shape[0] // rows)...  15.2 us
  transfers between devices with their start and end apart: 47, of which 27 were waited for; matrix products, arithmetic and copies ran while one was open for 24% of the time, Pallas kernels for 12%

profile of v3, /device:TPU:0, one launch (start us, length us, event | category | flops | bytes accessed | tf_op | source)
XLA Modules:
  0.0 515.9 jit_solution(760743251638020434)
XLA Ops:
  10.8 13.9 %all_to_all.30 = bf16[8,72,384]{2,1,0:T(8,128)(2,1)} all-to-all(bf16[8,72,384]{2,1,0:T(8,128)(2,1)S(1)} %copy.94), channel_id=1, replica_groups=mesh['ctx'=8,'fsdp'=4] {'ctx'}, dimensions={0} | all-to-all | bytes 884736 | tf_op jit(solution)/shard_map/all_to_all | solution.py:398
  29.1 10.4 %collective-permute-done = bf16[128,2048]{1,0:T(8,128)(2,1)S(1)} collective-permute-done((bf16[128,2048]{1,0:T(8,128)(2,1)S(1)}, bf16[128,2048]{1,0:T(8,128)(2,1)S(1)}, u32[]{:S(2)}, u32[]{:S(2)}) %collective-permute-start) | collective-permute-done | bytes 524320 | tf_op jit(solution)/shard_map/ppermute | solution.py:230
  40.4 9.6 %collective-permute-done.1 = bf16[128,2048]{1,0:T(8,128)(2,1)S(1)} collective-permute-done((bf16[128,2048]{1,0:T(8,128)(2,1)S(1)}, bf16[128,2048]{1,0:T(8,128)(2,1)S(1)}, u32[]{:S(2)}, u32[]{:S(2)}) %collective-permute-start.1) | collective-permute-done | bytes 524320 | tf_op jit(solution)/shard_map/ppermute | solution.py:230
  58.1 10.8 %all-gather.12.cloned.1.call-done = bf16[32,72,384]{2,1,0:T(8,128)(2,1)} async-done(((bf16[8,72,384]{2,1,0:T(8,128)(2,1)}), bf16[32,72,384]{2,1,0:T(8,128)(2,1)}) %all-gather.12.cloned.1.call-update) | async-done | bytes 1769488 | tf_op jit(solution)/shard_map/all_gather | solution.py:401
  72.6 3.0 convert_reduce_fusion
  83.2 4.2 all-to-all-start.1
  87.6 3.1 fusion.47
  94.8 8.8 %attend.1 = bf16[1024,256]{1,0:T(8,128)(2,1)} custom-call(bf16[1024,384]{1,0:T(8,128)(2,1)} %copy-done.9, bf16[1024,128]{1,0:T(8,128)(2,1)} %get-tuple-element.260.k_ref, bf16[1024,128]{1,0:T(8,128)(2,1)} %get-tuple-element.259.v_ref, s32[1024,1]{1,0:T(8,128)} %broadcast_minimum_fusion.row_limit_ref, s32[1,1024]{1,0:T(1,128)} %bitcast.173), custom_call_target="tpu_custom_call" | custom-call | tf_op jit(solution)/shard_map/attend/pallas_call | solution.py:61
  104.7 17.5 %all-to-all-done.1 = bf16[8,64,1024]{2,1,0:T(8,128)(2,1)} async-done(((bf16[8,64,1024]{2,1,0:T(8,128)(2,1)}), bf16[8,64,1024]{2,1,0:T(8,128)(2,1)}, u32[]{:S(2)}, u32[]{:S(2)}) %all-to-all-start.1) | async-done | bytes 1048608 | tf_op jit(solution)/shard_map/all_to_all | solution.py:419
  122.2 3.3 convolution_convert_fusion.1
  138.6 9.5 %collective-permute-done.11 = bf16[128,2048]{1,0:T(8,128)(2,1)S(1)} collective-permute-done((bf16[128,2048]{1,0:T(8,128)(2,1)S(1)}, bf16[128,2048]{1,0:T(8,128)(2,1)S(1)}, u32[]{:S(2)}, u32[]{:S(2)}) %collective-permute-start.11) | collective-permute-done | bytes 524320 | tf_op jit(solution)/shard_map/ppermute | solution.py:230
  148.1 10.8 %collective-permute-done.9 = bf16[128,2048]{1,0:T(8,128)(2,1)S(1)} collective-permute-done((bf16[128,2048]{1,0:T(8,128)(2,1)S(1)}, bf16[128,2048]{1,0:T(8,128)(2,1)S(1)}, u32[]{:S(2)}, u32[]{:S(2)}) %collective-permute-start.9) | collective-permute-done | bytes 524320 | tf_op jit(solution)/shard_map/ppermute | solution.py:230
  161.9 8.2 %all-gather.8.cloned.1.call-done.a_ref.b0_ref = bf16[512,2048]{1,0:T(8,128)(2,1)} async-done(((bf16[128,2048]{1,0:T(8,128)(2,1)}), bf16[512,2048]{1,0:T(8,128)(2,1)}) %all-gather.8.cloned.1.call-update) | async-done | bytes 2097168 | tf_op jit(solution)/shard_map/all_gather | solution.py:413
  172.4 5.8 %multiply.76.g0_ref = f32[512,1024]{1,0:T(8,128)} custom-call(bf16[512,2048]{1,0:T(8,128)(2,1)} %all-gather.8.cloned.1.call-done.a_ref.b0_ref, bf16[1024,2048]{1,0:T(8,128)(2,1)} %bitcast.132), custom_call_target="tpu_custom_call" | custom-call | tf_op jit(solution)/shard_map/multiply/pallas_call | solution.py:157
  179.5 6.0 %multiply.77.g1_ref = f32[512,1024]{1,0:T(8,128)} custom-call(bf16[512,2048]{1,0:T(8,128)(2,1)} %copy-done.10, bf16[1024,2048]{1,0:T(8,128)(2,1)} %bitcast.133), custom_call_target="tpu_custom_call" | custom-call | tf_op jit(solution)/shard_map/multiply/pallas_call | solution.py:157
  185.4 11.2 %collective-permute-done.12 = bf16[128,2048]{1,0:T(8,128)(2,1)} collective-permute-done((bf16[128,2048]{1,0:T(8,128)(2,1)}, bf16[128,2048]{1,0:T(8,128)(2,1)}, u32[]{:S(2)}, u32[]{:S(2)}) %collective-permute-start.12) | collective-permute-done | bytes 524320 | tf_op jit(solution)/shard_map/ppermute | solution.py:282
  200.3 22.2 %collective-permute-done.15 = bf16[128,2048]{1,0:T(8,128)(2,1)S(1)} collective-permute-done((bf16[128,2048]{1,0:T(8,128)(2,1)}, bf16[128,2048]{1,0:T(8,128)(2,1)S(1)}, u32[]{:S(2)}, u32[]{:S(2)}) %collective-permute-start.15) | collective-permute-done | bytes 524320 | tf_op jit(solution)/shard_map/ppermute | solution.py:282
  222.6 4.3 collective-permute-done.16.x1_ref.a1_ref
  226.9 11.4 %hidden_layer.1 = (bf16[512,1024]{1,0:T(8,128)(2,1)}, bf16[512,1024]{1,0:T(8,128)(2,1)}, bf16[512,1024]{1,0:T(8,128)(2,1)}, bf16[512,1024]{1,0:T(8,128)(2,1)}) custom-call(bf16[512,2048]{1,0:T(8,128)(2,1)} %bitcast.137, bf16[512,2048]{1,0:T(8,128)(2,1)} %collective-permute-done.16.x1_ref.a1_ref, bf16[2048,1024]{1,0:T(8,128)(2,1)} %all-gather.10.cloned.1.call-done.w_ref, ...), custom_call_target="tpu_custom_call" | custom-call | tf_op jit(solution)/shard_map/hidden_layer/pallas_call | solution.py:210
  238.3 6.4 %convolution_convert_fusion = bf16[512,2048]{1,0:T(8,128)(2,1)} fusion(bf16[512,1024]{1,0:T(8,128)(2,1)} %get-tuple-element.182.b1_ref, bf16[2048,1024]{1,0:T(8,128)(2,1)} %all-gather.10.cloned.1.call-done.w_ref), kind=kOutput, calls=%fused_computation.18 | convolution fusion | flops 2148532224 | bytes 7340032 | tf_op jit(solution)/shard_map/dot_general | solution.py:22
  244.8 4.6 fusion.57
  249.4 3.5 add_convert_fusion.5
  252.9 6.1 %multiply.79 = bf16[512,2048]{1,0:T(8,128)(2,1)} custom-call(bf16[512,1024]{1,0:T(8,128)(2,1)} %get-tuple-element.178.a_ref.a1_ref, bf16[1024,2048]{1,0:T(8,128)(2,1)} %bitcast.134), custom_call_target="tpu_custom_call" | custom-call | tf_op jit(solution)/shard_map/multiply/pallas_call | solution.py:157
  259.3 3.8 collective-permute-start.18
  263.1 6.4 %multiply.78 = f32[512,2048]{1,0:T(8,128)} custom-call(bf16[512,1024]{1,0:T(8,128)(2,1)} %get-tuple-element.177.a_ref.a0_ref, bf16[1024,2048]{1,0:T(8,128)(2,1)} %bitcast.135), custom_call_target="tpu_custom_call" | custom-call | tf_op jit(solution)/shard_map/multiply/pallas_call | solution.py:157
  269.5 10.0 %over_rows.2 = bf16[2048,1024]{1,0:T(8,128)(2,1)} custom-call(bf16[512,2048]{1,0:T(8,128)(2,1)} %bitcast.138, bf16[512,2048]{1,0:T(8,128)(2,1)} %collective-permute-done.16.x1_ref.a1_ref, bf16[512,1024]{1,0:T(8,128)(2,1)} %get-tuple-element.181.b0_ref, bf16[512,1024]{1,0:T(8,128)(2,1)} %get-tuple-element.182.b1_ref), custom_call_target="tpu_custom_call" | custom-call | tf_op jit(solution)/shard_map/over_rows/pallas_call | solution.py:178
  279.6 5.3 %collective-permute-done.18 = bf16[128,2048]{1,0:T(8,128)(2,1)} collective-permute-done((bf16[128,2048]{1,0:T(8,128)(2,1)}, bf16[128,2048]{1,0:T(8,128)(2,1)}, u32[]{:S(2)}, u32[]{:S(2)}) %collective-permute-start.18) | collective-permute-done | bytes 524320 | tf_op jit(solution)/shard_map/ppermute | solution.py:282
  287.9 8.7 %over_rows.3 = bf16[1024,2048]{1,0:T(8,128)(2,1)} custom-call(bf16[512,1024]{1,0:T(8,128)(2,1)} %get-tuple-element.177.a_ref.a0_ref, bf16[512,1024]{1,0:T(8,128)(2,1)} %get-tuple-element.178.a_ref.a1_ref, bf16[512,2048]{1,0:T(8,128)(2,1)} %all-gather.8.cloned.1.call-done.a_ref.b0_ref, bf16[512,2048]{1,0:T(8,128)(2,1)} %copy-done.10), custom_call_target="tpu_custom_call" | custom-call | tf_op jit(solution)/shard_map/over_rows/pallas_call | solution.py:178
  296.6 5.2 %add_convert_fusion = bf16[512,2048]{1,0:T(8,128)(2,1)} fusion(f32[512,2048]{1,0:T(8,128)} %multiply.78, bf16[512,2048]{1,0:T(8,128)(2,1)} %collective-permute-done.20), kind=kLoop, calls=%fused_computation.16 | loop fusion | flops 3145728 | bytes 8388608 | tf_op jit(solution)/shard_map/convert_element_type | solution.py:499
  301.9 8.8 %collective-permute-done.21 = bf16[128,2048]{1,0:T(8,128)(2,1)} collective-permute-done((bf16[128,2048]{1,0:T(8,128)(2,1)}, bf16[128,2048]{1,0:T(8,128)(2,1)}, u32[]{:S(2)}, u32[]{:S(2)}) %collective-permute-start.21) | collective-permute-done | bytes 524320 | tf_op jit(solution)/shard_map/ppermute | solution.py:282
  319.2 14.7 %collective-permute-done.22 = bf16[128,2048]{1,0:T(8,128)(2,1)} collective-permute-done((bf16[128,2048]{1,0:T(8,128)(2,1)S(1)}, bf16[128,2048]{1,0:T(8,128)(2,1)}, u32[]{:S(2)}, u32[]{:S(2)}) %collective-permute-start.22) | collective-permute-done | bytes 524320 | tf_op jit(solution)/shard_map/ppermute | solution.py:230
  335.8 3.9 collective-permute-done.23
  341.5 10.7 %collective-permute-done.24 = bf16[128,2048]{1,0:T(8,128)(2,1)} collective-permute-done((bf16[128,2048]{1,0:T(8,128)(2,1)S(1)}, bf16[128,2048]{1,0:T(8,128)(2,1)}, u32[]{:S(2)}, u32[]{:S(2)}) %collective-permute-start.24) | collective-permute-done | bytes 524320 | tf_op jit(solution)/shard_map/ppermute | solution.py:230
  364.2 15.2 %attend_back.1 = (bf16[1024,256]{1,0:T(8,128)(2,1)}, f32[1024,128]{1,0:T(8,128)}, f32[1024,128]{1,0:T(8,128)}) custom-call(bf16[1024,384]{1,0:T(8,128)(2,1)} %copy-done.9, bf16[1024,128]{1,0:T(8,128)(2,1)} %get-tuple-element.260.k_ref, bf16[1024,128]{1,0:T(8,128)(2,1)} %get-tuple-element.259.v_ref, bf16[1024,256]{1,0:T(8,128)(2,1)} %pad_maximum_fusion.2.grad_ref, ...), custom_call_target="tpu_custom_call" | custom-call | tf_op jit(solution)/shard_map/attend_back/pallas_call | solution.py:107
  392.1 4.3 fusion.58
  398.6 4.3 add_convert_fusion.3
  406.0 4.5 all-to-all-start.2
  410.5 3.2 fusion.45
  426.3 3.6 collective-permute-done.28
  429.9 20.8 %collective-permute-done.30 = bf16[128,2048]{1,0:T(8,128)(2,1)} collective-permute-done((bf16[128,2048]{1,0:T(8,128)(2,1)}, bf16[128,2048]{1,0:T(8,128)(2,1)}, u32[]{:S(2)}, u32[]{:S(2)}) %collective-permute-start.30) | collective-permute-done | bytes 524320 | tf_op jit(solution)/shard_map/ppermute | solution.py:230
  454.6 4.7 all-to-all-start.3
  461.3 5.2 %all-to-all-done.3 = f32[8,8,512]{2,1,0:T(8,128)S(1)} async-done(((f32[8,8,512]{2,1,0:T(8,128)}), f32[8,8,512]{2,1,0:T(8,128)S(1)}, u32[]{:S(2)}, u32[]{:S(2)}) %all-to-all-start.3) | async-done | bytes 131104 | tf_op jit(solution)/shard_map/all_to_all | solution.py:593
  467.3 3.2 all-to-all-start.4
  470.6 3.0 reshape.431
  473.6 2.8 copy.106
  483.4 3.9 all-to-all-start.5
  489.3 6.3 %all-to-all-done.5 = bf16[8,64,384]{2,1,0:T(8,128)(2,1)S(1)} async-done(((bf16[8,64,384]{2,1,0:T(8,128)(2,1)}), bf16[8,64,384]{2,1,0:T(8,128)(2,1)S(1)}, u32[]{:S(2)}, u32[]{:S(2)}) %all-to-all-start.5) | async-done | bytes 393248 | tf_op jit(solution)/shard_map/all_to_all | solution.py:576
  499.8 7.2 %reduce-scatter.11.cloned.1.call-done = bf16[64,2048]{1,0:T(8,128)(2,1)} async-done(((bf16[256,2048]{1,0:T(8,128)(2,1)}), bf16[64,2048]{1,0:T(8,128)(2,1)}) %reduce-scatter.11.cloned.1.call-update) | async-done | bytes 262160 | tf_op jit(solution)/shard_map/reduce_scatter | solution.py:602
  (343 shorter events, 135.5 us)
Async XLA Ops:
  7.2 61.7 %all-gather.12.cloned.1.call-start = ((), (), s32[]{:S(2)}) async-start(), calls=%async_computation.17 | async-start | bytes 2211840 | tf_op jit(solution)/shard_map/all_gather | solution.py:401
  24.7 14.8 %collective-permute-start = (bf16[128,2048]{1,0:T(8,128)(2,1)S(1)}, bf16[128,2048]{1,0:T(8,128)(2,1)S(1)}, u32[]{:S(2)}, u32[]{:S(2)}) collective-permute-start(bf16[128,2048]{1,0:T(8,128)(2,1)S(1)} %bitcast.139), channel_id=1, source_target_pairs={{0,8},{4,12},{8,0},{12,4},{16,24},{20,28},{24,16},{28,20},{1,9},{5... | collective-permute-start | bytes 1572872 | tf_op jit(solution)/shard_map/ppermute | solution.py:230
  25.3 24.7 %collective-permute-start.1 = (bf16[128,2048]{1,0:T(8,128)(2,1)S(1)}, bf16[128,2048]{1,0:T(8,128)(2,1)S(1)}, u32[]{:S(2)}, u32[]{:S(2)}) collective-permute-start(bf16[128,2048]{1,0:T(8,128)(2,1)S(1)} %bitcast.140), channel_id=1, source_target_pairs={{0,16},{4,20},{8,24},{12,28},{16,0},{20,4},{24,8},{28,12},{1,17},{... | collective-permute-start | bytes 1572872 | tf_op jit(solution)/shard_map/ppermute | solution.py:230
  25.8 25.0 %collective-permute-start.2 = (bf16[128,2048]{1,0:T(8,128)(2,1)S(1)}, bf16[128,2048]{1,0:T(8,128)(2,1)S(1)}, u32[]{:S(2)}, u32[]{:S(2)}) collective-permute-start(bf16[128,2048]{1,0:T(8,128)(2,1)S(1)} %bitcast.141), channel_id=1, source_target_pairs={{0,24},{4,28},{8,16},{12,20},{16,8},{20,12},{24,0},{28,4},{1,25},{... | collective-permute-start | bytes 1572872 | tf_op jit(solution)/shard_map/ppermute | solution.py:230
  29.0 75.7 %all-gather.6.cloned.1.call-start = ((), (), s32[]{:S(2)}) async-start(), calls=%async_computation.10 | async-start | bytes 1310720 | tf_op jit(solution)/shard_map/all_gather | solution.py:412
  51.6 6.5 %collective-permute-start.3 = (bf16[512,2048]{1,0:T(8,128)(2,1)}, bf16[512,2048]{1,0:T(8,128)(2,1)}, u32[]{:S(2)}, u32[]{:S(2)}) collective-permute-start(bf16[512,2048]{1,0:T(8,128)(2,1)} %constant_dynamic-update-slice_fusion), channel_id=1, source_target_pairs={{0,4},{4,0},{8,12},{12,8},{16,20},{20,16},{24,28},{28,24},{1,5},{5... | collective-permute-start | bytes 6291464 | tf_op jit(solution)/shard_map/ppermute | solution.py:230
  54.6 49.0 %collective-permute-start.7 = (bf16[256,2048]{1,0:T(8,128)(2,1)}, bf16[256,2048]{1,0:T(8,128)(2,1)}, u32[]{:S(2)}, u32[]{:S(2)}) collective-permute-start(bf16[256,2048]{1,0:T(8,128)(2,1)} %param.30), channel_id=1, source_target_pairs={{0,24},{4,28},{8,16},{12,20},{16,8},{20,12},{24,0},{28,4},{1,25},{... | collective-permute-start | bytes 3145736 | tf_op jit(solution)/shard_map/ppermute | solution.py:230
  55.0 48.6 %collective-permute-start.6 = (bf16[256,2048]{1,0:T(8,128)(2,1)}, bf16[256,2048]{1,0:T(8,128)(2,1)}, u32[]{:S(2)}, u32[]{:S(2)}) collective-permute-start(bf16[256,2048]{1,0:T(8,128)(2,1)} %param.30), channel_id=1, source_target_pairs={{0,16},{4,20},{8,24},{12,28},{16,0},{20,4},{24,8},{28,12},{1,17},{... | collective-permute-start | bytes 3145736 | tf_op jit(solution)/shard_map/ppermute | solution.py:230
  57.3 46.4 %collective-permute-start.5 = (bf16[256,2048]{1,0:T(8,128)(2,1)}, bf16[256,2048]{1,0:T(8,128)(2,1)}, u32[]{:S(2)}, u32[]{:S(2)}) collective-permute-start(bf16[256,2048]{1,0:T(8,128)(2,1)} %param.30), channel_id=1, source_target_pairs={{0,8},{4,12},{8,0},{12,4},{16,24},{20,28},{24,16},{28,20},{1,9},{5... | collective-permute-start | bytes 3145736 | tf_op jit(solution)/shard_map/ppermute | solution.py:230
  83.2 39.0 %all-to-all-start.1 = ((bf16[8,64,1024]{2,1,0:T(8,128)(2,1)}), bf16[8,64,1024]{2,1,0:T(8,128)(2,1)}, u32[]{:S(2)}, u32[]{:S(2)}) async-start(bf16[8,64,1024]{2,1,0:T(8,128)(2,1)} %reshape.410), calls=%async_computation.1 | async-start | bytes 2097152 | tf_op jit(solution)/shard_map/all_to_all | solution.py:419
  87.4 82.7 %all-gather.8.cloned.1.call-start = ((), (), s32[]{:S(2)}) async-start(), calls=%async_computation.11 | async-start | bytes 2621440 | tf_op jit(solution)/shard_map/all_gather | solution.py:413
  92.3 1.6 collective-permute-start.4
  125.5 4.9 collective-permute-start.8
  125.9 101.1 %all-gather.10.cloned.1.call-start = ((), (), s32[]{:S(2)}) async-start(), calls=%async_computation.12 | async-start | bytes 5242880 | tf_op jit(solution)/shard_map/all_gather | solution.py:468
  132.4 15.7 %collective-permute-start.11 = (bf16[128,2048]{1,0:T(8,128)(2,1)S(1)}, bf16[128,2048]{1,0:T(8,128)(2,1)S(1)}, u32[]{:S(2)}, u32[]{:S(2)}) collective-permute-start(bf16[128,2048]{1,0:T(8,128)(2,1)S(1)} %get-tuple-element.253), channel_id=1, source_target_pairs={{0,24},{4,28},{8,16},{12,20},{16,8},{20,12},{24,0},{28,4},{1,25},{... | collective-permute-start | bytes 1572872 | tf_op jit(solution)/shard_map/ppermute | solution.py:230
  134.8 24.1 %collective-permute-start.9 = (bf16[128,2048]{1,0:T(8,128)(2,1)S(1)}, bf16[128,2048]{1,0:T(8,128)(2,1)S(1)}, u32[]{:S(2)}, u32[]{:S(2)}) collective-permute-start(bf16[128,2048]{1,0:T(8,128)(2,1)S(1)} %get-tuple-element.252), channel_id=1, source_target_pairs={{0,8},{4,12},{8,0},{12,4},{16,24},{20,28},{24,16},{28,20},{1,9},{5... | collective-permute-start | bytes 1572872 | tf_op jit(solution)/shard_map/ppermute | solution.py:230
  135.4 23.5 %collective-permute-start.10 = (bf16[128,2048]{1,0:T(8,128)(2,1)S(1)}, bf16[128,2048]{1,0:T(8,128)(2,1)S(1)}, u32[]{:S(2)}, u32[]{:S(2)}) collective-permute-start(bf16[128,2048]{1,0:T(8,128)(2,1)S(1)} %get-tuple-element.254), channel_id=1, source_target_pairs={{0,16},{4,20},{8,24},{12,28},{16,0},{20,4},{24,8},{28,12},{1,17},{... | collective-permute-start | bytes 1572872 | tf_op jit(solution)/shard_map/ppermute | solution.py:230
  170.2 188.5 %reduce-scatter.5.cloned.1.call-start = ((), (), s32[]{:S(2)}) async-start(), calls=%async_computation.13 | async-start | bytes 5242880 | tf_op jit(solution)/shard_map/reduce_scatter | solution.py:485
  170.2 8.0 %collective-permute-start.14 = (bf16[512,2048]{1,0:T(8,128)(2,1)}, bf16[512,2048]{1,0:T(8,128)(2,1)S(1)}, u32[]{:S(2)}, u32[]{:S(2)}) collective-permute-start(bf16[512,2048]{1,0:T(8,128)(2,1)} %all-gather.8.cloned.1.call-done.a_ref.b0_ref), channel_id=1, source_target_pairs={{0,4},{4,0},{8,12},{12,8},{16,20},{20,16},{24,28},{28,24},{1,5},{5... | collective-permute-start | bytes 6291464 | tf_op jit(solution)/shard_map/ppermute | solution.py:230
  170.3 15.2 %collective-permute-start.13 = (bf16[128,2048]{1,0:T(8,128)(2,1)}, bf16[128,2048]{1,0:T(8,128)(2,1)}, u32[]{:S(2)}, u32[]{:S(2)}) collective-permute-start(bf16[128,2048]{1,0:T(8,128)(2,1)} %add_convert_fusion.8), channel_id=1, source_target_pairs={{0,3},{1,0},{2,1},{3,2},{4,7},{5,4},{6,5},{7,6},{8,11},{9,8},{10,9... | collective-permute-start | bytes 1572872 | tf_op jit(solution)/shard_map/ppermute | solution.py:282
  171.5 25.2 %collective-permute-start.12 = (bf16[128,2048]{1,0:T(8,128)(2,1)}, bf16[128,2048]{1,0:T(8,128)(2,1)}, u32[]{:S(2)}, u32[]{:S(2)}) collective-permute-start(bf16[128,2048]{1,0:T(8,128)(2,1)} %add_convert_fusion.8), channel_id=1, source_target_pairs={{0,1},{1,2},{2,3},{3,0},{4,5},{5,6},{6,7},{7,4},{8,9},{9,10},{10,1... | collective-permute-start | bytes 1572872 | tf_op jit(solution)/shard_map/ppermute | solution.py:282
  196.6 25.8 %collective-permute-start.15 = (bf16[128,2048]{1,0:T(8,128)(2,1)}, bf16[128,2048]{1,0:T(8,128)(2,1)S(1)}, u32[]{:S(2)}, u32[]{:S(2)}) collective-permute-start(bf16[128,2048]{1,0:T(8,128)(2,1)} %add_convert_fusion.8), channel_id=1, source_target_pairs={{0,2},{1,3},{2,0},{3,1},{4,6},{5,7},{6,4},{7,5},{8,10},{9,11},{10,... | collective-permute-start | bytes 1572872 | tf_op jit(solution)/shard_map/ppermute | solution.py:282
  222.6 4.4 collective-permute-start.16
  244.7 4.7 collective-permute-start.17
  258.9 25.9 %collective-permute-start.20 = (bf16[512,2048]{1,0:T(8,128)(2,1)}, bf16[512,2048]{1,0:T(8,128)(2,1)}, u32[]{:S(2)}, u32[]{:S(2)}) collective-permute-start(bf16[512,2048]{1,0:T(8,128)(2,1)} %multiply.79), channel_id=1, source_target_pairs={{0,4},{4,0},{8,12},{12,8},{16,20},{20,16},{24,28},{28,24},{1,5},{5... | collective-permute-start | bytes 6291464 | tf_op jit(solution)/shard_map/ppermute | solution.py:230
  259.3 20.3 %collective-permute-start.19 = (bf16[128,2048]{1,0:T(8,128)(2,1)}, bf16[128,2048]{1,0:T(8,128)(2,1)}, u32[]{:S(2)}, u32[]{:S(2)}) collective-permute-start(bf16[128,2048]{1,0:T(8,128)(2,1)} %get-tuple-element.249), channel_id=1, source_target_pairs={{0,1},{1,2},{2,3},{3,0},{4,5},{5,6},{6,7},{7,4},{8,9},{9,10},{10,1... | collective-permute-start | bytes 1572872 | tf_op jit(solution)/shard_map/ppermute | solution.py:282
  259.3 25.5 %collective-permute-start.18 = (bf16[128,2048]{1,0:T(8,128)(2,1)}, bf16[128,2048]{1,0:T(8,128)(2,1)}, u32[]{:S(2)}, u32[]{:S(2)}) collective-permute-start(bf16[128,2048]{1,0:T(8,128)(2,1)} %get-tuple-element.250), channel_id=1, source_target_pairs={{0,3},{1,0},{2,1},{3,2},{4,7},{5,4},{6,5},{7,6},{8,11},{9,8},{10,9... | collective-permute-start | bytes 1572872 | tf_op jit(solution)/shard_map/ppermute | solution.py:282
  284.8 113.8 %reduce-scatter.7.cloned.1.call-start = ((), (), s32[]{:S(2)}) async-start(), calls=%async_computation.14 | async-start | bytes 2621440 | tf_op jit(solution)/shard_map/reduce_scatter | solution.py:512
  285.1 25.6 %collective-permute-start.21 = (bf16[128,2048]{1,0:T(8,128)(2,1)}, bf16[128,2048]{1,0:T(8,128)(2,1)}, u32[]{:S(2)}, u32[]{:S(2)}) collective-permute-start(bf16[128,2048]{1,0:T(8,128)(2,1)} %get-tuple-element.169), channel_id=1, source_target_pairs={{0,2},{1,3},{2,0},{3,1},{4,6},{5,7},{6,4},{7,5},{8,10},{9,11},{10,... | collective-permute-start | bytes 1572872 | tf_op jit(solution)/shard_map/ppermute | solution.py:282
  314.8 19.1 %collective-permute-start.22 = (bf16[128,2048]{1,0:T(8,128)(2,1)S(1)}, bf16[128,2048]{1,0:T(8,128)(2,1)}, u32[]{:S(2)}, u32[]{:S(2)}) collective-permute-start(bf16[128,2048]{1,0:T(8,128)(2,1)S(1)} %get-tuple-element.183), channel_id=1, source_target_pairs={{0,8},{4,12},{8,0},{12,4},{16,24},{20,28},{24,16},{28,20},{1,9},{5... | collective-permute-start | bytes 1572872 | tf_op jit(solution)/shard_map/ppermute | solution.py:230
  316.2 23.4 %collective-permute-start.23 = (bf16[128,2048]{1,0:T(8,128)(2,1)S(1)}, bf16[128,2048]{1,0:T(8,128)(2,1)}, u32[]{:S(2)}, u32[]{:S(2)}) collective-permute-start(bf16[128,2048]{1,0:T(8,128)(2,1)S(1)} %get-tuple-element.183), channel_id=1, source_target_pairs={{0,16},{4,20},{8,24},{12,28},{16,0},{20,4},{24,8},{28,12},{1,17},{... | collective-permute-start | bytes 1572872 | tf_op jit(solution)/shard_map/ppermute | solution.py:230
  317.8 34.5 %collective-permute-start.24 = (bf16[128,2048]{1,0:T(8,128)(2,1)S(1)}, bf16[128,2048]{1,0:T(8,128)(2,1)}, u32[]{:S(2)}, u32[]{:S(2)}) collective-permute-start(bf16[128,2048]{1,0:T(8,128)(2,1)S(1)} %get-tuple-element.183), channel_id=1, source_target_pairs={{0,24},{4,28},{8,16},{12,20},{16,8},{20,12},{24,0},{28,4},{1,25},{... | collective-permute-start | bytes 1572872 | tf_op jit(solution)/shard_map/ppermute | solution.py:230
  319.1 39.5 %copy-start.21 = (bf16[256,2048]{1,0:T(8,128)(2,1)S(1)}, bf16[256,2048]{1,0:T(8,128)(2,1)}, u32[]{:S(2)}) copy-start(bf16[256,2048]{1,0:T(8,128)(2,1)} %all-gather.6.cloned.1.call-done) | copy-start | bytes 3145732
  319.1 162.0 %reduce-scatter.9.cloned.1.call-start = ((), (), s32[]{:S(2)}) async-start(), calls=%async_computation.15 | async-start | bytes 5242880 | tf_op jit(solution)/shard_map/reduce_scatter | solution.py:485
  354.1 4.5 collective-permute-start.25
  380.6 1.6 collective-permute-start.26
  386.7 9.7 %collective-permute-start.27 = (bf16[512,2048]{1,0:T(8,128)(2,1)}, bf16[512,2048]{1,0:T(8,128)(2,1)}, u32[]{:S(2)}, u32[]{:S(2)}) collective-permute-start(bf16[512,2048]{1,0:T(8,128)(2,1)} %convolution_convert_fusion.2), channel_id=1, source_target_pairs={{0,4},{4,0},{8,12},{12,8},{16,20},{20,16},{24,28},{28,24},{1,5},{5... | collective-permute-start | bytes 6291464 | tf_op jit(solution)/shard_map/ppermute | solution.py:230
  403.0 23.4 %collective-permute-start.29 = (bf16[128,2048]{1,0:T(8,128)(2,1)}, bf16[128,2048]{1,0:T(8,128)(2,1)}, u32[]{:S(2)}, u32[]{:S(2)}) collective-permute-start(bf16[128,2048]{1,0:T(8,128)(2,1)} %get-tuple-element.244), channel_id=1, source_target_pairs={{0,16},{4,20},{8,24},{12,28},{16,0},{20,4},{24,8},{28,12},{1,17},{... | collective-permute-start | bytes 1572872 | tf_op jit(solution)/shard_map/ppermute | solution.py:230
  404.5 25.4 %collective-permute-start.28 = (bf16[128,2048]{1,0:T(8,128)(2,1)}, bf16[128,2048]{1,0:T(8,128)(2,1)}, u32[]{:S(2)}, u32[]{:S(2)}) collective-permute-start(bf16[128,2048]{1,0:T(8,128)(2,1)} %get-tuple-element.246), channel_id=1, source_target_pairs={{0,8},{4,12},{8,0},{12,4},{16,24},{20,28},{24,16},{28,20},{1,9},{5... | collective-permute-start | bytes 1572872 | tf_op jit(solution)/shard_map/ppermute | solution.py:230
  406.0 47.2 %all-to-all-start.2 = ((bf16[8,64,1024]{2,1,0:T(8,128)(2,1)}), bf16[8,64,1024]{2,1,0:T(8,128)(2,1)}, u32[]{:S(2)}, u32[]{:S(2)}) async-start(bf16[8,64,1024]{2,1,0:T(8,128)(2,1)} %bitcast.165), calls=%async_computation.4 | async-start | bytes 2097152 | tf_op jit(solution)/shard_map/all_to_all | solution.py:541
  416.7 34.0 %collective-permute-start.30 = (bf16[128,2048]{1,0:T(8,128)(2,1)}, bf16[128,2048]{1,0:T(8,128)(2,1)}, u32[]{:S(2)}, u32[]{:S(2)}) collective-permute-start(bf16[128,2048]{1,0:T(8,128)(2,1)} %get-tuple-element.203), channel_id=1, source_target_pairs={{0,24},{4,28},{8,16},{12,20},{16,8},{20,12},{24,0},{28,4},{1,25},{... | collective-permute-start | bytes 1572872 | tf_op jit(solution)/shard_map/ppermute | solution.py:230
  420.2 32.9 %collective-permute-start.32 = (bf16[512,384]{1,0:T(8,128)(2,1)}, bf16[512,384]{1,0:T(8,128)(2,1)}, u32[]{:S(2)}, u32[]{:S(2)}) collective-permute-start(bf16[512,384]{1,0:T(8,128)(2,1)} %get-tuple-element.255), channel_id=1, source_target_pairs={{0,1},{1,2},{2,3},{3,0},{4,5},{5,6},{6,7},{7,4},{8,9},{9,10},{10,1... | collective-permute-start | bytes 1179656 | tf_op jit(solution)/shard_map/ppermute | solution.py:282
  422.2 30.9 %collective-permute-start.31 = (bf16[512,384]{1,0:T(8,128)(2,1)}, bf16[512,384]{1,0:T(8,128)(2,1)}, u32[]{:S(2)}, u32[]{:S(2)}) collective-permute-start(bf16[512,384]{1,0:T(8,128)(2,1)} %get-tuple-element.257), channel_id=1, source_target_pairs={{0,3},{1,0},{2,1},{3,2},{4,7},{5,4},{6,5},{7,6},{8,11},{9,8},{10,9... | collective-permute-start | bytes 1179656 | tf_op jit(solution)/shard_map/ppermute | solution.py:282
  454.6 11.9 %all-to-all-start.3 = ((f32[8,8,512]{2,1,0:T(8,128)}), f32[8,8,512]{2,1,0:T(8,128)S(1)}, u32[]{:S(2)}, u32[]{:S(2)}) async-start(f32[8,8,512]{2,1,0:T(8,128)} %pad_maximum_fusion.5), calls=%async_computation.5 | async-start | bytes 262144 | tf_op jit(solution)/shard_map/all_to_all | solution.py:593
  459.3 21.9 %collective-permute-start.33 = (bf16[512,384]{1,0:T(8,128)(2,1)}, bf16[512,384]{1,0:T(8,128)(2,1)}, u32[]{:S(2)}, u32[]{:S(2)}) collective-permute-start(bf16[512,384]{1,0:T(8,128)(2,1)} %get-tuple-element.216), channel_id=1, source_target_pairs={{0,2},{1,3},{2,0},{3,1},{4,6},{5,7},{6,4},{7,5},{8,10},{9,11},{10,... | collective-permute-start | bytes 1179656 | tf_op jit(solution)/shard_map/ppermute | solution.py:282
  467.3 12.6 %all-to-all-start.4 = ((f32[4,1,512]{2,1,0:T(1,128)}), f32[4,1,512]{2,1,0:T(1,128)S(1)}, u32[]{:S(2)}, u32[]{:S(2)}) async-start(f32[4,1,512]{2,1,0:T(1,128)} %reshape.475), calls=%async_computation.6 | async-start | bytes 16384 | tf_op jit(solution)/shard_map/all_to_all | solution.py:600
  470.6 36.5 %reduce-scatter.11.cloned.1.call-start = ((), (), s32[]{:S(2)}) async-start(), calls=%async_computation.16 | async-start | bytes 1310720 | tf_op jit(solution)/shard_map/reduce_scatter | solution.py:602
  483.4 12.2 %all-to-all-start.5 = ((bf16[8,64,384]{2,1,0:T(8,128)(2,1)}), bf16[8,64,384]{2,1,0:T(8,128)(2,1)S(1)}, u32[]{:S(2)}, u32[]{:S(2)}) async-start(bf16[8,64,384]{2,1,0:T(8,128)(2,1)} %bitcast.162), calls=%async_computation.8 | async-start | bytes 786432 | tf_op jit(solution)/shard_map/all_to_all | solution.py:576
  (57 other events, 575.0 us)
Sparse Core Ops, SparseCore 0:
  29.2 39.6 all-gather.11
  72.7 31.9 all-gather.5
  126.0 44.1 all-gather.7
  171.8 51.4 all-gather.9
  285.0 68.7 reduce-scatter.4
  356.6 41.9 reduce-scatter.6
  401.6 71.5 reduce-scatter.8
  481.3 25.6 reduce-scatter.10

commit v4 on v3

--- a/solution.py
+++ b/solution.py
@@ -12,7 +12,7 @@
 HD = 128
 EPS = 1e-05
 NEG = -1e30
-TILE = 256
+TILE = 512
 BOTH = ("ctx", "fsdp")
 BF = jnp.bfloat16
 F32 = jnp.float32
@@ -490,13 +490,13 @@
 
     held = stage(normed_halves, grad_before, active, mlp_halves, two_parts)
     normed, grads, acts, mlps = held[:4]
-    out_other = exchange(multiply(acts[1], down_local, 0, BF), 1)
+    out_other = multiply(acts[1], down_local, 0, BF)
     out_own = multiply(acts[0], down_local, 0)
     up_term = dot_over_rows(normed, grads)
     near, two_parts, up_term, out_own, out_other = stage(
         column_near(two_parts), two_parts, up_term, out_own, out_other
     )
-    out_term = (out_own + out_other.astype(F32)).astype(BF)
+    out_term = (out_own + exchange(out_other, 1).astype(F32)).astype(BF)
     up_grad = chip_sum(up_term)
     acts, mlps, grads = stage(acts, mlps, grads, near)[:3]
     down_term = dot_over_rows(acts, mlps)
@@ -593,14 +593,14 @@
     first = lax.all_to_all(
         jnp.concatenate([early + late, ub], 2), "ctx", 0, 0, tiled=True
     )
+    down_grad, proj_term = stage(down_grad, proj_term, first)[:2]
+    proj_grad = lax.psum_scatter(proj_term, "fsdp", scatter_dimension=0, tiled=True)
+    proj_grad, down_grad = proj_grad.astype(F32), down_grad.astype(F32)
     first = jnp.sum(first, 0)
     ubias_grad = first[0, block:]
     second = first[:, :block] + jnp.pad(mixed_term[None, :qcols], ((7, 0), (0, 0)))
     second = second.reshape(8, depth, wrows).transpose(1, 0, 2)
     second = lax.all_to_all(second, "fsdp", 0, 0, tiled=True)
-    second, down_grad, proj_term = stage(second, down_grad, proj_term)
-    proj_grad = lax.psum_scatter(proj_term, "fsdp", scatter_dimension=0, tiled=True)
-    proj_grad, down_grad = proj_grad.astype(F32), down_grad.astype(F32)
     second = jnp.sum(second, 0)
     wide_grads = [second[i] for i in (5, 6, 0, 1, 2, 3)]
     vbias_grad = second[4, : value_bias.shape[0]]

time: 526 us -> 523 us (level)
  waiting for transfers between devices: 210 us -> 200 us
  starting transfers between devices: 54.9 us -> 63.4 us
    all_gather x1, starting transfers between devices: 0.51 us -> 9.93 us  [body(): lax.all_gather(up_parts, 'ctx', axis=0, tiled=True, axis_index_groups=chi...]
    all_gather x1, waiting for transfers between devices: 8.22 us -> 0.01 us  [body(): mlp_rows = lax.all_gather(grad_mlp_own, 'fsdp', axis=0, tiled=True)]
    unnamed x124 -> x125, local copies, waits for them, and re-layouts: 12.8 us -> 14 us
  transfers between devices with their start and end apart: 47 -> 47, of which waited for: 27 -> 25; matrix products, arithmetic and copies ran while one was open for 24% -> 24% of each run, Pallas kernels for 12% -> 12%
where the time goes in v4:
time: 523 us; the launch traced here: 512 us
  waiting for transfers between devices  200 us (38%)
  Pallas kernels  75.1 us (14%)
  starting transfers between devices  63.4 us (12%)
  other arithmetic  57.1 us (11%)
  local copies, waits for them, and re-layouts  46.6 us (9%)
  matrix products  40.1 us (8%)
  between operations  16.2 us (3%)
  blocking collectives  13.9 us (3%)
    ppermute x25, waiting for transfers between devices, exchange(): return lax.ppermute(value, 'ctx', [(i, i ^ mask) for i in range(count)])  102 us
    ppermute x9, waiting for transfers between devices, turned(): lax.ppermute(value, 'fsdp', [(i, (i + by) % depth) for i in range(depth)])  48.3 us
    dot_general x14, matrix products, dot(): lax.dot_general(a, b, (((da,), (db,)), ((), ())), preferred_element_type=...  40.1 us
    pallas_call x4, Pallas kernels, multiply(): call(functools.partial(multiply_kernel, dim), (columns // tile,), [pl.Blo...  24.1 us
    ppermute x25, starting transfers between devices, exchange(): return lax.ppermute(value, 'ctx', [(i, i ^ mask) for i in range(count)])  18.9 us
    pallas_call x2, Pallas kernels, dot_over_rows(): call(over_rows_kernel, (height // tile,), [left, left, right, right], pl....  18.8 us
    all_to_all x1, waiting for transfers between devices, body(): lax.all_to_all(up_parts, BOTH, 0, 0, tiled=True, axis_index_groups=chip_d...  17.5 us
    unnamed x125, local copies, waits for them, and re-layouts  14 us
  transfers between devices with their start and end apart: 47, of which 25 were waited for; matrix products, arithmetic and copies ran while one was open for 24% of the time, Pallas kernels for 12%

profile of v4, /device:TPU:0, one launch (start us, length us, event | category | flops | bytes accessed | tf_op | source)
XLA Modules:
  0.0 512.5 jit_solution(3075160948889116158)
XLA Ops:
  10.8 13.9 %all_to_all.30 = bf16[8,72,384]{2,1,0:T(8,128)(2,1)} all-to-all(bf16[8,72,384]{2,1,0:T(8,128)(2,1)S(1)} %copy.94), channel_id=1, replica_groups=mesh['ctx'=8,'fsdp'=4] {'ctx'}, dimensions={0} | all-to-all | bytes 884736 | tf_op jit(solution)/shard_map/all_to_all | solution.py:398
  29.1 10.4 %collective-permute-done = bf16[128,2048]{1,0:T(8,128)(2,1)S(1)} collective-permute-done((bf16[128,2048]{1,0:T(8,128)(2,1)S(1)}, bf16[128,2048]{1,0:T(8,128)(2,1)S(1)}, u32[]{:S(2)}, u32[]{:S(2)}) %collective-permute-start) | collective-permute-done | bytes 524320 | tf_op jit(solution)/shard_map/ppermute | solution.py:230
  40.4 9.6 %collective-permute-done.1 = bf16[128,2048]{1,0:T(8,128)(2,1)S(1)} collective-permute-done((bf16[128,2048]{1,0:T(8,128)(2,1)S(1)}, bf16[128,2048]{1,0:T(8,128)(2,1)S(1)}, u32[]{:S(2)}, u32[]{:S(2)}) %collective-permute-start.1) | collective-permute-done | bytes 524320 | tf_op jit(solution)/shard_map/ppermute | solution.py:230
  58.1 10.8 %all-gather.12.cloned.1.call-done = bf16[32,72,384]{2,1,0:T(8,128)(2,1)} async-done(((bf16[8,72,384]{2,1,0:T(8,128)(2,1)}), bf16[32,72,384]{2,1,0:T(8,128)(2,1)}) %all-gather.12.cloned.1.call-update) | async-done | bytes 1769488 | tf_op jit(solution)/shard_map/all_gather | solution.py:401
  69.8 2.7 slice.221
  72.6 3.0 convert_reduce_fusion
  83.2 4.3 all-to-all-start.1
  87.6 3.1 fusion.47
  94.8 8.7 %attend.1 = bf16[1024,256]{1,0:T(8,128)(2,1)} custom-call(bf16[1024,384]{1,0:T(8,128)(2,1)} %copy-done.10, bf16[1024,128]{1,0:T(8,128)(2,1)} %get-tuple-element.258.k_ref, bf16[1024,128]{1,0:T(8,128)(2,1)} %get-tuple-element.257.v_ref, s32[1024,1]{1,0:T(8,128)} %broadcast_minimum_fusion.row_limit_ref, s32[1,1024]{1,0:T(1,128)} %bitcast.172), custom_call_target="tpu_custom_call" | custom-call | tf_op jit(solution)/shard_map/attend/pallas_call | solution.py:61
  104.7 17.5 %all-to-all-done.1 = bf16[8,64,1024]{2,1,0:T(8,128)(2,1)} async-done(((bf16[8,64,1024]{2,1,0:T(8,128)(2,1)}), bf16[8,64,1024]{2,1,0:T(8,128)(2,1)}, u32[]{:S(2)}, u32[]{:S(2)}) %all-to-all-start.1) | async-done | bytes 1048608 | tf_op jit(solution)/shard_map/all_to_all | solution.py:419
  122.2 3.3 convolution_convert_fusion.1
  125.9 9.9 %all-gather.10.cloned.1.call-start = ((), (), s32[]{:S(2)}) async-start(), calls=%async_computation.12 | async-start | bytes 5242880 | tf_op jit(solution)/shard_map/all_gather | solution.py:468
  147.9 9.5 %collective-permute-done.11 = bf16[128,2048]{1,0:T(8,128)(2,1)S(1)} collective-permute-done((bf16[128,2048]{1,0:T(8,128)(2,1)S(1)}, bf16[128,2048]{1,0:T(8,128)(2,1)S(1)}, u32[]{:S(2)}, u32[]{:S(2)}) %collective-permute-start.11) | collective-permute-done | bytes 524320 | tf_op jit(solution)/shard_map/ppermute | solution.py:230
  157.5 10.7 %collective-permute-done.9 = bf16[128,2048]{1,0:T(8,128)(2,1)S(1)} collective-permute-done((bf16[128,2048]{1,0:T(8,128)(2,1)S(1)}, bf16[128,2048]{1,0:T(8,128)(2,1)S(1)}, u32[]{:S(2)}, u32[]{:S(2)}) %collective-permute-start.9) | collective-permute-done | bytes 524320 | tf_op jit(solution)/shard_map/ppermute | solution.py:230
  173.5 5.8 %multiply.76.g0_ref = f32[512,1024]{1,0:T(8,128)} custom-call(bf16[512,2048]{1,0:T(8,128)(2,1)} %all-gather.8.cloned.1.call-done.a_ref.b0_ref, bf16[1024,2048]{1,0:T(8,128)(2,1)} %bitcast.132), custom_call_target="tpu_custom_call" | custom-call | tf_op jit(solution)/shard_map/multiply/pallas_call | solution.py:157
  180.6 5.8 %multiply.77.g1_ref = f32[512,1024]{1,0:T(8,128)} custom-call(bf16[512,2048]{1,0:T(8,128)(2,1)} %copy-done.11, bf16[1024,2048]{1,0:T(8,128)(2,1)} %bitcast.133), custom_call_target="tpu_custom_call" | custom-call | tf_op jit(solution)/shard_map/multiply/pallas_call | solution.py:157
  186.5 10.8 %collective-permute-done.12 = bf16[128,2048]{1,0:T(8,128)(2,1)} collective-permute-done((bf16[128,2048]{1,0:T(8,128)(2,1)}, bf16[128,2048]{1,0:T(8,128)(2,1)}, u32[]{:S(2)}, u32[]{:S(2)}) %collective-permute-start.12) | collective-permute-done | bytes 524320 | tf_op jit(solution)/shard_map/ppermute | solution.py:282
  201.1 21.9 %collective-permute-done.15 = bf16[128,2048]{1,0:T(8,128)(2,1)S(1)} collective-permute-done((bf16[128,2048]{1,0:T(8,128)(2,1)}, bf16[128,2048]{1,0:T(8,128)(2,1)S(1)}, u32[]{:S(2)}, u32[]{:S(2)}) %collective-permute-start.15) | collective-permute-done | bytes 524320 | tf_op jit(solution)/shard_map/ppermute | solution.py:282
  223.2 4.3 collective-permute-done.16.x1_ref.a1_ref
  227.4 11.4 %hidden_layer.1 = (bf16[512,1024]{1,0:T(8,128)(2,1)}, bf16[512,1024]{1,0:T(8,128)(2,1)}, bf16[512,1024]{1,0:T(8,128)(2,1)}, bf16[512,1024]{1,0:T(8,128)(2,1)}) custom-call(bf16[512,2048]{1,0:T(8,128)(2,1)} %bitcast.137, bf16[512,2048]{1,0:T(8,128)(2,1)} %collective-permute-done.16.x1_ref.a1_ref, bf16[2048,1024]{1,0:T(8,128)(2,1)} %all-gather.10.cloned.1.call-done.w_ref, ...), custom_call_target="tpu_custom_call" | custom-call | tf_op jit(solution)/shard_map/hidden_layer/pallas_call | solution.py:210
  238.9 6.4 %convolution_convert_fusion = bf16[512,2048]{1,0:T(8,128)(2,1)} fusion(bf16[512,1024]{1,0:T(8,128)(2,1)} %get-tuple-element.181.b1_ref, bf16[2048,1024]{1,0:T(8,128)(2,1)} %all-gather.10.cloned.1.call-done.w_ref), kind=kOutput, calls=%fused_computation.18 | convolution fusion | flops 2148532224 | bytes 7340032 | tf_op jit(solution)/shard_map/dot_general | solution.py:22
  245.4 4.6 fusion.57
  250.0 3.5 add_convert_fusion.5
  253.4 3.8 collective-permute-start.18
  257.3 6.0 %multiply.79 = bf16[512,2048]{1,0:T(8,128)(2,1)} custom-call(bf16[512,1024]{1,0:T(8,128)(2,1)} %get-tuple-element.177.a_ref.a1_ref, bf16[1024,2048]{1,0:T(8,128)(2,1)} %bitcast.134), custom_call_target="tpu_custom_call" | custom-call | tf_op jit(solution)/shard_map/multiply/pallas_call | solution.py:157
  263.3 6.5 %multiply.78 = f32[512,2048]{1,0:T(8,128)} custom-call(bf16[512,1024]{1,0:T(8,128)(2,1)} %get-tuple-element.176.a_ref.a0_ref, bf16[1024,2048]{1,0:T(8,128)(2,1)} %bitcast.135), custom_call_target="tpu_custom_call" | custom-call | tf_op jit(solution)/shard_map/multiply/pallas_call | solution.py:157
  269.8 10.0 %over_rows.2 = bf16[2048,1024]{1,0:T(8,128)(2,1)} custom-call(bf16[512,2048]{1,0:T(8,128)(2,1)} %bitcast.138, bf16[512,2048]{1,0:T(8,128)(2,1)} %collective-permute-done.16.x1_ref.a1_ref, bf16[512,1024]{1,0:T(8,128)(2,1)} %get-tuple-element.180.b0_ref, bf16[512,1024]{1,0:T(8,128)(2,1)} %get-tuple-element.181.b1_ref), custom_call_target="tpu_custom_call" | custom-call | tf_op jit(solution)/shard_map/over_rows/pallas_call | solution.py:178
  282.6 8.8 %over_rows.3 = bf16[1024,2048]{1,0:T(8,128)(2,1)} custom-call(bf16[512,1024]{1,0:T(8,128)(2,1)} %get-tuple-element.176.a_ref.a0_ref, bf16[512,1024]{1,0:T(8,128)(2,1)} %get-tuple-element.177.a_ref.a1_ref, bf16[512,2048]{1,0:T(8,128)(2,1)} %all-gather.8.cloned.1.call-done.a_ref.b0_ref, bf16[512,2048]{1,0:T(8,128)(2,1)} %copy-done.11), custom_call_target="tpu_custom_call" | custom-call | tf_op jit(solution)/shard_map/over_rows/pallas_call | solution.py:178
  291.4 15.5 %collective-permute-done.20 = bf16[128,2048]{1,0:T(8,128)(2,1)} collective-permute-done((bf16[128,2048]{1,0:T(8,128)(2,1)}, bf16[128,2048]{1,0:T(8,128)(2,1)}, u32[]{:S(2)}, u32[]{:S(2)}) %collective-permute-start.20) | collective-permute-done | bytes 524320 | tf_op jit(solution)/shard_map/ppermute | solution.py:282
  306.9 2.6 multiply_reduce_fusion
  312.2 3.7 add_convert_fusion
  320.3 21.4 %collective-permute-done.22 = bf16[128,2048]{1,0:T(8,128)(2,1)} collective-permute-done((bf16[128,2048]{1,0:T(8,128)(2,1)S(1)}, bf16[128,2048]{1,0:T(8,128)(2,1)}, u32[]{:S(2)}, u32[]{:S(2)}) %collective-permute-start.22) | collective-permute-done | bytes 524320 | tf_op jit(solution)/shard_map/ppermute | solution.py:230
  345.4 7.8 %collective-permute-done.24 = bf16[128,2048]{1,0:T(8,128)(2,1)} collective-permute-done((bf16[128,2048]{1,0:T(8,128)(2,1)S(1)}, bf16[128,2048]{1,0:T(8,128)(2,1)}, u32[]{:S(2)}, u32[]{:S(2)}) %collective-permute-start.24) | collective-permute-done | bytes 524320 | tf_op jit(solution)/shard_map/ppermute | solution.py:230
  365.1 12.0 %attend_back.1 = (bf16[1024,256]{1,0:T(8,128)(2,1)}, f32[1024,128]{1,0:T(8,128)}, f32[1024,128]{1,0:T(8,128)}) custom-call(bf16[1024,384]{1,0:T(8,128)(2,1)} %copy-done.10, bf16[1024,128]{1,0:T(8,128)(2,1)} %get-tuple-element.258.k_ref, bf16[1024,128]{1,0:T(8,128)(2,1)} %get-tuple-element.257.v_ref, bf16[1024,256]{1,0:T(8,128)(2,1)} %pad_maximum_fusion.2.grad_ref, ...), custom_call_target="tpu_custom_call" | custom-call | tf_op jit(solution)/shard_map/attend_back/pallas_call | solution.py:107
  381.9 2.6 convolution_convert_fusion.2
  385.4 2.5 fusion.29
  389.8 4.3 fusion.58
  394.1 5.5 %reduce-scatter.7.cloned.1.call-done = bf16[128,2048]{1,0:T(8,128)(2,1)} async-done(((bf16[512,2048]{1,0:T(8,128)(2,1)}), bf16[128,2048]{1,0:T(8,128)(2,1)}) %reduce-scatter.7.cloned.1.call-update) | async-done | bytes 524304 | tf_op jit(solution)/shard_map/reduce_scatter | solution.py:512
  399.6 4.3 add_convert_fusion.3
  406.9 4.4 all-to-all-start.2
  411.4 3.2 fusion.45
  427.6 3.2 collective-permute-done.28
  430.8 20.8 %collective-permute-done.30 = bf16[128,2048]{1,0:T(8,128)(2,1)} collective-permute-done((bf16[128,2048]{1,0:T(8,128)(2,1)}, bf16[128,2048]{1,0:T(8,128)(2,1)}, u32[]{:S(2)}, u32[]{:S(2)}) %collective-permute-start.30) | collective-permute-done | bytes 524320 | tf_op jit(solution)/shard_map/ppermute | solution.py:230
  455.6 4.7 all-to-all-start.3
  463.4 4.1 all-to-all-done.3
  469.6 3.2 all-to-all-start.4
  486.8 3.5 all-to-all-start.5
  491.3 7.2 %all-to-all-done.5 = bf16[8,64,384]{2,1,0:T(8,128)(2,1)S(1)} async-done(((bf16[8,64,384]{2,1,0:T(8,128)(2,1)}), bf16[8,64,384]{2,1,0:T(8,128)(2,1)S(1)}, u32[]{:S(2)}, u32[]{:S(2)}) %all-to-all-start.5) | async-done | bytes 393248 | tf_op jit(solution)/shard_map/all_to_all | solution.py:576
  (342 shorter events, 132.7 us)
Async XLA Ops:
  7.2 61.7 %all-gather.12.cloned.1.call-start = ((), (), s32[]{:S(2)}) async-start(), calls=%async_computation.17 | async-start | bytes 2211840 | tf_op jit(solution)/shard_map/all_gather | solution.py:401
  24.7 14.8 %collective-permute-start = (bf16[128,2048]{1,0:T(8,128)(2,1)S(1)}, bf16[128,2048]{1,0:T(8,128)(2,1)S(1)}, u32[]{:S(2)}, u32[]{:S(2)}) collective-permute-start(bf16[128,2048]{1,0:T(8,128)(2,1)S(1)} %bitcast.139), channel_id=1, source_target_pairs={{0,8},{4,12},{8,0},{12,4},{16,24},{20,28},{24,16},{28,20},{1,9},{5... | collective-permute-start | bytes 1572872 | tf_op jit(solution)/shard_map/ppermute | solution.py:230
  25.3 24.7 %collective-permute-start.1 = (bf16[128,2048]{1,0:T(8,128)(2,1)S(1)}, bf16[128,2048]{1,0:T(8,128)(2,1)S(1)}, u32[]{:S(2)}, u32[]{:S(2)}) collective-permute-start(bf16[128,2048]{1,0:T(8,128)(2,1)S(1)} %bitcast.140), channel_id=1, source_target_pairs={{0,16},{4,20},{8,24},{12,28},{16,0},{20,4},{24,8},{28,12},{1,17},{... | collective-permute-start | bytes 1572872 | tf_op jit(solution)/shard_map/ppermute | solution.py:230
  25.8 25.0 %collective-permute-start.2 = (bf16[128,2048]{1,0:T(8,128)(2,1)S(1)}, bf16[128,2048]{1,0:T(8,128)(2,1)S(1)}, u32[]{:S(2)}, u32[]{:S(2)}) collective-permute-start(bf16[128,2048]{1,0:T(8,128)(2,1)S(1)} %bitcast.141), channel_id=1, source_target_pairs={{0,24},{4,28},{8,16},{12,20},{16,8},{20,12},{24,0},{28,4},{1,25},{... | collective-permute-start | bytes 1572872 | tf_op jit(solution)/shard_map/ppermute | solution.py:230
  29.0 75.7 %all-gather.6.cloned.1.call-start = ((), (), s32[]{:S(2)}) async-start(), calls=%async_computation.10 | async-start | bytes 1310720 | tf_op jit(solution)/shard_map/all_gather | solution.py:412
  51.6 6.5 %collective-permute-start.3 = (bf16[512,2048]{1,0:T(8,128)(2,1)}, bf16[512,2048]{1,0:T(8,128)(2,1)}, u32[]{:S(2)}, u32[]{:S(2)}) collective-permute-start(bf16[512,2048]{1,0:T(8,128)(2,1)} %constant_dynamic-update-slice_fusion), channel_id=1, source_target_pairs={{0,4},{4,0},{8,12},{12,8},{16,20},{20,16},{24,28},{28,24},{1,5},{5... | collective-permute-start | bytes 6291464 | tf_op jit(solution)/shard_map/ppermute | solution.py:230
  54.6 48.9 %collective-permute-start.7 = (bf16[256,2048]{1,0:T(8,128)(2,1)}, bf16[256,2048]{1,0:T(8,128)(2,1)}, u32[]{:S(2)}, u32[]{:S(2)}) collective-permute-start(bf16[256,2048]{1,0:T(8,128)(2,1)} %param.30), channel_id=1, source_target_pairs={{0,24},{4,28},{8,16},{12,20},{16,8},{20,12},{24,0},{28,4},{1,25},{... | collective-permute-start | bytes 3145736 | tf_op jit(solution)/shard_map/ppermute | solution.py:230
  55.0 48.6 %collective-permute-start.6 = (bf16[256,2048]{1,0:T(8,128)(2,1)}, bf16[256,2048]{1,0:T(8,128)(2,1)}, u32[]{:S(2)}, u32[]{:S(2)}) collective-permute-start(bf16[256,2048]{1,0:T(8,128)(2,1)} %param.30), channel_id=1, source_target_pairs={{0,16},{4,20},{8,24},{12,28},{16,0},{20,4},{24,8},{28,12},{1,17},{... | collective-permute-start | bytes 3145736 | tf_op jit(solution)/shard_map/ppermute | solution.py:230
  57.3 46.4 %collective-permute-start.5 = (bf16[256,2048]{1,0:T(8,128)(2,1)}, bf16[256,2048]{1,0:T(8,128)(2,1)}, u32[]{:S(2)}, u32[]{:S(2)}) collective-permute-start(bf16[256,2048]{1,0:T(8,128)(2,1)} %param.30), channel_id=1, source_target_pairs={{0,8},{4,12},{8,0},{12,4},{16,24},{20,28},{24,16},{28,20},{1,9},{5... | collective-permute-start | bytes 3145736 | tf_op jit(solution)/shard_map/ppermute | solution.py:230
  83.2 39.0 %all-to-all-start.1 = ((bf16[8,64,1024]{2,1,0:T(8,128)(2,1)}), bf16[8,64,1024]{2,1,0:T(8,128)(2,1)}, u32[]{:S(2)}, u32[]{:S(2)}) async-start(bf16[8,64,1024]{2,1,0:T(8,128)(2,1)} %reshape.410), calls=%async_computation.1 | async-start | bytes 2097152 | tf_op jit(solution)/shard_map/all_to_all | solution.py:419
  87.4 83.8 %all-gather.8.cloned.1.call-start = ((), (), s32[]{:S(2)}) async-start(), calls=%async_computation.11 | async-start | bytes 2621440 | tf_op jit(solution)/shard_map/all_gather | solution.py:413
  92.3 1.6 collective-permute-start.4
  125.5 14.3 %collective-permute-start.8 = (bf16[512,2048]{1,0:T(8,128)(2,1)}, bf16[512,2048]{1,0:T(8,128)(2,1)}, u32[]{:S(2)}, u32[]{:S(2)}) collective-permute-start(bf16[512,2048]{1,0:T(8,128)(2,1)} %convolution_convert_fusion.1), channel_id=1, source_target_pairs={{0,4},{4,0},{8,12},{12,8},{16,20},{20,16},{24,28},{28,24},{1,5},{5... | collective-permute-start | bytes 6291464 | tf_op jit(solution)/shard_map/ppermute | solution.py:230
  125.8 42.3 %copy-start.36 = (f32[128]{0:T(128)}, f32[128]{0:T(128)S(1)}, u32[]{:S(2)}) copy-start(f32[128]{0:T(128)S(1)} %broadcast_multiply_fusion.4) | copy-start | bytes 1540
  125.9 101.6 %all-gather.10.cloned.1.call-start = ((), (), s32[]{:S(2)}) async-start(), calls=%async_computation.12 | async-start | bytes 5242880 | tf_op jit(solution)/shard_map/all_gather | solution.py:468
  141.7 15.8 %collective-permute-start.11 = (bf16[128,2048]{1,0:T(8,128)(2,1)S(1)}, bf16[128,2048]{1,0:T(8,128)(2,1)S(1)}, u32[]{:S(2)}, u32[]{:S(2)}) collective-permute-start(bf16[128,2048]{1,0:T(8,128)(2,1)S(1)} %get-tuple-element.251), channel_id=1, source_target_pairs={{0,24},{4,28},{8,16},{12,20},{16,8},{20,12},{24,0},{28,4},{1,25},{... | collective-permute-start | bytes 1572872 | tf_op jit(solution)/shard_map/ppermute | solution.py:230
  144.2 24.0 %collective-permute-start.9 = (bf16[128,2048]{1,0:T(8,128)(2,1)S(1)}, bf16[128,2048]{1,0:T(8,128)(2,1)S(1)}, u32[]{:S(2)}, u32[]{:S(2)}) collective-permute-start(bf16[128,2048]{1,0:T(8,128)(2,1)S(1)} %get-tuple-element.250), channel_id=1, source_target_pairs={{0,8},{4,12},{8,0},{12,4},{16,24},{20,28},{24,16},{28,20},{1,9},{5... | collective-permute-start | bytes 1572872 | tf_op jit(solution)/shard_map/ppermute | solution.py:230
  144.7 23.4 %collective-permute-start.10 = (bf16[128,2048]{1,0:T(8,128)(2,1)S(1)}, bf16[128,2048]{1,0:T(8,128)(2,1)S(1)}, u32[]{:S(2)}, u32[]{:S(2)}) collective-permute-start(bf16[128,2048]{1,0:T(8,128)(2,1)S(1)} %get-tuple-element.252), channel_id=1, source_target_pairs={{0,16},{4,20},{8,24},{12,28},{16,0},{20,4},{24,8},{28,12},{1,17},{... | collective-permute-start | bytes 1572872 | tf_op jit(solution)/shard_map/ppermute | solution.py:230
  171.2 188.3 %reduce-scatter.5.cloned.1.call-start = ((), (), s32[]{:S(2)}) async-start(), calls=%async_computation.13 | async-start | bytes 5242880 | tf_op jit(solution)/shard_map/reduce_scatter | solution.py:485
  171.3 8.0 %collective-permute-start.14 = (bf16[512,2048]{1,0:T(8,128)(2,1)}, bf16[512,2048]{1,0:T(8,128)(2,1)S(1)}, u32[]{:S(2)}, u32[]{:S(2)}) collective-permute-start(bf16[512,2048]{1,0:T(8,128)(2,1)} %all-gather.8.cloned.1.call-done.a_ref.b0_ref), channel_id=1, source_target_pairs={{0,4},{4,0},{8,12},{12,8},{16,20},{20,16},{24,28},{28,24},{1,5},{5... | collective-permute-start | bytes 6291464 | tf_op jit(solution)/shard_map/ppermute | solution.py:230
  171.4 15.1 %collective-permute-start.13 = (bf16[128,2048]{1,0:T(8,128)(2,1)}, bf16[128,2048]{1,0:T(8,128)(2,1)}, u32[]{:S(2)}, u32[]{:S(2)}) collective-permute-start(bf16[128,2048]{1,0:T(8,128)(2,1)} %add_convert_fusion.8), channel_id=1, source_target_pairs={{0,3},{1,0},{2,1},{3,2},{4,7},{5,4},{6,5},{7,6},{8,11},{9,8},{10,9... | collective-permute-start | bytes 1572872 | tf_op jit(solution)/shard_map/ppermute | solution.py:282
  171.5 25.8 %collective-permute-start.12 = (bf16[128,2048]{1,0:T(8,128)(2,1)}, bf16[128,2048]{1,0:T(8,128)(2,1)}, u32[]{:S(2)}, u32[]{:S(2)}) collective-permute-start(bf16[128,2048]{1,0:T(8,128)(2,1)} %add_convert_fusion.8), channel_id=1, source_target_pairs={{0,1},{1,2},{2,3},{3,0},{4,5},{5,6},{6,7},{7,4},{8,9},{9,10},{10,1... | collective-permute-start | bytes 1572872 | tf_op jit(solution)/shard_map/ppermute | solution.py:282
  197.3 25.8 %collective-permute-start.15 = (bf16[128,2048]{1,0:T(8,128)(2,1)}, bf16[128,2048]{1,0:T(8,128)(2,1)S(1)}, u32[]{:S(2)}, u32[]{:S(2)}) collective-permute-start(bf16[128,2048]{1,0:T(8,128)(2,1)} %add_convert_fusion.8), channel_id=1, source_target_pairs={{0,2},{1,3},{2,0},{3,1},{4,6},{5,7},{6,4},{7,5},{8,10},{9,11},{10,... | collective-permute-start | bytes 1572872 | tf_op jit(solution)/shard_map/ppermute | solution.py:282
  223.1 4.4 collective-permute-start.16
  245.2 4.7 collective-permute-start.17
  253.4 26.4 %collective-permute-start.19 = (bf16[128,2048]{1,0:T(8,128)(2,1)}, bf16[128,2048]{1,0:T(8,128)(2,1)}, u32[]{:S(2)}, u32[]{:S(2)}) collective-permute-start(bf16[128,2048]{1,0:T(8,128)(2,1)} %get-tuple-element.247), channel_id=1, source_target_pairs={{0,1},{1,2},{2,3},{3,0},{4,5},{5,6},{6,7},{7,4},{8,9},{9,10},{10,1... | collective-permute-start | bytes 1572872 | tf_op jit(solution)/shard_map/ppermute | solution.py:282
  253.4 26.4 %collective-permute-start.18 = (bf16[128,2048]{1,0:T(8,128)(2,1)}, bf16[128,2048]{1,0:T(8,128)(2,1)}, u32[]{:S(2)}, u32[]{:S(2)}) collective-permute-start(bf16[128,2048]{1,0:T(8,128)(2,1)} %get-tuple-element.248), channel_id=1, source_target_pairs={{0,3},{1,0},{2,1},{3,2},{4,7},{5,4},{6,5},{7,6},{8,11},{9,8},{10,9... | collective-permute-start | bytes 1572872 | tf_op jit(solution)/shard_map/ppermute | solution.py:282
  279.8 119.7 %reduce-scatter.7.cloned.1.call-start = ((), (), s32[]{:S(2)}) async-start(), calls=%async_computation.14 | async-start | bytes 2621440 | tf_op jit(solution)/shard_map/reduce_scatter | solution.py:512
  280.3 30.7 %collective-permute-start.21 = (bf16[512,2048]{1,0:T(8,128)(2,1)}, bf16[512,2048]{1,0:T(8,128)(2,1)}, u32[]{:S(2)}, u32[]{:S(2)}) collective-permute-start(bf16[512,2048]{1,0:T(8,128)(2,1)} %multiply.79), channel_id=1, source_target_pairs={{0,4},{4,0},{8,12},{12,8},{16,20},{20,16},{24,28},{28,24},{1,5},{5... | collective-permute-start | bytes 6291464 | tf_op jit(solution)/shard_map/ppermute | solution.py:230
  280.4 26.5 %collective-permute-start.20 = (bf16[128,2048]{1,0:T(8,128)(2,1)}, bf16[128,2048]{1,0:T(8,128)(2,1)}, u32[]{:S(2)}, u32[]{:S(2)}) collective-permute-start(bf16[128,2048]{1,0:T(8,128)(2,1)} %get-tuple-element.168), channel_id=1, source_target_pairs={{0,2},{1,3},{2,0},{3,1},{4,6},{5,7},{6,4},{7,5},{8,10},{9,11},{10,... | collective-permute-start | bytes 1572872 | tf_op jit(solution)/shard_map/ppermute | solution.py:282
  315.9 25.8 %collective-permute-start.22 = (bf16[128,2048]{1,0:T(8,128)(2,1)S(1)}, bf16[128,2048]{1,0:T(8,128)(2,1)}, u32[]{:S(2)}, u32[]{:S(2)}) collective-permute-start(bf16[128,2048]{1,0:T(8,128)(2,1)S(1)} %get-tuple-element.182), channel_id=1, source_target_pairs={{0,8},{4,12},{8,0},{12,4},{16,24},{20,28},{24,16},{28,20},{1,9},{5... | collective-permute-start | bytes 1572872 | tf_op jit(solution)/shard_map/ppermute | solution.py:230
  317.4 26.2 %collective-permute-start.23 = (bf16[128,2048]{1,0:T(8,128)(2,1)S(1)}, bf16[128,2048]{1,0:T(8,128)(2,1)}, u32[]{:S(2)}, u32[]{:S(2)}) collective-permute-start(bf16[128,2048]{1,0:T(8,128)(2,1)S(1)} %get-tuple-element.182), channel_id=1, source_target_pairs={{0,16},{4,20},{8,24},{12,28},{16,0},{20,4},{24,8},{28,12},{1,17},{... | collective-permute-start | bytes 1572872 | tf_op jit(solution)/shard_map/ppermute | solution.py:230
  318.7 34.5 %collective-permute-start.24 = (bf16[128,2048]{1,0:T(8,128)(2,1)S(1)}, bf16[128,2048]{1,0:T(8,128)(2,1)}, u32[]{:S(2)}, u32[]{:S(2)}) collective-permute-start(bf16[128,2048]{1,0:T(8,128)(2,1)S(1)} %get-tuple-element.182), channel_id=1, source_target_pairs={{0,24},{4,28},{8,16},{12,20},{16,8},{20,12},{24,0},{28,4},{1,25},{... | collective-permute-start | bytes 1572872 | tf_op jit(solution)/shard_map/ppermute | solution.py:230
  320.2 153.9 %reduce-scatter.9.cloned.1.call-start = ((), (), s32[]{:S(2)}) async-start(), calls=%async_computation.15 | async-start | bytes 5242880 | tf_op jit(solution)/shard_map/reduce_scatter | solution.py:485
  355.1 4.5 collective-permute-start.25
  378.4 1.6 collective-permute-start.26
  384.5 9.7 %collective-permute-start.27 = (bf16[512,2048]{1,0:T(8,128)(2,1)}, bf16[512,2048]{1,0:T(8,128)(2,1)}, u32[]{:S(2)}, u32[]{:S(2)}) collective-permute-start(bf16[512,2048]{1,0:T(8,128)(2,1)} %convolution_convert_fusion.2), channel_id=1, source_target_pairs={{0,4},{4,0},{8,12},{12,8},{16,20},{20,16},{24,28},{28,24},{1,5},{5... | collective-permute-start | bytes 6291464 | tf_op jit(solution)/shard_map/ppermute | solution.py:230
  403.9 23.7 %collective-permute-start.29 = (bf16[128,2048]{1,0:T(8,128)(2,1)}, bf16[128,2048]{1,0:T(8,128)(2,1)}, u32[]{:S(2)}, u32[]{:S(2)}) collective-permute-start(bf16[128,2048]{1,0:T(8,128)(2,1)} %get-tuple-element.242), channel_id=1, source_target_pairs={{0,16},{4,20},{8,24},{12,28},{16,0},{20,4},{24,8},{28,12},{1,17},{... | collective-permute-start | bytes 1572872 | tf_op jit(solution)/shard_map/ppermute | solution.py:230
  405.4 25.4 %collective-permute-start.28 = (bf16[128,2048]{1,0:T(8,128)(2,1)}, bf16[128,2048]{1,0:T(8,128)(2,1)}, u32[]{:S(2)}, u32[]{:S(2)}) collective-permute-start(bf16[128,2048]{1,0:T(8,128)(2,1)} %get-tuple-element.244), channel_id=1, source_target_pairs={{0,8},{4,12},{8,0},{12,4},{16,24},{20,28},{24,16},{28,20},{1,9},{5... | collective-permute-start | bytes 1572872 | tf_op jit(solution)/shard_map/ppermute | solution.py:230
  406.9 47.2 %all-to-all-start.2 = ((bf16[8,64,1024]{2,1,0:T(8,128)(2,1)}), bf16[8,64,1024]{2,1,0:T(8,128)(2,1)}, u32[]{:S(2)}, u32[]{:S(2)}) async-start(bf16[8,64,1024]{2,1,0:T(8,128)(2,1)} %bitcast.164), calls=%async_computation.4 | async-start | bytes 2097152 | tf_op jit(solution)/shard_map/all_to_all | solution.py:541
  417.6 34.0 %collective-permute-start.30 = (bf16[128,2048]{1,0:T(8,128)(2,1)}, bf16[128,2048]{1,0:T(8,128)(2,1)}, u32[]{:S(2)}, u32[]{:S(2)}) collective-permute-start(bf16[128,2048]{1,0:T(8,128)(2,1)} %get-tuple-element.202), channel_id=1, source_target_pairs={{0,24},{4,28},{8,16},{12,20},{16,8},{20,12},{24,0},{28,4},{1,25},{... | collective-permute-start | bytes 1572872 | tf_op jit(solution)/shard_map/ppermute | solution.py:230
  421.7 32.4 %collective-permute-start.32 = (bf16[512,384]{1,0:T(8,128)(2,1)}, bf16[512,384]{1,0:T(8,128)(2,1)}, u32[]{:S(2)}, u32[]{:S(2)}) collective-permute-start(bf16[512,384]{1,0:T(8,128)(2,1)} %get-tuple-element.253), channel_id=1, source_target_pairs={{0,1},{1,2},{2,3},{3,0},{4,5},{5,6},{6,7},{7,4},{8,9},{9,10},{10,1... | collective-permute-start | bytes 1179656 | tf_op jit(solution)/shard_map/ppermute | solution.py:282
  423.7 30.4 %collective-permute-start.31 = (bf16[512,384]{1,0:T(8,128)(2,1)}, bf16[512,384]{1,0:T(8,128)(2,1)}, u32[]{:S(2)}, u32[]{:S(2)}) collective-permute-start(bf16[512,384]{1,0:T(8,128)(2,1)} %get-tuple-element.255), channel_id=1, source_target_pairs={{0,3},{1,0},{2,1},{3,2},{4,7},{5,4},{6,5},{7,6},{8,11},{9,8},{10,9... | collective-permute-start | bytes 1179656 | tf_op jit(solution)/shard_map/ppermute | solution.py:282
  455.6 11.9 %all-to-all-start.3 = ((f32[8,8,512]{2,1,0:T(8,128)}), f32[8,8,512]{2,1,0:T(8,128)S(1)}, u32[]{:S(2)}, u32[]{:S(2)}) async-start(f32[8,8,512]{2,1,0:T(8,128)} %pad_maximum_fusion.5), calls=%async_computation.5 | async-start | bytes 262144 | tf_op jit(solution)/shard_map/all_to_all | solution.py:593
  460.3 24.3 %collective-permute-start.33 = (bf16[512,384]{1,0:T(8,128)(2,1)}, bf16[512,384]{1,0:T(8,128)(2,1)}, u32[]{:S(2)}, u32[]{:S(2)}) collective-permute-start(bf16[512,384]{1,0:T(8,128)(2,1)} %get-tuple-element.212), channel_id=1, source_target_pairs={{0,2},{1,3},{2,0},{3,1},{4,6},{5,7},{6,4},{7,5},{8,10},{9,11},{10,... | collective-permute-start | bytes 1179656 | tf_op jit(solution)/shard_map/ppermute | solution.py:282
  469.6 13.7 %all-to-all-start.4 = ((f32[4,1,512]{2,1,0:T(1,128)}), f32[4,1,512]{2,1,0:T(1,128)S(1)}, u32[]{:S(2)}, u32[]{:S(2)}) async-start(f32[4,1,512]{2,1,0:T(1,128)} %reshape.475), calls=%async_computation.6 | async-start | bytes 16384 | tf_op jit(solution)/shard_map/all_to_all | solution.py:603
  472.9 30.8 %reduce-scatter.11.cloned.1.call-start = ((), (), s32[]{:S(2)}) async-start(), calls=%async_computation.16 | async-start | bytes 1310720 | tf_op jit(solution)/shard_map/reduce_scatter | solution.py:597
  486.8 11.7 %all-to-all-start.5 = ((bf16[8,64,384]{2,1,0:T(8,128)(2,1)}), bf16[8,64,384]{2,1,0:T(8,128)(2,1)S(1)}, u32[]{:S(2)}, u32[]{:S(2)}) async-start(bf16[8,64,384]{2,1,0:T(8,128)(2,1)} %bitcast.62), calls=%async_computation.7 | async-start | bytes 786432 | tf_op jit(solution)/shard_map/all_to_all | solution.py:576
  (56 other events, 596.4 us)
Sparse Core Ops, SparseCore 0:
  29.2 39.6 all-gather.11
  72.7 31.9 all-gather.5
  126.0 44.1 all-gather.7
  171.8 51.4 all-gather.9
  280.0 63.1 reduce-scatter.4
  345.9 53.5 reduce-scatter.6
  402.5 71.5 reduce-scatter.8
  476.6 27.0 reduce-scatter.10

commit v5 on v4

--- a/solution.py
+++ b/solution.py
@@ -405,17 +405,17 @@
     own_rows = hidden_own.astype(F32)
     upstream = jnp.where(live, upstream.astype(F32), 0.0)
     grad_mlp_own = upstream.astype(BF)
-    attn_all, row_halves, grad_mlp_own, proj_own, up_own = stage(
-        attn_all, row_halves, grad_mlp_own, proj_weight, up_weight
+    up_parts = (
+        up_weight.reshape(wrows, chips, 2 * depth, frows)
+        .transpose(2, 0, 1, 3)
+        .reshape(2 * depth, wrows, chips * frows)
+    )
+    attn_all, row_halves, grad_mlp_own, proj_own, up_parts = stage(
+        attn_all, row_halves, grad_mlp_own, proj_weight, up_parts
     )
 
     proj_local = lax.all_gather(proj_own, "fsdp", axis=0, tiled=True)
     mlp_rows = lax.all_gather(grad_mlp_own, "fsdp", axis=0, tiled=True)
-    up_parts = (
-        up_own.reshape(wrows, chips, 2 * depth, frows)
-        .transpose(2, 0, 1, 3)
-        .reshape(2 * depth, wrows, chips * frows)
-    )
     up_parts = lax.all_to_all(
         up_parts, BOTH, 0, 0, tiled=True, axis_index_groups=chip_devices()
     ).reshape(2 * depth * wrows, chips * frows)
@@ -535,7 +535,7 @@
     mixed_halves = grad_mixed[: total // 2], grad_mixed[total // 2 :]
     proj_term = plain_over_rows(attended_halves, branch_halves)
     one_sums = core_sum(mixed_halves, qkv_local, 1)
-    one_sums, proj_term, out_sum = stage(one_sums, proj_term, out_sum)
+    one_sums, proj_term = stage(one_sums, proj_term)
     one_parts = plane_parts(one_sums)
     up_grad = stage(up_grad, one_parts)[0]
     up_grad = lax.all_to_all(
@@ -558,9 +558,9 @@
     scaled_one, inverse_one = normalize(own_rows)
     gain_one_term = jnp.sum(grad_one * scaled_one, 0)
     shift_one_term = jnp.sum(grad_one, 0)
-    held = (grad_one, qkv_term, qkv_near, up_grad, proj_term)
+    held = (grad_one, qkv_term, qkv_near, up_grad, proj_term, out_sum)
     gain_one_term, shift_one_term, held = stage(gain_one_term, shift_one_term, held)
-    grad_one, qkv_term, qkv_near, up_grad, proj_term = held
+    grad_one, qkv_term, qkv_near, up_grad, proj_term, out_sum = held
 
     result = middle + out_sum.astype(F32) + dbias
     layer_out = jnp.where(live, result, 0.0).astype(BF)

time: 523 us -> 516 us (0.987)
  other arithmetic: 57.1 us -> 51.1 us
  waiting for transfers between devices: 200 us -> 194 us
  starting transfers between devices: 63.4 us -> 68.8 us
    all_to_all x1, waiting for transfers between devices: 17.5 us -> 4.36 us  [body(): lax.all_to_all(up_parts, BOTH, 0, 0, tiled=True, axis_index_groups=chip_d...]
    all_gather x1, waiting for transfers between devices: 1.11 us -> 12.1 us  [body(): proj_local = lax.all_gather(proj_own, 'fsdp', axis=0, tiled=True)]
    reduce_scatter x2, waiting for transfers between devices: 1.26 us -> 10.8 us  [chip_sum(): lax.psum_scatter(term, 'ctx', scatter_dimension=0, tiled=True, axis_index...]
    reduce_scatter x1, waiting for transfers between devices: 5.46 us -> 0.01 us  [body(): lax.psum_scatter(out_term, 'fsdp', scatter_dimension=0, tiled=True)]
    unnamed x125 -> x109, local copies, waits for them, and re-layouts: 14 us -> 14.9 us
  transfers between devices with their start and end apart: 47 -> 47, of which waited for: 25 -> 22; matrix products, arithmetic and copies ran while one was open for 24% -> 23% of each run, Pallas kernels for 12% -> 13%
where the time goes in v5:
time: 516 us; the launch traced here: 506 us
  waiting for transfers between devices  194 us (38%)
  Pallas kernels  75 us (15%)
  starting transfers between devices  68.8 us (13%)
  other arithmetic  51.1 us (10%)
  local copies, waits for them, and re-layouts  48.2 us (9%)
  matrix products  38.1 us (7%)
  between operations  16.1 us (3%)
  blocking collectives  13.9 us (3%)
    ppermute x25, waiting for transfers between devices, exchange(): return lax.ppermute(value, 'ctx', [(i, i ^ mask) for i in range(count)])  100 us
    ppermute x9, waiting for transfers between devices, turned(): lax.ppermute(value, 'fsdp', [(i, (i + by) % depth) for i in range(depth)])  50.7 us
    dot_general x14, matrix products, dot(): lax.dot_general(a, b, (((da,), (db,)), ((), ())), preferred_element_type=...  38.1 us
    pallas_call x4, Pallas kernels, multiply(): call(functools.partial(multiply_kernel, dim), (columns // tile,), [pl.Blo...  24.1 us
    ppermute x25, starting transfers between devices, exchange(): return lax.ppermute(value, 'ctx', [(i, i ^ mask) for i in range(count)])  19.7 us
    pallas_call x2, Pallas kernels, dot_over_rows(): call(over_rows_kernel, (height // tile,), [left, left, right, right], pl....  18.8 us
    ppermute x9, starting transfers between devices, turned(): lax.ppermute(value, 'fsdp', [(i, (i + by) % depth) for i in range(depth)])  17.6 us
    unnamed x109, local copies, waits for them, and re-layouts  14.9 us
  transfers between devices with their start and end apart: 47, of which 22 were waited for; matrix products, arithmetic and copies ran while one was open for 23% of the time, Pallas kernels for 13%

profile of v5, /device:TPU:0, one launch (start us, length us, event | category | flops | bytes accessed | tf_op | source)
XLA Modules:
  0.0 505.5 jit_solution(9699155795643893981)
XLA Ops:
  10.8 13.9 %all_to_all.30 = bf16[8,72,384]{2,1,0:T(8,128)(2,1)} all-to-all(bf16[8,72,384]{2,1,0:T(8,128)(2,1)S(1)} %copy.94), channel_id=1, replica_groups=mesh['ctx'=8,'fsdp'=4] {'ctx'}, dimensions={0} | all-to-all | bytes 884736 | tf_op jit(solution)/shard_map/all_to_all | solution.py:398
  29.1 10.4 %collective-permute-done = bf16[128,2048]{1,0:T(8,128)(2,1)S(1)} collective-permute-done((bf16[128,2048]{1,0:T(8,128)(2,1)S(1)}, bf16[128,2048]{1,0:T(8,128)(2,1)S(1)}, u32[]{:S(2)}, u32[]{:S(2)}) %collective-permute-start) | collective-permute-done | bytes 524320 | tf_op jit(solution)/shard_map/ppermute | solution.py:230
  40.4 9.6 %collective-permute-done.1 = bf16[128,2048]{1,0:T(8,128)(2,1)S(1)} collective-permute-done((bf16[128,2048]{1,0:T(8,128)(2,1)S(1)}, bf16[128,2048]{1,0:T(8,128)(2,1)S(1)}, u32[]{:S(2)}, u32[]{:S(2)}) %collective-permute-start.1) | collective-permute-done | bytes 524320 | tf_op jit(solution)/shard_map/ppermute | solution.py:230
  60.3 8.6 %all-gather.12.cloned.1.call-done = bf16[32,72,384]{2,1,0:T(8,128)(2,1)} async-done(((bf16[8,72,384]{2,1,0:T(8,128)(2,1)}), bf16[32,72,384]{2,1,0:T(8,128)(2,1)}) %all-gather.12.cloned.1.call-update) | async-done | bytes 1769488 | tf_op jit(solution)/shard_map/all_gather | solution.py:401
  69.8 2.7 slice.221
  72.6 3.0 convert_reduce_fusion
  78.6 4.2 all-to-all-start.1
  85.4 3.1 fusion.47
  92.6 8.7 %attend.1 = bf16[1024,256]{1,0:T(8,128)(2,1)} custom-call(bf16[1024,384]{1,0:T(8,128)(2,1)} %copy-done.10, bf16[1024,128]{1,0:T(8,128)(2,1)} %get-tuple-element.258.k_ref, bf16[1024,128]{1,0:T(8,128)(2,1)} %get-tuple-element.257.v_ref, s32[1024,1]{1,0:T(8,128)} %broadcast_minimum_fusion.row_limit_ref, s32[1,1024]{1,0:T(1,128)} %bitcast.171), custom_call_target="tpu_custom_call" | custom-call | tf_op jit(solution)/shard_map/attend/pallas_call | solution.py:61
  101.3 4.5 collective-permute-done.6
  105.8 12.1 %all-gather.6.cloned.1.call-done = bf16[256,2048]{1,0:T(8,128)(2,1)} async-done(((bf16[64,2048]{1,0:T(8,128)(2,1)}), bf16[256,2048]{1,0:T(8,128)(2,1)}) %all-gather.6.cloned.1.call-update) | async-done | bytes 1048592 | tf_op jit(solution)/shard_map/all_gather | solution.py:417
  117.9 4.4 all-to-all-done.1
  122.2 3.3 convolution_convert_fusion.1
  125.9 9.9 %all-gather.10.cloned.1.call-start = ((), (), s32[]{:S(2)}) async-start(), calls=%async_computation.12 | async-start | bytes 5242880 | tf_op jit(solution)/shard_map/all_gather | solution.py:468
  148.0 9.5 %collective-permute-done.11 = bf16[128,2048]{1,0:T(8,128)(2,1)S(1)} collective-permute-done((bf16[128,2048]{1,0:T(8,128)(2,1)S(1)}, bf16[128,2048]{1,0:T(8,128)(2,1)S(1)}, u32[]{:S(2)}, u32[]{:S(2)}) %collective-permute-start.11) | collective-permute-done | bytes 524320 | tf_op jit(solution)/shard_map/ppermute | solution.py:230
  157.5 10.7 %collective-permute-done.9 = bf16[128,2048]{1,0:T(8,128)(2,1)S(1)} collective-permute-done((bf16[128,2048]{1,0:T(8,128)(2,1)S(1)}, bf16[128,2048]{1,0:T(8,128)(2,1)S(1)}, u32[]{:S(2)}, u32[]{:S(2)}) %collective-permute-start.9) | collective-permute-done | bytes 524320 | tf_op jit(solution)/shard_map/ppermute | solution.py:230
  173.5 5.8 %multiply.76.g0_ref = f32[512,1024]{1,0:T(8,128)} custom-call(bf16[512,2048]{1,0:T(8,128)(2,1)} %all-gather.8.cloned.1.call-done.a_ref.b0_ref, bf16[1024,2048]{1,0:T(8,128)(2,1)} %bitcast.132), custom_call_target="tpu_custom_call" | custom-call | tf_op jit(solution)/shard_map/multiply/pallas_call | solution.py:157
  180.6 5.8 %multiply.77.g1_ref = f32[512,1024]{1,0:T(8,128)} custom-call(bf16[512,2048]{1,0:T(8,128)(2,1)} %copy-done.11, bf16[1024,2048]{1,0:T(8,128)(2,1)} %bitcast.133), custom_call_target="tpu_custom_call" | custom-call | tf_op jit(solution)/shard_map/multiply/pallas_call | solution.py:157
  186.5 10.8 %collective-permute-done.12 = bf16[128,2048]{1,0:T(8,128)(2,1)} collective-permute-done((bf16[128,2048]{1,0:T(8,128)(2,1)}, bf16[128,2048]{1,0:T(8,128)(2,1)}, u32[]{:S(2)}, u32[]{:S(2)}) %collective-permute-start.12) | collective-permute-done | bytes 524320 | tf_op jit(solution)/shard_map/ppermute | solution.py:282
  201.1 21.9 %collective-permute-done.15 = bf16[128,2048]{1,0:T(8,128)(2,1)S(1)} collective-permute-done((bf16[128,2048]{1,0:T(8,128)(2,1)}, bf16[128,2048]{1,0:T(8,128)(2,1)S(1)}, u32[]{:S(2)}, u32[]{:S(2)}) %collective-permute-start.15) | collective-permute-done | bytes 524320 | tf_op jit(solution)/shard_map/ppermute | solution.py:282
  223.2 4.3 collective-permute-done.16.x1_ref.a1_ref
  227.5 11.4 %hidden_layer.1 = (bf16[512,1024]{1,0:T(8,128)(2,1)}, bf16[512,1024]{1,0:T(8,128)(2,1)}, bf16[512,1024]{1,0:T(8,128)(2,1)}, bf16[512,1024]{1,0:T(8,128)(2,1)}) custom-call(bf16[512,2048]{1,0:T(8,128)(2,1)} %bitcast.137, bf16[512,2048]{1,0:T(8,128)(2,1)} %collective-permute-done.16.x1_ref.a1_ref, bf16[2048,1024]{1,0:T(8,128)(2,1)} %all-gather.10.cloned.1.call-done.w_ref, ...), custom_call_target="tpu_custom_call" | custom-call | tf_op jit(solution)/shard_map/hidden_layer/pallas_call | solution.py:210
  238.9 6.4 %convolution_convert_fusion = bf16[512,2048]{1,0:T(8,128)(2,1)} fusion(bf16[512,1024]{1,0:T(8,128)(2,1)} %get-tuple-element.181.b1_ref, bf16[2048,1024]{1,0:T(8,128)(2,1)} %all-gather.10.cloned.1.call-done.w_ref), kind=kOutput, calls=%fused_computation.18 | convolution fusion | flops 2148532224 | bytes 7340032 | tf_op jit(solution)/shard_map/dot_general | solution.py:22
  245.4 4.6 fusion.57
  249.9 3.4 add_convert_fusion.5
  253.4 3.8 collective-permute-start.18
  257.2 6.0 %multiply.79 = bf16[512,2048]{1,0:T(8,128)(2,1)} custom-call(bf16[512,1024]{1,0:T(8,128)(2,1)} %get-tuple-element.177.a_ref.a1_ref, bf16[1024,2048]{1,0:T(8,128)(2,1)} %bitcast.134), custom_call_target="tpu_custom_call" | custom-call | tf_op jit(solution)/shard_map/multiply/pallas_call | solution.py:157
  263.2 6.4 %multiply.78 = f32[512,2048]{1,0:T(8,128)} custom-call(bf16[512,1024]{1,0:T(8,128)(2,1)} %get-tuple-element.176.a_ref.a0_ref, bf16[1024,2048]{1,0:T(8,128)(2,1)} %bitcast.135), custom_call_target="tpu_custom_call" | custom-call | tf_op jit(solution)/shard_map/multiply/pallas_call | solution.py:157
  269.7 10.1 %over_rows.2 = bf16[2048,1024]{1,0:T(8,128)(2,1)} custom-call(bf16[512,2048]{1,0:T(8,128)(2,1)} %bitcast.138, bf16[512,2048]{1,0:T(8,128)(2,1)} %collective-permute-done.16.x1_ref.a1_ref, bf16[512,1024]{1,0:T(8,128)(2,1)} %get-tuple-element.180.b0_ref, bf16[512,1024]{1,0:T(8,128)(2,1)} %get-tuple-element.181.b1_ref), custom_call_target="tpu_custom_call" | custom-call | tf_op jit(solution)/shard_map/over_rows/pallas_call | solution.py:178
  282.6 8.8 %over_rows.3 = bf16[1024,2048]{1,0:T(8,128)(2,1)} custom-call(bf16[512,1024]{1,0:T(8,128)(2,1)} %get-tuple-element.176.a_ref.a0_ref, bf16[512,1024]{1,0:T(8,128)(2,1)} %get-tuple-element.177.a_ref.a1_ref, bf16[512,2048]{1,0:T(8,128)(2,1)} %all-gather.8.cloned.1.call-done.a_ref.b0_ref, bf16[512,2048]{1,0:T(8,128)(2,1)} %copy-done.11), custom_call_target="tpu_custom_call" | custom-call | tf_op jit(solution)/shard_map/over_rows/pallas_call | solution.py:178
  291.3 15.4 %collective-permute-done.20 = bf16[128,2048]{1,0:T(8,128)(2,1)} collective-permute-done((bf16[128,2048]{1,0:T(8,128)(2,1)}, bf16[128,2048]{1,0:T(8,128)(2,1)}, u32[]{:S(2)}, u32[]{:S(2)}) %collective-permute-start.20) | collective-permute-done | bytes 524320 | tf_op jit(solution)/shard_map/ppermute | solution.py:282
  306.7 2.6 multiply_reduce_fusion
  312.0 3.7 add_convert_fusion
  320.1 21.5 %collective-permute-done.22 = bf16[128,2048]{1,0:T(8,128)(2,1)} collective-permute-done((bf16[128,2048]{1,0:T(8,128)(2,1)S(1)}, bf16[128,2048]{1,0:T(8,128)(2,1)}, u32[]{:S(2)}, u32[]{:S(2)}) %collective-permute-start.22) | collective-permute-done | bytes 524320 | tf_op jit(solution)/shard_map/ppermute | solution.py:230
  345.4 7.7 %collective-permute-done.24 = bf16[128,2048]{1,0:T(8,128)(2,1)} collective-permute-done((bf16[128,2048]{1,0:T(8,128)(2,1)S(1)}, bf16[128,2048]{1,0:T(8,128)(2,1)}, u32[]{:S(2)}, u32[]{:S(2)}) %collective-permute-start.24) | collective-permute-done | bytes 524320 | tf_op jit(solution)/shard_map/ppermute | solution.py:230
  364.9 12.0 %attend_back.1 = (bf16[1024,256]{1,0:T(8,128)(2,1)}, f32[1024,128]{1,0:T(8,128)}, f32[1024,128]{1,0:T(8,128)}) custom-call(bf16[1024,384]{1,0:T(8,128)(2,1)} %copy-done.10, bf16[1024,128]{1,0:T(8,128)(2,1)} %get-tuple-element.258.k_ref, bf16[1024,128]{1,0:T(8,128)(2,1)} %get-tuple-element.257.v_ref, bf16[1024,256]{1,0:T(8,128)(2,1)} %pad_maximum_fusion.2.grad_ref, ...), custom_call_target="tpu_custom_call" | custom-call | tf_op jit(solution)/shard_map/attend_back/pallas_call | solution.py:107
  391.7 3.3 add_convert_fusion.3
  395.9 2.9 collective-permute-start.28
  398.9 4.4 all-to-all-start.2
  403.3 3.2 fusion.45
  418.8 17.9 %collective-permute-done.30 = bf16[128,2048]{1,0:T(8,128)(2,1)} collective-permute-done((bf16[128,2048]{1,0:T(8,128)(2,1)S(1)}, bf16[128,2048]{1,0:T(8,128)(2,1)}, u32[]{:S(2)}, u32[]{:S(2)}) %collective-permute-start.30) | collective-permute-done | bytes 524320 | tf_op jit(solution)/shard_map/ppermute | solution.py:230
  436.6 2.9 fusion.49
  443.6 3.7 all-to-all-start.3
  447.3 4.8 collective-permute-start.33
  454.7 10.8 %reduce-scatter.9.cloned.1.call-done = bf16[256,2048]{1,0:T(8,128)(2,1)} async-done(((bf16[1024,2048]{1,0:T(8,128)(2,1)}), bf16[256,2048]{1,0:T(8,128)(2,1)}) %reduce-scatter.9.cloned.1.call-update) | async-done | bytes 1048592 | tf_op jit(solution)/shard_map/reduce_scatter | solution.py:485
  466.3 5.1 %all-to-all-start.4 = ((f32[4,1,512]{2,1,0:T(1,128)}), f32[4,1,512]{2,1,0:T(1,128)S(1)}, u32[]{:S(2)}, u32[]{:S(2)}) async-start(f32[4,1,512]{2,1,0:T(1,128)} %reshape.475), calls=%async_computation.6 | async-start | bytes 16384 | tf_op jit(solution)/shard_map/all_to_all | solution.py:603
  481.9 3.5 all-to-all-start.5
  486.4 7.2 %all-to-all-done.5 = bf16[8,64,384]{2,1,0:T(8,128)(2,1)S(1)} async-done(((bf16[8,64,384]{2,1,0:T(8,128)(2,1)}), bf16[8,64,384]{2,1,0:T(8,128)(2,1)S(1)}, u32[]{:S(2)}, u32[]{:S(2)}) %all-to-all-start.5) | async-done | bytes 393248 | tf_op jit(solution)/shard_map/all_to_all | solution.py:576
  (326 shorter events, 128.8 us)
Async XLA Ops:
  7.2 61.7 %all-gather.12.cloned.1.call-start = ((), (), s32[]{:S(2)}) async-start(), calls=%async_computation.17 | async-start | bytes 2211840 | tf_op jit(solution)/shard_map/all_gather | solution.py:401
  24.7 14.8 %collective-permute-start = (bf16[128,2048]{1,0:T(8,128)(2,1)S(1)}, bf16[128,2048]{1,0:T(8,128)(2,1)S(1)}, u32[]{:S(2)}, u32[]{:S(2)}) collective-permute-start(bf16[128,2048]{1,0:T(8,128)(2,1)S(1)} %bitcast.139), channel_id=1, source_target_pairs={{0,8},{4,12},{8,0},{12,4},{16,24},{20,28},{24,16},{28,20},{1,9},{5... | collective-permute-start | bytes 1572872 | tf_op jit(solution)/shard_map/ppermute | solution.py:230
  25.3 24.7 %collective-permute-start.1 = (bf16[128,2048]{1,0:T(8,128)(2,1)S(1)}, bf16[128,2048]{1,0:T(8,128)(2,1)S(1)}, u32[]{:S(2)}, u32[]{:S(2)}) collective-permute-start(bf16[128,2048]{1,0:T(8,128)(2,1)S(1)} %bitcast.140), channel_id=1, source_target_pairs={{0,16},{4,20},{8,24},{12,28},{16,0},{20,4},{24,8},{28,12},{1,17},{... | collective-permute-start | bytes 1572872 | tf_op jit(solution)/shard_map/ppermute | solution.py:230
  25.8 25.0 %collective-permute-start.2 = (bf16[128,2048]{1,0:T(8,128)(2,1)S(1)}, bf16[128,2048]{1,0:T(8,128)(2,1)S(1)}, u32[]{:S(2)}, u32[]{:S(2)}) collective-permute-start(bf16[128,2048]{1,0:T(8,128)(2,1)S(1)} %bitcast.141), channel_id=1, source_target_pairs={{0,24},{4,28},{8,16},{12,20},{16,8},{20,12},{24,0},{28,4},{1,25},{... | collective-permute-start | bytes 1572872 | tf_op jit(solution)/shard_map/ppermute | solution.py:230
  29.0 88.8 %all-gather.6.cloned.1.call-start = ((), (), s32[]{:S(2)}) async-start(), calls=%async_computation.10 | async-start | bytes 1310720 | tf_op jit(solution)/shard_map/all_gather | solution.py:417
  51.7 8.6 %collective-permute-start.3 = (bf16[512,2048]{1,0:T(8,128)(2,1)}, bf16[512,2048]{1,0:T(8,128)(2,1)}, u32[]{:S(2)}, u32[]{:S(2)}) collective-permute-start(bf16[512,2048]{1,0:T(8,128)(2,1)} %constant_dynamic-update-slice_fusion), channel_id=1, source_target_pairs={{0,4},{4,0},{8,12},{12,8},{16,20},{20,16},{24,28},{28,24},{1,5},{5... | collective-permute-start | bytes 6291464 | tf_op jit(solution)/shard_map/ppermute | solution.py:230
  55.0 254.4 %copy-start.44 = (pred[128]{0:T(512)(128)(4,1)}, pred[128]{0:T(512)(128)(4,1)S(1)}, u32[]{:S(2)}) copy-start(pred[128]{0:T(512)(128)(4,1)S(1)} %add_compare_fusion) | copy-start | bytes 388
  56.8 44.5 %collective-permute-start.7 = (bf16[256,2048]{1,0:T(8,128)(2,1)}, bf16[256,2048]{1,0:T(8,128)(2,1)}, u32[]{:S(2)}, u32[]{:S(2)}) collective-permute-start(bf16[256,2048]{1,0:T(8,128)(2,1)} %param.30), channel_id=1, source_target_pairs={{0,24},{4,28},{8,16},{12,20},{16,8},{20,12},{24,0},{28,4},{1,25},{... | collective-permute-start | bytes 3145736 | tf_op jit(solution)/shard_map/ppermute | solution.py:230
  57.1 48.7 %collective-permute-start.6 = (bf16[256,2048]{1,0:T(8,128)(2,1)}, bf16[256,2048]{1,0:T(8,128)(2,1)}, u32[]{:S(2)}, u32[]{:S(2)}) collective-permute-start(bf16[256,2048]{1,0:T(8,128)(2,1)} %param.30), channel_id=1, source_target_pairs={{0,16},{4,20},{8,24},{12,28},{16,0},{20,4},{24,8},{28,12},{1,17},{... | collective-permute-start | bytes 3145736 | tf_op jit(solution)/shard_map/ppermute | solution.py:230
  59.4 46.4 %collective-permute-start.5 = (bf16[256,2048]{1,0:T(8,128)(2,1)}, bf16[256,2048]{1,0:T(8,128)(2,1)}, u32[]{:S(2)}, u32[]{:S(2)}) collective-permute-start(bf16[256,2048]{1,0:T(8,128)(2,1)} %param.30), channel_id=1, source_target_pairs={{0,8},{4,12},{8,0},{12,4},{16,24},{20,28},{24,16},{28,20},{1,9},{5... | collective-permute-start | bytes 3145736 | tf_op jit(solution)/shard_map/ppermute | solution.py:230
  78.6 43.6 %all-to-all-start.1 = ((bf16[8,64,1024]{2,1,0:T(8,128)(2,1)}), bf16[8,64,1024]{2,1,0:T(8,128)(2,1)}, u32[]{:S(2)}, u32[]{:S(2)}) async-start(bf16[8,64,1024]{2,1,0:T(8,128)(2,1)} %reshape.408), calls=%async_computation.1 | async-start | bytes 2097152 | tf_op jit(solution)/shard_map/all_to_all | solution.py:419
  82.9 88.4 %all-gather.8.cloned.1.call-start = ((), (), s32[]{:S(2)}) async-start(), calls=%async_computation.11 | async-start | bytes 2621440 | tf_op jit(solution)/shard_map/all_gather | solution.py:418
  90.1 1.6 collective-permute-start.4
  125.6 14.3 %collective-permute-start.8 = (bf16[512,2048]{1,0:T(8,128)(2,1)}, bf16[512,2048]{1,0:T(8,128)(2,1)}, u32[]{:S(2)}, u32[]{:S(2)}) collective-permute-start(bf16[512,2048]{1,0:T(8,128)(2,1)} %convolution_convert_fusion.1), channel_id=1, source_target_pairs={{0,4},{4,0},{8,12},{12,8},{16,20},{20,16},{24,28},{28,24},{1,5},{5... | collective-permute-start | bytes 6291464 | tf_op jit(solution)/shard_map/ppermute | solution.py:230
  125.9 101.6 %all-gather.10.cloned.1.call-start = ((), (), s32[]{:S(2)}) async-start(), calls=%async_computation.12 | async-start | bytes 5242880 | tf_op jit(solution)/shard_map/all_gather | solution.py:468
  141.8 15.8 %collective-permute-start.11 = (bf16[128,2048]{1,0:T(8,128)(2,1)S(1)}, bf16[128,2048]{1,0:T(8,128)(2,1)S(1)}, u32[]{:S(2)}, u32[]{:S(2)}) collective-permute-start(bf16[128,2048]{1,0:T(8,128)(2,1)S(1)} %get-tuple-element.251), channel_id=1, source_target_pairs={{0,24},{4,28},{8,16},{12,20},{16,8},{20,12},{24,0},{28,4},{1,25},{... | collective-permute-start | bytes 1572872 | tf_op jit(solution)/shard_map/ppermute | solution.py:230
  144.2 24.0 %collective-permute-start.9 = (bf16[128,2048]{1,0:T(8,128)(2,1)S(1)}, bf16[128,2048]{1,0:T(8,128)(2,1)S(1)}, u32[]{:S(2)}, u32[]{:S(2)}) collective-permute-start(bf16[128,2048]{1,0:T(8,128)(2,1)S(1)} %get-tuple-element.250), channel_id=1, source_target_pairs={{0,8},{4,12},{8,0},{12,4},{16,24},{20,28},{24,16},{28,20},{1,9},{5... | collective-permute-start | bytes 1572872 | tf_op jit(solution)/shard_map/ppermute | solution.py:230
  144.8 23.4 %collective-permute-start.10 = (bf16[128,2048]{1,0:T(8,128)(2,1)S(1)}, bf16[128,2048]{1,0:T(8,128)(2,1)S(1)}, u32[]{:S(2)}, u32[]{:S(2)}) collective-permute-start(bf16[128,2048]{1,0:T(8,128)(2,1)S(1)} %get-tuple-element.252), channel_id=1, source_target_pairs={{0,16},{4,20},{8,24},{12,28},{16,0},{20,4},{24,8},{28,12},{1,17},{... | collective-permute-start | bytes 1572872 | tf_op jit(solution)/shard_map/ppermute | solution.py:230
  171.3 188.1 %reduce-scatter.5.cloned.1.call-start = ((), (), s32[]{:S(2)}) async-start(), calls=%async_computation.13 | async-start | bytes 5242880 | tf_op jit(solution)/shard_map/reduce_scatter | solution.py:485
  171.3 8.0 %collective-permute-start.14 = (bf16[512,2048]{1,0:T(8,128)(2,1)}, bf16[512,2048]{1,0:T(8,128)(2,1)S(1)}, u32[]{:S(2)}, u32[]{:S(2)}) collective-permute-start(bf16[512,2048]{1,0:T(8,128)(2,1)} %all-gather.8.cloned.1.call-done.a_ref.b0_ref), channel_id=1, source_target_pairs={{0,4},{4,0},{8,12},{12,8},{16,20},{20,16},{24,28},{28,24},{1,5},{5... | collective-permute-start | bytes 6291464 | tf_op jit(solution)/shard_map/ppermute | solution.py:230
  171.5 15.1 %collective-permute-start.13 = (bf16[128,2048]{1,0:T(8,128)(2,1)}, bf16[128,2048]{1,0:T(8,128)(2,1)}, u32[]{:S(2)}, u32[]{:S(2)}) collective-permute-start(bf16[128,2048]{1,0:T(8,128)(2,1)} %add_convert_fusion.8), channel_id=1, source_target_pairs={{0,3},{1,0},{2,1},{3,2},{4,7},{5,4},{6,5},{7,6},{8,11},{9,8},{10,9... | collective-permute-start | bytes 1572872 | tf_op jit(solution)/shard_map/ppermute | solution.py:282
  171.5 25.8 %collective-permute-start.12 = (bf16[128,2048]{1,0:T(8,128)(2,1)}, bf16[128,2048]{1,0:T(8,128)(2,1)}, u32[]{:S(2)}, u32[]{:S(2)}) collective-permute-start(bf16[128,2048]{1,0:T(8,128)(2,1)} %add_convert_fusion.8), channel_id=1, source_target_pairs={{0,1},{1,2},{2,3},{3,0},{4,5},{5,6},{6,7},{7,4},{8,9},{9,10},{10,1... | collective-permute-start | bytes 1572872 | tf_op jit(solution)/shard_map/ppermute | solution.py:282
  197.3 25.7 %collective-permute-start.15 = (bf16[128,2048]{1,0:T(8,128)(2,1)}, bf16[128,2048]{1,0:T(8,128)(2,1)S(1)}, u32[]{:S(2)}, u32[]{:S(2)}) collective-permute-start(bf16[128,2048]{1,0:T(8,128)(2,1)} %add_convert_fusion.8), channel_id=1, source_target_pairs={{0,2},{1,3},{2,0},{3,1},{4,6},{5,7},{6,4},{7,5},{8,10},{9,11},{10,... | collective-permute-start | bytes 1572872 | tf_op jit(solution)/shard_map/ppermute | solution.py:282
  223.1 4.4 collective-permute-start.16
  245.2 4.7 collective-permute-start.17
  253.4 26.4 %collective-permute-start.19 = (bf16[128,2048]{1,0:T(8,128)(2,1)}, bf16[128,2048]{1,0:T(8,128)(2,1)}, u32[]{:S(2)}, u32[]{:S(2)}) collective-permute-start(bf16[128,2048]{1,0:T(8,128)(2,1)} %get-tuple-element.247), channel_id=1, source_target_pairs={{0,1},{1,2},{2,3},{3,0},{4,5},{5,6},{6,7},{7,4},{8,9},{9,10},{10,1... | collective-permute-start | bytes 1572872 | tf_op jit(solution)/shard_map/ppermute | solution.py:282
  253.4 26.4 %collective-permute-start.18 = (bf16[128,2048]{1,0:T(8,128)(2,1)}, bf16[128,2048]{1,0:T(8,128)(2,1)}, u32[]{:S(2)}, u32[]{:S(2)}) collective-permute-start(bf16[128,2048]{1,0:T(8,128)(2,1)} %get-tuple-element.248), channel_id=1, source_target_pairs={{0,3},{1,0},{2,1},{3,2},{4,7},{5,4},{6,5},{7,6},{8,11},{9,8},{10,9... | collective-permute-start | bytes 1572872 | tf_op jit(solution)/shard_map/ppermute | solution.py:282
  279.8 159.7 %reduce-scatter.7.cloned.1.call-start = ((), (), s32[]{:S(2)}) async-start(), calls=%async_computation.14 | async-start | bytes 2621440 | tf_op jit(solution)/shard_map/reduce_scatter | solution.py:512
  280.3 30.6 %collective-permute-start.21 = (bf16[512,2048]{1,0:T(8,128)(2,1)}, bf16[512,2048]{1,0:T(8,128)(2,1)}, u32[]{:S(2)}, u32[]{:S(2)}) collective-permute-start(bf16[512,2048]{1,0:T(8,128)(2,1)} %multiply.79), channel_id=1, source_target_pairs={{0,4},{4,0},{8,12},{12,8},{16,20},{20,16},{24,28},{28,24},{1,5},{5... | collective-permute-start | bytes 6291464 | tf_op jit(solution)/shard_map/ppermute | solution.py:230
  280.3 26.4 %collective-permute-start.20 = (bf16[128,2048]{1,0:T(8,128)(2,1)}, bf16[128,2048]{1,0:T(8,128)(2,1)}, u32[]{:S(2)}, u32[]{:S(2)}) collective-permute-start(bf16[128,2048]{1,0:T(8,128)(2,1)} %get-tuple-element.168), channel_id=1, source_target_pairs={{0,2},{1,3},{2,0},{3,1},{4,6},{5,7},{6,4},{7,5},{8,10},{9,11},{10,... | collective-permute-start | bytes 1572872 | tf_op jit(solution)/shard_map/ppermute | solution.py:282
  315.7 25.9 %collective-permute-start.22 = (bf16[128,2048]{1,0:T(8,128)(2,1)S(1)}, bf16[128,2048]{1,0:T(8,128)(2,1)}, u32[]{:S(2)}, u32[]{:S(2)}) collective-permute-start(bf16[128,2048]{1,0:T(8,128)(2,1)S(1)} %get-tuple-element.182), channel_id=1, source_target_pairs={{0,8},{4,12},{8,0},{12,4},{16,24},{20,28},{24,16},{28,20},{1,9},{5... | collective-permute-start | bytes 1572872 | tf_op jit(solution)/shard_map/ppermute | solution.py:230
  317.1 26.3 %collective-permute-start.23 = (bf16[128,2048]{1,0:T(8,128)(2,1)S(1)}, bf16[128,2048]{1,0:T(8,128)(2,1)}, u32[]{:S(2)}, u32[]{:S(2)}) collective-permute-start(bf16[128,2048]{1,0:T(8,128)(2,1)S(1)} %get-tuple-element.182), channel_id=1, source_target_pairs={{0,16},{4,20},{8,24},{12,28},{16,0},{20,4},{24,8},{28,12},{1,17},{... | collective-permute-start | bytes 1572872 | tf_op jit(solution)/shard_map/ppermute | solution.py:230
  318.5 34.5 %collective-permute-start.24 = (bf16[128,2048]{1,0:T(8,128)(2,1)S(1)}, bf16[128,2048]{1,0:T(8,128)(2,1)}, u32[]{:S(2)}, u32[]{:S(2)}) collective-permute-start(bf16[128,2048]{1,0:T(8,128)(2,1)S(1)} %get-tuple-element.182), channel_id=1, source_target_pairs={{0,24},{4,28},{8,16},{12,20},{16,8},{20,12},{24,0},{28,4},{1,25},{... | collective-permute-start | bytes 1572872 | tf_op jit(solution)/shard_map/ppermute | solution.py:230
  320.0 145.5 %reduce-scatter.9.cloned.1.call-start = ((), (), s32[]{:S(2)}) async-start(), calls=%async_computation.15 | async-start | bytes 5242880 | tf_op jit(solution)/shard_map/reduce_scatter | solution.py:485
  354.9 4.5 collective-permute-start.25
  378.2 1.6 collective-permute-start.26
  384.3 7.4 %collective-permute-start.27 = (bf16[512,2048]{1,0:T(8,128)(2,1)}, bf16[512,2048]{1,0:T(8,128)(2,1)}, u32[]{:S(2)}, u32[]{:S(2)}) collective-permute-start(bf16[512,2048]{1,0:T(8,128)(2,1)} %convolution_convert_fusion.2), channel_id=1, source_target_pairs={{0,4},{4,0},{8,12},{12,8},{16,20},{20,16},{24,28},{28,24},{1,5},{5... | collective-permute-start | bytes 6291464 | tf_op jit(solution)/shard_map/ppermute | solution.py:230
  395.0 23.0 %collective-permute-start.29 = (bf16[128,2048]{1,0:T(8,128)(2,1)}, bf16[128,2048]{1,0:T(8,128)(2,1)S(1)}, u32[]{:S(2)}, u32[]{:S(2)}) collective-permute-start(bf16[128,2048]{1,0:T(8,128)(2,1)} %get-tuple-element.242), channel_id=1, source_target_pairs={{0,16},{4,20},{8,24},{12,28},{16,0},{20,4},{24,8},{28,12},{1,17},{... | collective-permute-start | bytes 1572872 | tf_op jit(solution)/shard_map/ppermute | solution.py:230
  395.9 22.0 %collective-permute-start.28 = (bf16[128,2048]{1,0:T(8,128)(2,1)}, bf16[128,2048]{1,0:T(8,128)(2,1)}, u32[]{:S(2)}, u32[]{:S(2)}) collective-permute-start(bf16[128,2048]{1,0:T(8,128)(2,1)} %get-tuple-element.244), channel_id=1, source_target_pairs={{0,8},{4,12},{8,0},{12,4},{16,24},{20,28},{24,16},{28,20},{1,9},{5... | collective-permute-start | bytes 1572872 | tf_op jit(solution)/shard_map/ppermute | solution.py:230
  398.9 43.2 %all-to-all-start.2 = ((bf16[8,64,1024]{2,1,0:T(8,128)(2,1)}), bf16[8,64,1024]{2,1,0:T(8,128)(2,1)}, u32[]{:S(2)}, u32[]{:S(2)}) async-start(bf16[8,64,1024]{2,1,0:T(8,128)(2,1)} %bitcast.46), calls=%async_computation.3 | async-start | bytes 2097152 | tf_op jit(solution)/shard_map/all_to_all | solution.py:541
  409.8 26.8 %collective-permute-start.30 = (bf16[128,2048]{1,0:T(8,128)(2,1)S(1)}, bf16[128,2048]{1,0:T(8,128)(2,1)}, u32[]{:S(2)}, u32[]{:S(2)}) collective-permute-start(bf16[128,2048]{1,0:T(8,128)(2,1)S(1)} %get-tuple-element.199), channel_id=1, source_target_pairs={{0,24},{4,28},{8,16},{12,20},{16,8},{20,12},{24,0},{28,4},{1,25},{... | collective-permute-start | bytes 1572872 | tf_op jit(solution)/shard_map/ppermute | solution.py:230
  410.6 28.9 %collective-permute-start.32 = (bf16[512,384]{1,0:T(8,128)(2,1)}, bf16[512,384]{1,0:T(8,128)(2,1)S(1)}, u32[]{:S(2)}, u32[]{:S(2)}) collective-permute-start(bf16[512,384]{1,0:T(8,128)(2,1)} %get-tuple-element.253), channel_id=1, source_target_pairs={{0,1},{1,2},{2,3},{3,0},{4,5},{5,6},{6,7},{7,4},{8,9},{9,10},{10,1... | collective-permute-start | bytes 1179656 | tf_op jit(solution)/shard_map/ppermute | solution.py:282
  412.6 29.5 %collective-permute-start.31 = (bf16[512,384]{1,0:T(8,128)(2,1)}, bf16[512,384]{1,0:T(8,128)(2,1)S(1)}, u32[]{:S(2)}, u32[]{:S(2)}) collective-permute-start(bf16[512,384]{1,0:T(8,128)(2,1)} %get-tuple-element.255), channel_id=1, source_target_pairs={{0,3},{1,0},{2,1},{3,2},{4,7},{5,4},{6,5},{7,6},{8,11},{9,8},{10,9... | collective-permute-start | bytes 1179656 | tf_op jit(solution)/shard_map/ppermute | solution.py:282
  443.6 11.1 %all-to-all-start.3 = ((f32[8,8,512]{2,1,0:T(8,128)}), f32[8,8,512]{2,1,0:T(8,128)S(1)}, u32[]{:S(2)}, u32[]{:S(2)}) async-start(f32[8,8,512]{2,1,0:T(8,128)} %pad_maximum_fusion.5), calls=%async_computation.5 | async-start | bytes 262144 | tf_op jit(solution)/shard_map/all_to_all | solution.py:593
  447.3 49.5 %reduce-scatter.11.cloned.1.call-start = ((), (), s32[]{:S(2)}) async-start(), calls=%async_computation.16 | async-start | bytes 1310720 | tf_op jit(solution)/shard_map/reduce_scatter | solution.py:597
  447.3 32.7 %collective-permute-start.33 = (bf16[512,384]{1,0:T(8,128)(2,1)}, bf16[512,384]{1,0:T(8,128)(2,1)}, u32[]{:S(2)}, u32[]{:S(2)}) collective-permute-start(bf16[512,384]{1,0:T(8,128)(2,1)} %get-tuple-element.212), channel_id=1, source_target_pairs={{0,2},{1,3},{2,0},{3,1},{4,6},{5,7},{6,4},{7,5},{8,10},{9,11},{10,... | collective-permute-start | bytes 1179656 | tf_op jit(solution)/shard_map/ppermute | solution.py:282
  466.3 12.4 %all-to-all-start.4 = ((f32[4,1,512]{2,1,0:T(1,128)}), f32[4,1,512]{2,1,0:T(1,128)S(1)}, u32[]{:S(2)}, u32[]{:S(2)}) async-start(f32[4,1,512]{2,1,0:T(1,128)} %reshape.475), calls=%async_computation.6 | async-start | bytes 16384 | tf_op jit(solution)/shard_map/all_to_all | solution.py:603
  481.9 11.7 %all-to-all-start.5 = ((bf16[8,64,384]{2,1,0:T(8,128)(2,1)}), bf16[8,64,384]{2,1,0:T(8,128)(2,1)S(1)}, u32[]{:S(2)}, u32[]{:S(2)}) async-start(bf16[8,64,384]{2,1,0:T(8,128)(2,1)} %bitcast.62), calls=%async_computation.7 | async-start | bytes 786432 | tf_op jit(solution)/shard_map/all_to_all | solution.py:576
  (48 other events, 477.8 us)
Sparse Core Ops, SparseCore 0:
  29.2 39.6 all-gather.11
  72.7 45.1 all-gather.5
  126.0 44.1 all-gather.7
  171.9 51.4 all-gather.9
  279.9 63.1 reduce-scatter.4
  346.0 53.2 reduce-scatter.6
  402.2 63.2 reduce-scatter.8
  467.9 27.5 reduce-scatter.10

commit v6 on v4

--- a/solution.py
+++ b/solution.py
@@ -535,7 +535,7 @@
     mixed_halves = grad_mixed[: total // 2], grad_mixed[total // 2 :]
     proj_term = plain_over_rows(attended_halves, branch_halves)
     one_sums = core_sum(mixed_halves, qkv_local, 1)
-    one_sums, proj_term, out_sum = stage(one_sums, proj_term, out_sum)
+    one_sums, proj_term = stage(one_sums, proj_term)
     one_parts = plane_parts(one_sums)
     up_grad = stage(up_grad, one_parts)[0]
     up_grad = lax.all_to_all(
@@ -558,9 +558,9 @@
     scaled_one, inverse_one = normalize(own_rows)
     gain_one_term = jnp.sum(grad_one * scaled_one, 0)
     shift_one_term = jnp.sum(grad_one, 0)
-    held = (grad_one, qkv_term, qkv_near, up_grad, proj_term)
+    held = (grad_one, qkv_term, qkv_near, up_grad, proj_term, out_sum)
     gain_one_term, shift_one_term, held = stage(gain_one_term, shift_one_term, held)
-    grad_one, qkv_term, qkv_near, up_grad, proj_term = held
+    grad_one, qkv_term, qkv_near, up_grad, proj_term, out_sum = held
 
     result = middle + out_sum.astype(F32) + dbias
     layer_out = jnp.where(live, result, 0.0).astype(BF)

time: 523 us -> 516 us (0.987)
  waiting for transfers between devices: 200 us -> 194 us
    reduce_scatter x2, waiting for transfers between devices: 1.26 us -> 11 us  [chip_sum(): lax.psum_scatter(term, 'ctx', scatter_dimension=0, tiled=True, axis_index...]
    ppermute x25, waiting for transfers between devices: 102 us -> 96 us  [exchange(): return lax.ppermute(value, 'ctx', [(i, i ^ mask) for i in range(count)])]
    reduce_scatter x1, waiting for transfers between devices: 5.46 us -> 0.01 us  [body(): lax.psum_scatter(out_term, 'fsdp', scatter_dimension=0, tiled=True)]
    unnamed x125 -> x139, local copies, waits for them, and re-layouts: 14 us -> 15 us
  transfers between devices with their start and end apart: 47 -> 47, of which waited for: 25 -> 21; matrix products, arithmetic and copies ran while one was open for 24% -> 23% of each run, Pallas kernels for 12% -> 13%
where the time goes in v6:
time: 516 us; the launch traced here: 506 us
  waiting for transfers between devices  194 us (38%)
  Pallas kernels  75 us (15%)
  starting transfers between devices  68.6 us (13%)
  other arithmetic  52.5 us (10%)
  local copies, waits for them, and re-layouts  46.9 us (9%)
  matrix products  38.2 us (7%)
  between operations  16.3 us (3%)
  blocking collectives  13.9 us (3%)
    ppermute x25, waiting for transfers between devices, exchange(): return lax.ppermute(value, 'ctx', [(i, i ^ mask) for i in range(count)])  96 us
    ppermute x9, waiting for transfers between devices, turned(): lax.ppermute(value, 'fsdp', [(i, (i + by) % depth) for i in range(depth)])  50.8 us
    dot_general x14, matrix products, dot(): lax.dot_general(a, b, (((da,), (db,)), ((), ())), preferred_element_type=...  38.2 us
    pallas_call x4, Pallas kernels, multiply(): call(functools.partial(multiply_kernel, dim), (columns // tile,), [pl.Blo...  24.1 us
    ppermute x25, starting transfers between devices, exchange(): return lax.ppermute(value, 'ctx', [(i, i ^ mask) for i in range(count)])  19.5 us
    pallas_call x2, Pallas kernels, dot_over_rows(): call(over_rows_kernel, (height // tile,), [left, left, right, right], pl....  18.9 us
    ppermute x9, starting transfers between devices, turned(): lax.ppermute(value, 'fsdp', [(i, (i + by) % depth) for i in range(depth)])  17.6 us
    all_to_all x1, waiting for transfers between devices, body(): lax.all_to_all(up_parts, BOTH, 0, 0, tiled=True, axis_index_groups=chip_d...  17.5 us
  transfers between devices with their start and end apart: 47, of which 21 were waited for; matrix products, arithmetic and copies ran while one was open for 23% of the time, Pallas kernels for 13%

profile of v6, /device:TPU:0, one launch (start us, length us, event | category | flops | bytes accessed | tf_op | source)
XLA Modules:
  0.0 505.7 jit_solution(4248202941682812944)
XLA Ops:
  10.8 13.9 %all_to_all.30 = bf16[8,72,384]{2,1,0:T(8,128)(2,1)} all-to-all(bf16[8,72,384]{2,1,0:T(8,128)(2,1)S(1)} %copy.94), channel_id=1, replica_groups=mesh['ctx'=8,'fsdp'=4] {'ctx'}, dimensions={0} | all-to-all | bytes 884736 | tf_op jit(solution)/shard_map/all_to_all | solution.py:398
  29.1 10.4 %collective-permute-done = bf16[128,2048]{1,0:T(8,128)(2,1)S(1)} collective-permute-done((bf16[128,2048]{1,0:T(8,128)(2,1)S(1)}, bf16[128,2048]{1,0:T(8,128)(2,1)S(1)}, u32[]{:S(2)}, u32[]{:S(2)}) %collective-permute-start) | collective-permute-done | bytes 524320 | tf_op jit(solution)/shard_map/ppermute | solution.py:230
  40.4 9.6 %collective-permute-done.1 = bf16[128,2048]{1,0:T(8,128)(2,1)S(1)} collective-permute-done((bf16[128,2048]{1,0:T(8,128)(2,1)S(1)}, bf16[128,2048]{1,0:T(8,128)(2,1)S(1)}, u32[]{:S(2)}, u32[]{:S(2)}) %collective-permute-start.1) | collective-permute-done | bytes 524320 | tf_op jit(solution)/shard_map/ppermute | solution.py:230
  58.1 10.7 %all-gather.12.cloned.1.call-done = bf16[32,72,384]{2,1,0:T(8,128)(2,1)} async-done(((bf16[8,72,384]{2,1,0:T(8,128)(2,1)}), bf16[32,72,384]{2,1,0:T(8,128)(2,1)}) %all-gather.12.cloned.1.call-update) | async-done | bytes 1769488 | tf_op jit(solution)/shard_map/all_gather | solution.py:401
  69.8 2.7 slice.221
  72.6 3.0 convert_reduce_fusion
  83.2 4.3 all-to-all-start.1
  87.6 3.1 fusion.47
  94.8 8.7 %attend.1 = bf16[1024,256]{1,0:T(8,128)(2,1)} custom-call(bf16[1024,384]{1,0:T(8,128)(2,1)} %copy-done.10, bf16[1024,128]{1,0:T(8,128)(2,1)} %get-tuple-element.258.k_ref, bf16[1024,128]{1,0:T(8,128)(2,1)} %get-tuple-element.257.v_ref, s32[1024,1]{1,0:T(8,128)} %broadcast_minimum_fusion.row_limit_ref, s32[1,1024]{1,0:T(1,128)} %bitcast.171), custom_call_target="tpu_custom_call" | custom-call | tf_op jit(solution)/shard_map/attend/pallas_call | solution.py:61
  104.7 17.5 %all-to-all-done.1 = bf16[8,64,1024]{2,1,0:T(8,128)(2,1)} async-done(((bf16[8,64,1024]{2,1,0:T(8,128)(2,1)}), bf16[8,64,1024]{2,1,0:T(8,128)(2,1)}, u32[]{:S(2)}, u32[]{:S(2)}) %all-to-all-start.1) | async-done | bytes 1048608 | tf_op jit(solution)/shard_map/all_to_all | solution.py:419
  122.2 3.3 convolution_convert_fusion.1
  125.9 9.9 %all-gather.10.cloned.1.call-start = ((), (), s32[]{:S(2)}) async-start(), calls=%async_computation.12 | async-start | bytes 5242880 | tf_op jit(solution)/shard_map/all_gather | solution.py:468
  147.9 9.5 %collective-permute-done.11 = bf16[128,2048]{1,0:T(8,128)(2,1)S(1)} collective-permute-done((bf16[128,2048]{1,0:T(8,128)(2,1)S(1)}, bf16[128,2048]{1,0:T(8,128)(2,1)S(1)}, u32[]{:S(2)}, u32[]{:S(2)}) %collective-permute-start.11) | collective-permute-done | bytes 524320 | tf_op jit(solution)/shard_map/ppermute | solution.py:230
  157.5 10.7 %collective-permute-done.9 = bf16[128,2048]{1,0:T(8,128)(2,1)S(1)} collective-permute-done((bf16[128,2048]{1,0:T(8,128)(2,1)S(1)}, bf16[128,2048]{1,0:T(8,128)(2,1)S(1)}, u32[]{:S(2)}, u32[]{:S(2)}) %collective-permute-start.9) | collective-permute-done | bytes 524320 | tf_op jit(solution)/shard_map/ppermute | solution.py:230
  173.5 5.8 %multiply.76.g0_ref = f32[512,1024]{1,0:T(8,128)} custom-call(bf16[512,2048]{1,0:T(8,128)(2,1)} %all-gather.8.cloned.1.call-done.a_ref.b0_ref, bf16[1024,2048]{1,0:T(8,128)(2,1)} %bitcast.132), custom_call_target="tpu_custom_call" | custom-call | tf_op jit(solution)/shard_map/multiply/pallas_call | solution.py:157
  180.6 5.8 %multiply.77.g1_ref = f32[512,1024]{1,0:T(8,128)} custom-call(bf16[512,2048]{1,0:T(8,128)(2,1)} %copy-done.11, bf16[1024,2048]{1,0:T(8,128)(2,1)} %bitcast.133), custom_call_target="tpu_custom_call" | custom-call | tf_op jit(solution)/shard_map/multiply/pallas_call | solution.py:157
  186.5 10.8 %collective-permute-done.12 = bf16[128,2048]{1,0:T(8,128)(2,1)} collective-permute-done((bf16[128,2048]{1,0:T(8,128)(2,1)}, bf16[128,2048]{1,0:T(8,128)(2,1)}, u32[]{:S(2)}, u32[]{:S(2)}) %collective-permute-start.12) | collective-permute-done | bytes 524320 | tf_op jit(solution)/shard_map/ppermute | solution.py:282
  201.1 21.9 %collective-permute-done.15 = bf16[128,2048]{1,0:T(8,128)(2,1)S(1)} collective-permute-done((bf16[128,2048]{1,0:T(8,128)(2,1)}, bf16[128,2048]{1,0:T(8,128)(2,1)S(1)}, u32[]{:S(2)}, u32[]{:S(2)}) %collective-permute-start.15) | collective-permute-done | bytes 524320 | tf_op jit(solution)/shard_map/ppermute | solution.py:282
  223.2 4.3 collective-permute-done.16.x1_ref.a1_ref
  227.4 11.4 %hidden_layer.1 = (bf16[512,1024]{1,0:T(8,128)(2,1)}, bf16[512,1024]{1,0:T(8,128)(2,1)}, bf16[512,1024]{1,0:T(8,128)(2,1)}, bf16[512,1024]{1,0:T(8,128)(2,1)}) custom-call(bf16[512,2048]{1,0:T(8,128)(2,1)} %bitcast.137, bf16[512,2048]{1,0:T(8,128)(2,1)} %collective-permute-done.16.x1_ref.a1_ref, bf16[2048,1024]{1,0:T(8,128)(2,1)} %all-gather.10.cloned.1.call-done.w_ref, ...), custom_call_target="tpu_custom_call" | custom-call | tf_op jit(solution)/shard_map/hidden_layer/pallas_call | solution.py:210
  238.8 6.3 %convolution_convert_fusion = bf16[512,2048]{1,0:T(8,128)(2,1)} fusion(bf16[512,1024]{1,0:T(8,128)(2,1)} %get-tuple-element.181.b1_ref, bf16[2048,1024]{1,0:T(8,128)(2,1)} %all-gather.10.cloned.1.call-done.w_ref), kind=kOutput, calls=%fused_computation.18 | convolution fusion | flops 2148532224 | bytes 7340032 | tf_op jit(solution)/shard_map/dot_general | solution.py:22
  245.3 4.6 fusion.57
  249.9 3.4 add_convert_fusion.5
  253.3 3.8 collective-permute-start.18
  257.2 6.0 %multiply.79 = bf16[512,2048]{1,0:T(8,128)(2,1)} custom-call(bf16[512,1024]{1,0:T(8,128)(2,1)} %get-tuple-element.177.a_ref.a1_ref, bf16[1024,2048]{1,0:T(8,128)(2,1)} %bitcast.134), custom_call_target="tpu_custom_call" | custom-call | tf_op jit(solution)/shard_map/multiply/pallas_call | solution.py:157
  263.2 6.4 %multiply.78 = f32[512,2048]{1,0:T(8,128)} custom-call(bf16[512,1024]{1,0:T(8,128)(2,1)} %get-tuple-element.176.a_ref.a0_ref, bf16[1024,2048]{1,0:T(8,128)(2,1)} %bitcast.135), custom_call_target="tpu_custom_call" | custom-call | tf_op jit(solution)/shard_map/multiply/pallas_call | solution.py:157
  269.6 10.1 %over_rows.2 = bf16[2048,1024]{1,0:T(8,128)(2,1)} custom-call(bf16[512,2048]{1,0:T(8,128)(2,1)} %bitcast.138, bf16[512,2048]{1,0:T(8,128)(2,1)} %collective-permute-done.16.x1_ref.a1_ref, bf16[512,1024]{1,0:T(8,128)(2,1)} %get-tuple-element.180.b0_ref, bf16[512,1024]{1,0:T(8,128)(2,1)} %get-tuple-element.181.b1_ref), custom_call_target="tpu_custom_call" | custom-call | tf_op jit(solution)/shard_map/over_rows/pallas_call | solution.py:178
  282.5 8.8 %over_rows.3 = bf16[1024,2048]{1,0:T(8,128)(2,1)} custom-call(bf16[512,1024]{1,0:T(8,128)(2,1)} %get-tuple-element.176.a_ref.a0_ref, bf16[512,1024]{1,0:T(8,128)(2,1)} %get-tuple-element.177.a_ref.a1_ref, bf16[512,2048]{1,0:T(8,128)(2,1)} %all-gather.8.cloned.1.call-done.a_ref.b0_ref, bf16[512,2048]{1,0:T(8,128)(2,1)} %copy-done.11), custom_call_target="tpu_custom_call" | custom-call | tf_op jit(solution)/shard_map/over_rows/pallas_call | solution.py:178
  291.3 15.5 %collective-permute-done.20 = bf16[128,2048]{1,0:T(8,128)(2,1)} collective-permute-done((bf16[128,2048]{1,0:T(8,128)(2,1)}, bf16[128,2048]{1,0:T(8,128)(2,1)}, u32[]{:S(2)}, u32[]{:S(2)}) %collective-permute-start.20) | collective-permute-done | bytes 524320 | tf_op jit(solution)/shard_map/ppermute | solution.py:282
  306.9 2.6 multiply_reduce_fusion
  312.1 3.7 add_convert_fusion
  320.2 21.4 %collective-permute-done.22 = bf16[128,2048]{1,0:T(8,128)(2,1)} collective-permute-done((bf16[128,2048]{1,0:T(8,128)(2,1)S(1)}, bf16[128,2048]{1,0:T(8,128)(2,1)}, u32[]{:S(2)}, u32[]{:S(2)}) %collective-permute-start.22) | collective-permute-done | bytes 524320 | tf_op jit(solution)/shard_map/ppermute | solution.py:230
  345.4 7.7 %collective-permute-done.24 = bf16[128,2048]{1,0:T(8,128)(2,1)} collective-permute-done((bf16[128,2048]{1,0:T(8,128)(2,1)S(1)}, bf16[128,2048]{1,0:T(8,128)(2,1)}, u32[]{:S(2)}, u32[]{:S(2)}) %collective-permute-start.24) | collective-permute-done | bytes 524320 | tf_op jit(solution)/shard_map/ppermute | solution.py:230
  365.1 12.0 %attend_back.1 = (bf16[1024,256]{1,0:T(8,128)(2,1)}, f32[1024,128]{1,0:T(8,128)}, f32[1024,128]{1,0:T(8,128)}) custom-call(bf16[1024,384]{1,0:T(8,128)(2,1)} %copy-done.10, bf16[1024,128]{1,0:T(8,128)(2,1)} %get-tuple-element.258.k_ref, bf16[1024,128]{1,0:T(8,128)(2,1)} %get-tuple-element.257.v_ref, bf16[1024,256]{1,0:T(8,128)(2,1)} %pad_maximum_fusion.2.grad_ref, ...), custom_call_target="tpu_custom_call" | custom-call | tf_op jit(solution)/shard_map/attend_back/pallas_call | solution.py:107
  381.9 2.7 convolution_convert_fusion.2
  385.4 2.6 fusion.29
  391.9 3.3 add_convert_fusion.3
  396.2 2.8 collective-permute-start.28
  399.0 4.4 all-to-all-start.2
  403.5 3.2 fusion.45
  418.9 18.0 %collective-permute-done.30 = bf16[128,2048]{1,0:T(8,128)(2,1)} collective-permute-done((bf16[128,2048]{1,0:T(8,128)(2,1)S(1)}, bf16[128,2048]{1,0:T(8,128)(2,1)}, u32[]{:S(2)}, u32[]{:S(2)}) %collective-permute-start.30) | collective-permute-done | bytes 524320 | tf_op jit(solution)/shard_map/ppermute | solution.py:230
  436.9 2.9 fusion.49
  443.7 3.8 all-to-all-start.3
  447.6 4.7 collective-permute-start.33
  454.8 11.0 %reduce-scatter.9.cloned.1.call-done = bf16[256,2048]{1,0:T(8,128)(2,1)} async-done(((bf16[1024,2048]{1,0:T(8,128)(2,1)}), bf16[256,2048]{1,0:T(8,128)(2,1)}) %reduce-scatter.9.cloned.1.call-update) | async-done | bytes 1048592 | tf_op jit(solution)/shard_map/reduce_scatter | solution.py:485
  466.6 5.0 all-to-all-start.4
  482.1 3.5 all-to-all-start.5
  486.6 7.2 %all-to-all-done.5 = bf16[8,64,384]{2,1,0:T(8,128)(2,1)S(1)} async-done(((bf16[8,64,384]{2,1,0:T(8,128)(2,1)}), bf16[8,64,384]{2,1,0:T(8,128)(2,1)S(1)}, u32[]{:S(2)}, u32[]{:S(2)}) %all-to-all-start.5) | async-done | bytes 393248 | tf_op jit(solution)/shard_map/all_to_all | solution.py:576
  (356 shorter events, 124.7 us)
Async XLA Ops:
  7.2 61.7 %all-gather.12.cloned.1.call-start = ((), (), s32[]{:S(2)}) async-start(), calls=%async_computation.17 | async-start | bytes 2211840 | tf_op jit(solution)/shard_map/all_gather | solution.py:401
  24.7 14.8 %collective-permute-start = (bf16[128,2048]{1,0:T(8,128)(2,1)S(1)}, bf16[128,2048]{1,0:T(8,128)(2,1)S(1)}, u32[]{:S(2)}, u32[]{:S(2)}) collective-permute-start(bf16[128,2048]{1,0:T(8,128)(2,1)S(1)} %bitcast.139), channel_id=1, source_target_pairs={{0,8},{4,12},{8,0},{12,4},{16,24},{20,28},{24,16},{28,20},{1,9},{5... | collective-permute-start | bytes 1572872 | tf_op jit(solution)/shard_map/ppermute | solution.py:230
  25.3 24.7 %collective-permute-start.1 = (bf16[128,2048]{1,0:T(8,128)(2,1)S(1)}, bf16[128,2048]{1,0:T(8,128)(2,1)S(1)}, u32[]{:S(2)}, u32[]{:S(2)}) collective-permute-start(bf16[128,2048]{1,0:T(8,128)(2,1)S(1)} %bitcast.140), channel_id=1, source_target_pairs={{0,16},{4,20},{8,24},{12,28},{16,0},{20,4},{24,8},{28,12},{1,17},{... | collective-permute-start | bytes 1572872 | tf_op jit(solution)/shard_map/ppermute | solution.py:230
  25.8 25.0 %collective-permute-start.2 = (bf16[128,2048]{1,0:T(8,128)(2,1)S(1)}, bf16[128,2048]{1,0:T(8,128)(2,1)S(1)}, u32[]{:S(2)}, u32[]{:S(2)}) collective-permute-start(bf16[128,2048]{1,0:T(8,128)(2,1)S(1)} %bitcast.141), channel_id=1, source_target_pairs={{0,24},{4,28},{8,16},{12,20},{16,8},{20,12},{24,0},{28,4},{1,25},{... | collective-permute-start | bytes 1572872 | tf_op jit(solution)/shard_map/ppermute | solution.py:230
  29.0 75.7 %all-gather.6.cloned.1.call-start = ((), (), s32[]{:S(2)}) async-start(), calls=%async_computation.10 | async-start | bytes 1310720 | tf_op jit(solution)/shard_map/all_gather | solution.py:412
  51.7 6.5 %collective-permute-start.3 = (bf16[512,2048]{1,0:T(8,128)(2,1)}, bf16[512,2048]{1,0:T(8,128)(2,1)}, u32[]{:S(2)}, u32[]{:S(2)}) collective-permute-start(bf16[512,2048]{1,0:T(8,128)(2,1)} %constant_dynamic-update-slice_fusion), channel_id=1, source_target_pairs={{0,4},{4,0},{8,12},{12,8},{16,20},{20,16},{24,28},{28,24},{1,5},{5... | collective-permute-start | bytes 6291464 | tf_op jit(solution)/shard_map/ppermute | solution.py:230
  54.7 48.9 %collective-permute-start.7 = (bf16[256,2048]{1,0:T(8,128)(2,1)}, bf16[256,2048]{1,0:T(8,128)(2,1)}, u32[]{:S(2)}, u32[]{:S(2)}) collective-permute-start(bf16[256,2048]{1,0:T(8,128)(2,1)} %param.30), channel_id=1, source_target_pairs={{0,24},{4,28},{8,16},{12,20},{16,8},{20,12},{24,0},{28,4},{1,25},{... | collective-permute-start | bytes 3145736 | tf_op jit(solution)/shard_map/ppermute | solution.py:230
  55.0 48.6 %collective-permute-start.6 = (bf16[256,2048]{1,0:T(8,128)(2,1)}, bf16[256,2048]{1,0:T(8,128)(2,1)}, u32[]{:S(2)}, u32[]{:S(2)}) collective-permute-start(bf16[256,2048]{1,0:T(8,128)(2,1)} %param.30), channel_id=1, source_target_pairs={{0,16},{4,20},{8,24},{12,28},{16,0},{20,4},{24,8},{28,12},{1,17},{... | collective-permute-start | bytes 3145736 | tf_op jit(solution)/shard_map/ppermute | solution.py:230
  57.3 46.4 %collective-permute-start.5 = (bf16[256,2048]{1,0:T(8,128)(2,1)}, bf16[256,2048]{1,0:T(8,128)(2,1)}, u32[]{:S(2)}, u32[]{:S(2)}) collective-permute-start(bf16[256,2048]{1,0:T(8,128)(2,1)} %param.30), channel_id=1, source_target_pairs={{0,8},{4,12},{8,0},{12,4},{16,24},{20,28},{24,16},{28,20},{1,9},{5... | collective-permute-start | bytes 3145736 | tf_op jit(solution)/shard_map/ppermute | solution.py:230
  83.2 39.0 %all-to-all-start.1 = ((bf16[8,64,1024]{2,1,0:T(8,128)(2,1)}), bf16[8,64,1024]{2,1,0:T(8,128)(2,1)}, u32[]{:S(2)}, u32[]{:S(2)}) async-start(bf16[8,64,1024]{2,1,0:T(8,128)(2,1)} %reshape.410), calls=%async_computation.1 | async-start | bytes 2097152 | tf_op jit(solution)/shard_map/all_to_all | solution.py:419
  87.4 83.8 %all-gather.8.cloned.1.call-start = ((), (), s32[]{:S(2)}) async-start(), calls=%async_computation.11 | async-start | bytes 2621440 | tf_op jit(solution)/shard_map/all_gather | solution.py:413
  92.3 1.6 collective-permute-start.4
  125.5 14.3 %collective-permute-start.8 = (bf16[512,2048]{1,0:T(8,128)(2,1)}, bf16[512,2048]{1,0:T(8,128)(2,1)}, u32[]{:S(2)}, u32[]{:S(2)}) collective-permute-start(bf16[512,2048]{1,0:T(8,128)(2,1)} %convolution_convert_fusion.1), channel_id=1, source_target_pairs={{0,4},{4,0},{8,12},{12,8},{16,20},{20,16},{24,28},{28,24},{1,5},{5... | collective-permute-start | bytes 6291464 | tf_op jit(solution)/shard_map/ppermute | solution.py:230
  125.8 42.3 %copy-start.43 = (f32[128]{0:T(128)}, f32[128]{0:T(128)S(1)}, u32[]{:S(2)}) copy-start(f32[128]{0:T(128)S(1)} %broadcast_multiply_fusion.4) | copy-start | bytes 1540
  125.9 101.6 %all-gather.10.cloned.1.call-start = ((), (), s32[]{:S(2)}) async-start(), calls=%async_computation.12 | async-start | bytes 5242880 | tf_op jit(solution)/shard_map/all_gather | solution.py:468
  141.7 15.8 %collective-permute-start.11 = (bf16[128,2048]{1,0:T(8,128)(2,1)S(1)}, bf16[128,2048]{1,0:T(8,128)(2,1)S(1)}, u32[]{:S(2)}, u32[]{:S(2)}) collective-permute-start(bf16[128,2048]{1,0:T(8,128)(2,1)S(1)} %get-tuple-element.251), channel_id=1, source_target_pairs={{0,24},{4,28},{8,16},{12,20},{16,8},{20,12},{24,0},{28,4},{1,25},{... | collective-permute-start | bytes 1572872 | tf_op jit(solution)/shard_map/ppermute | solution.py:230
  144.2 24.0 %collective-permute-start.9 = (bf16[128,2048]{1,0:T(8,128)(2,1)S(1)}, bf16[128,2048]{1,0:T(8,128)(2,1)S(1)}, u32[]{:S(2)}, u32[]{:S(2)}) collective-permute-start(bf16[128,2048]{1,0:T(8,128)(2,1)S(1)} %get-tuple-element.250), channel_id=1, source_target_pairs={{0,8},{4,12},{8,0},{12,4},{16,24},{20,28},{24,16},{28,20},{1,9},{5... | collective-permute-start | bytes 1572872 | tf_op jit(solution)/shard_map/ppermute | solution.py:230
  144.7 23.4 %collective-permute-start.10 = (bf16[128,2048]{1,0:T(8,128)(2,1)S(1)}, bf16[128,2048]{1,0:T(8,128)(2,1)S(1)}, u32[]{:S(2)}, u32[]{:S(2)}) collective-permute-start(bf16[128,2048]{1,0:T(8,128)(2,1)S(1)} %get-tuple-element.252), channel_id=1, source_target_pairs={{0,16},{4,20},{8,24},{12,28},{16,0},{20,4},{24,8},{28,12},{1,17},{... | collective-permute-start | bytes 1572872 | tf_op jit(solution)/shard_map/ppermute | solution.py:230
  171.3 188.3 %reduce-scatter.5.cloned.1.call-start = ((), (), s32[]{:S(2)}) async-start(), calls=%async_computation.13 | async-start | bytes 5242880 | tf_op jit(solution)/shard_map/reduce_scatter | solution.py:485
  171.3 8.0 %collective-permute-start.14 = (bf16[512,2048]{1,0:T(8,128)(2,1)}, bf16[512,2048]{1,0:T(8,128)(2,1)S(1)}, u32[]{:S(2)}, u32[]{:S(2)}) collective-permute-start(bf16[512,2048]{1,0:T(8,128)(2,1)} %all-gather.8.cloned.1.call-done.a_ref.b0_ref), channel_id=1, source_target_pairs={{0,4},{4,0},{8,12},{12,8},{16,20},{20,16},{24,28},{28,24},{1,5},{5... | collective-permute-start | bytes 6291464 | tf_op jit(solution)/shard_map/ppermute | solution.py:230
  171.4 15.0 %collective-permute-start.13 = (bf16[128,2048]{1,0:T(8,128)(2,1)}, bf16[128,2048]{1,0:T(8,128)(2,1)}, u32[]{:S(2)}, u32[]{:S(2)}) collective-permute-start(bf16[128,2048]{1,0:T(8,128)(2,1)} %add_convert_fusion.8), channel_id=1, source_target_pairs={{0,3},{1,0},{2,1},{3,2},{4,7},{5,4},{6,5},{7,6},{8,11},{9,8},{10,9... | collective-permute-start | bytes 1572872 | tf_op jit(solution)/shard_map/ppermute | solution.py:282
  171.5 25.8 %collective-permute-start.12 = (bf16[128,2048]{1,0:T(8,128)(2,1)}, bf16[128,2048]{1,0:T(8,128)(2,1)}, u32[]{:S(2)}, u32[]{:S(2)}) collective-permute-start(bf16[128,2048]{1,0:T(8,128)(2,1)} %add_convert_fusion.8), channel_id=1, source_target_pairs={{0,1},{1,2},{2,3},{3,0},{4,5},{5,6},{6,7},{7,4},{8,9},{9,10},{10,1... | collective-permute-start | bytes 1572872 | tf_op jit(solution)/shard_map/ppermute | solution.py:282
  197.3 25.8 %collective-permute-start.15 = (bf16[128,2048]{1,0:T(8,128)(2,1)}, bf16[128,2048]{1,0:T(8,128)(2,1)S(1)}, u32[]{:S(2)}, u32[]{:S(2)}) collective-permute-start(bf16[128,2048]{1,0:T(8,128)(2,1)} %add_convert_fusion.8), channel_id=1, source_target_pairs={{0,2},{1,3},{2,0},{3,1},{4,6},{5,7},{6,4},{7,5},{8,10},{9,11},{10,... | collective-permute-start | bytes 1572872 | tf_op jit(solution)/shard_map/ppermute | solution.py:282
  223.1 4.4 collective-permute-start.16
  245.2 4.7 collective-permute-start.17
  253.3 26.4 %collective-permute-start.19 = (bf16[128,2048]{1,0:T(8,128)(2,1)}, bf16[128,2048]{1,0:T(8,128)(2,1)}, u32[]{:S(2)}, u32[]{:S(2)}) collective-permute-start(bf16[128,2048]{1,0:T(8,128)(2,1)} %get-tuple-element.247), channel_id=1, source_target_pairs={{0,1},{1,2},{2,3},{3,0},{4,5},{5,6},{6,7},{7,4},{8,9},{9,10},{10,1... | collective-permute-start | bytes 1572872 | tf_op jit(solution)/shard_map/ppermute | solution.py:282
  253.3 26.4 %collective-permute-start.18 = (bf16[128,2048]{1,0:T(8,128)(2,1)}, bf16[128,2048]{1,0:T(8,128)(2,1)}, u32[]{:S(2)}, u32[]{:S(2)}) collective-permute-start(bf16[128,2048]{1,0:T(8,128)(2,1)} %get-tuple-element.248), channel_id=1, source_target_pairs={{0,3},{1,0},{2,1},{3,2},{4,7},{5,4},{6,5},{7,6},{8,11},{9,8},{10,9... | collective-permute-start | bytes 1572872 | tf_op jit(solution)/shard_map/ppermute | solution.py:282
  279.7 160.0 %reduce-scatter.7.cloned.1.call-start = ((), (), s32[]{:S(2)}) async-start(), calls=%async_computation.14 | async-start | bytes 2621440 | tf_op jit(solution)/shard_map/reduce_scatter | solution.py:512
  280.2 30.8 %collective-permute-start.21 = (bf16[512,2048]{1,0:T(8,128)(2,1)}, bf16[512,2048]{1,0:T(8,128)(2,1)}, u32[]{:S(2)}, u32[]{:S(2)}) collective-permute-start(bf16[512,2048]{1,0:T(8,128)(2,1)} %multiply.79), channel_id=1, source_target_pairs={{0,4},{4,0},{8,12},{12,8},{16,20},{20,16},{24,28},{28,24},{1,5},{5... | collective-permute-start | bytes 6291464 | tf_op jit(solution)/shard_map/ppermute | solution.py:230
  280.3 26.6 %collective-permute-start.20 = (bf16[128,2048]{1,0:T(8,128)(2,1)}, bf16[128,2048]{1,0:T(8,128)(2,1)}, u32[]{:S(2)}, u32[]{:S(2)}) collective-permute-start(bf16[128,2048]{1,0:T(8,128)(2,1)} %get-tuple-element.168), channel_id=1, source_target_pairs={{0,2},{1,3},{2,0},{3,1},{4,6},{5,7},{6,4},{7,5},{8,10},{9,11},{10,... | collective-permute-start | bytes 1572872 | tf_op jit(solution)/shard_map/ppermute | solution.py:282
  315.8 25.8 %collective-permute-start.22 = (bf16[128,2048]{1,0:T(8,128)(2,1)S(1)}, bf16[128,2048]{1,0:T(8,128)(2,1)}, u32[]{:S(2)}, u32[]{:S(2)}) collective-permute-start(bf16[128,2048]{1,0:T(8,128)(2,1)S(1)} %get-tuple-element.182), channel_id=1, source_target_pairs={{0,8},{4,12},{8,0},{12,4},{16,24},{20,28},{24,16},{28,20},{1,9},{5... | collective-permute-start | bytes 1572872 | tf_op jit(solution)/shard_map/ppermute | solution.py:230
  317.4 26.2 %collective-permute-start.23 = (bf16[128,2048]{1,0:T(8,128)(2,1)S(1)}, bf16[128,2048]{1,0:T(8,128)(2,1)}, u32[]{:S(2)}, u32[]{:S(2)}) collective-permute-start(bf16[128,2048]{1,0:T(8,128)(2,1)S(1)} %get-tuple-element.182), channel_id=1, source_target_pairs={{0,16},{4,20},{8,24},{12,28},{16,0},{20,4},{24,8},{28,12},{1,17},{... | collective-permute-start | bytes 1572872 | tf_op jit(solution)/shard_map/ppermute | solution.py:230
  318.8 34.4 %collective-permute-start.24 = (bf16[128,2048]{1,0:T(8,128)(2,1)S(1)}, bf16[128,2048]{1,0:T(8,128)(2,1)}, u32[]{:S(2)}, u32[]{:S(2)}) collective-permute-start(bf16[128,2048]{1,0:T(8,128)(2,1)S(1)} %get-tuple-element.182), channel_id=1, source_target_pairs={{0,24},{4,28},{8,16},{12,20},{16,8},{20,12},{24,0},{28,4},{1,25},{... | collective-permute-start | bytes 1572872 | tf_op jit(solution)/shard_map/ppermute | solution.py:230
  320.2 145.6 %reduce-scatter.9.cloned.1.call-start = ((), (), s32[]{:S(2)}) async-start(), calls=%async_computation.15 | async-start | bytes 5242880 | tf_op jit(solution)/shard_map/reduce_scatter | solution.py:485
  355.1 4.5 collective-permute-start.25
  378.3 1.6 collective-permute-start.26
  384.5 7.4 %collective-permute-start.27 = (bf16[512,2048]{1,0:T(8,128)(2,1)}, bf16[512,2048]{1,0:T(8,128)(2,1)}, u32[]{:S(2)}, u32[]{:S(2)}) collective-permute-start(bf16[512,2048]{1,0:T(8,128)(2,1)} %convolution_convert_fusion.2), channel_id=1, source_target_pairs={{0,4},{4,0},{8,12},{12,8},{16,20},{20,16},{24,28},{28,24},{1,5},{5... | collective-permute-start | bytes 6291464 | tf_op jit(solution)/shard_map/ppermute | solution.py:230
  395.2 22.9 %collective-permute-start.29 = (bf16[128,2048]{1,0:T(8,128)(2,1)}, bf16[128,2048]{1,0:T(8,128)(2,1)S(1)}, u32[]{:S(2)}, u32[]{:S(2)}) collective-permute-start(bf16[128,2048]{1,0:T(8,128)(2,1)} %get-tuple-element.242), channel_id=1, source_target_pairs={{0,16},{4,20},{8,24},{12,28},{16,0},{20,4},{24,8},{28,12},{1,17},{... | collective-permute-start | bytes 1572872 | tf_op jit(solution)/shard_map/ppermute | solution.py:230
  396.2 21.9 %collective-permute-start.28 = (bf16[128,2048]{1,0:T(8,128)(2,1)}, bf16[128,2048]{1,0:T(8,128)(2,1)}, u32[]{:S(2)}, u32[]{:S(2)}) collective-permute-start(bf16[128,2048]{1,0:T(8,128)(2,1)} %get-tuple-element.244), channel_id=1, source_target_pairs={{0,8},{4,12},{8,0},{12,4},{16,24},{20,28},{24,16},{28,20},{1,9},{5... | collective-permute-start | bytes 1572872 | tf_op jit(solution)/shard_map/ppermute | solution.py:230
  399.0 43.2 %all-to-all-start.2 = ((bf16[8,64,1024]{2,1,0:T(8,128)(2,1)}), bf16[8,64,1024]{2,1,0:T(8,128)(2,1)}, u32[]{:S(2)}, u32[]{:S(2)}) async-start(bf16[8,64,1024]{2,1,0:T(8,128)(2,1)} %bitcast.46), calls=%async_computation.3 | async-start | bytes 2097152 | tf_op jit(solution)/shard_map/all_to_all | solution.py:541
  410.0 26.8 %collective-permute-start.30 = (bf16[128,2048]{1,0:T(8,128)(2,1)S(1)}, bf16[128,2048]{1,0:T(8,128)(2,1)}, u32[]{:S(2)}, u32[]{:S(2)}) collective-permute-start(bf16[128,2048]{1,0:T(8,128)(2,1)S(1)} %get-tuple-element.199), channel_id=1, source_target_pairs={{0,24},{4,28},{8,16},{12,20},{16,8},{20,12},{24,0},{28,4},{1,25},{... | collective-permute-start | bytes 1572872 | tf_op jit(solution)/shard_map/ppermute | solution.py:230
  410.7 29.1 %collective-permute-start.32 = (bf16[512,384]{1,0:T(8,128)(2,1)}, bf16[512,384]{1,0:T(8,128)(2,1)S(1)}, u32[]{:S(2)}, u32[]{:S(2)}) collective-permute-start(bf16[512,384]{1,0:T(8,128)(2,1)} %get-tuple-element.253), channel_id=1, source_target_pairs={{0,1},{1,2},{2,3},{3,0},{4,5},{5,6},{6,7},{7,4},{8,9},{9,10},{10,1... | collective-permute-start | bytes 1179656 | tf_op jit(solution)/shard_map/ppermute | solution.py:282
  412.8 29.5 %collective-permute-start.31 = (bf16[512,384]{1,0:T(8,128)(2,1)}, bf16[512,384]{1,0:T(8,128)(2,1)S(1)}, u32[]{:S(2)}, u32[]{:S(2)}) collective-permute-start(bf16[512,384]{1,0:T(8,128)(2,1)} %get-tuple-element.255), channel_id=1, source_target_pairs={{0,3},{1,0},{2,1},{3,2},{4,7},{5,4},{6,5},{7,6},{8,11},{9,8},{10,9... | collective-permute-start | bytes 1179656 | tf_op jit(solution)/shard_map/ppermute | solution.py:282
  443.7 11.1 %all-to-all-start.3 = ((f32[8,8,512]{2,1,0:T(8,128)}), f32[8,8,512]{2,1,0:T(8,128)S(1)}, u32[]{:S(2)}, u32[]{:S(2)}) async-start(f32[8,8,512]{2,1,0:T(8,128)} %pad_maximum_fusion.5), calls=%async_computation.5 | async-start | bytes 262144 | tf_op jit(solution)/shard_map/all_to_all | solution.py:593
  447.5 49.4 %reduce-scatter.11.cloned.1.call-start = ((), (), s32[]{:S(2)}) async-start(), calls=%async_computation.16 | async-start | bytes 1310720 | tf_op jit(solution)/shard_map/reduce_scatter | solution.py:597
  447.6 32.6 %collective-permute-start.33 = (bf16[512,384]{1,0:T(8,128)(2,1)}, bf16[512,384]{1,0:T(8,128)(2,1)}, u32[]{:S(2)}, u32[]{:S(2)}) collective-permute-start(bf16[512,384]{1,0:T(8,128)(2,1)} %get-tuple-element.212), channel_id=1, source_target_pairs={{0,2},{1,3},{2,0},{3,1},{4,6},{5,7},{6,4},{7,5},{8,10},{9,11},{10,... | collective-permute-start | bytes 1179656 | tf_op jit(solution)/shard_map/ppermute | solution.py:282
  466.6 12.3 %all-to-all-start.4 = ((f32[4,1,512]{2,1,0:T(1,128)}), f32[4,1,512]{2,1,0:T(1,128)S(1)}, u32[]{:S(2)}, u32[]{:S(2)}) async-start(f32[4,1,512]{2,1,0:T(1,128)} %reshape.475), calls=%async_computation.6 | async-start | bytes 16384 | tf_op jit(solution)/shard_map/all_to_all | solution.py:603
  482.1 11.7 %all-to-all-start.5 = ((bf16[8,64,384]{2,1,0:T(8,128)(2,1)}), bf16[8,64,384]{2,1,0:T(8,128)(2,1)S(1)}, u32[]{:S(2)}, u32[]{:S(2)}) async-start(bf16[8,64,384]{2,1,0:T(8,128)(2,1)} %bitcast.62), calls=%async_computation.7 | async-start | bytes 786432 | tf_op jit(solution)/shard_map/all_to_all | solution.py:576
  (63 other events, 573.8 us)
Sparse Core Ops, SparseCore 0:
  29.2 39.6 all-gather.11
  72.7 31.9 all-gather.5
  126.0 44.1 all-gather.7
  171.8 51.4 all-gather.9
  279.9 63.1 reduce-scatter.4
  345.9 53.4 reduce-scatter.6
  402.4 63.3 reduce-scatter.8
  468.2 27.4 reduce-scatter.10
